TPU v7x, 32 devices: a whole 2x2x4 slice. The times are simulated.
32 devices in a mesh: sector: 8 (over z, x), band: 4 (over y, core).
Axes of the slice: x: 2, y: 2, z: 4, core: 2. Of those that a mesh axis runs over, the one named last changes fastest.
Arguments:
- queries: bfloat16 [128, 256, 256], P('sector', 'band'), may hold values from -6 to 6
- norm_gain: float32 [256], replicated, may hold values from 0.5 to 1.5
- w_query: bfloat16 [256, 256], replicated, may hold values from -0.375 to 0.375
- w_key: bfloat16 [256, 256], replicated, may hold values from -0.375 to 0.375
- w_value: bfloat16 [256, 256], replicated, may hold values from -0.375 to 0.375
- w_out: bfloat16 [256, 256], replicated, may hold values from -0.375 to 0.375
- features: bfloat16 [65536, 256], P(('sector', 'band')), may hold values from -160 to 160
- visible: int32 [128, 256, 3], P('sector', 'band'), may hold values from 0 to 3071, as said below
- live: int32 [128, 256, 3], P('sector', 'band'), may hold values from 0 to 1, as said below
Outputs:
- attended: bfloat16 [128, 256, 256], P('sector', 'band')
Inputs may be any that keep to these rules, and one draw needn't show every extreme that they name: `visible`: on each device (s, j), the 3072 entries name every code from 0 to 3071 exactly once. `live`: 1 marks an entry that contributes, 0 one that does not.
All inputs are finite; a program needn't handle non-finite values.
Results may differ from a plain program's by a relative error of at most 0.0025.
The roundings to bfloat16 on the way count: a program that leaves them out, or rounds other values in their place, can miss the bound.
Values may be sent and summed in bfloat16 or wider, within the bound.
No kernel may reach another device: no remote copies, remote signals or barrier semaphores. Data moves between devices by JAX's collectives and lax.ppermute only.
A program may use at most 128 MiB of HBM per device.

v0:
```python
import functools

import jax
import jax.numpy as jnp
from jax import lax
from jax.experimental import pallas as pl
from jax.experimental.pallas import tpu as pltpu
from jax.sharding import PartitionSpec as P

HEADS = 8
BLK_DEV = 8
CAP = 128
LOG2_E = 1.4426950408889634
VMEM_BYTES = 24 << 20
UNROLL = 2


def params():
    return pltpu.CompilerParams(vmem_limit_bytes=VMEM_BYTES)


def shifted(block, axis, distance):
    count = lax.axis_size(axis)
    return lax.ppermute(block, axis, [(i, (i + distance) % count) for i in range(count)])


def swapped(block, axis, bit):
    count = lax.axis_size(axis)
    return lax.ppermute(block, axis, [(i, i ^ bit) for i in range(count)])


def fill_slots(codes_ref, rows, out_refs, group):
    blocks = out_refs[0].shape[0]
    queries = rows.shape[0]
    for step in range(0, BLK_DEV, 2):
        slot = lax.broadcasted_iota(jnp.int32, (2 * CAP, queries), 0) + (group * BLK_DEV + step) * CAP
        hit = slot == codes_ref[0:1, :]
        for entry in range(1, codes_ref.shape[0]):
            hit = hit | (slot == codes_ref[entry:entry + 1, :])
        pick = jnp.where(hit, 1.0, 0.0).astype(jnp.bfloat16)
        got = jnp.dot(pick, rows, preferred_element_type=jnp.float32).astype(jnp.bfloat16)
        at = step % blocks
        out_refs[step // blocks][at:at + 2] = got.reshape(2, CAP, got.shape[1])


def project_kernel(codes_ref, queries_ref, gain_ref, weight_ref, rows_ref, *slot_refs):
    values = queries_ref[...].astype(jnp.float32)
    average = jnp.mean(values, axis=-1, keepdims=True)
    centred = values - average
    spread = jnp.mean(centred * centred, axis=-1, keepdims=True)
    normed = (centred * lax.rsqrt(spread + 1e-05) * gain_ref[...]).astype(jnp.bfloat16)
    rows = jnp.dot(normed, weight_ref[...], preferred_element_type=jnp.float32).astype(jnp.bfloat16)
    rows_ref[...] = rows
    parts = len(slot_refs) // 2
    fill_slots(codes_ref, rows, slot_refs[:parts], 2)
    fill_slots(codes_ref, rows, slot_refs[parts:], 0)


def slot_shapes(parts, width):
    return (jax.ShapeDtypeStruct((BLK_DEV // parts, CAP, width), jnp.bfloat16),) * parts


def project(codes, queries, gain, weight, parts):
    count, width = queries.shape
    return pl.pallas_call(
        project_kernel,
        out_shape=(jax.ShapeDtypeStruct((count, width), jnp.bfloat16),) + 2 * slot_shapes(parts, width),
        compiler_params=params(),
        cost_estimate=pl.CostEstimate(flops=4 << 30, bytes_accessed=2 << 20, transcendentals=0),
        name="project",
    )(codes, queries, gain, weight)


def scatter_kernel(codes_ref, rows_ref, *slot_refs):
    fill_slots(codes_ref, rows_ref[...], slot_refs, 1)


def scatter(codes, rows, parts):
    return pl.pallas_call(
        scatter_kernel,
        out_shape=slot_shapes(parts, rows.shape[1]),
        compiler_params=params(),
        cost_estimate=pl.CostEstimate(flops=1 << 30, bytes_accessed=2 << 20, transcendentals=0),
        name="scatter",
    )(codes, rows)


def kv_kernel(key_ref, value_ref, *refs):
    out_ref = refs[-1]
    keys, width = out_ref.shape[1], key_ref.shape[1]
    done = 0
    for ref in refs[:-1]:
        for at in range(0, ref.shape[0], keys):
            rows = ref[at:at + keys]
            for side, weight_ref in enumerate((key_ref, value_ref)):
                got = jnp.dot(rows, weight_ref[...], preferred_element_type=jnp.float32)
                out_ref[done, :, side * width:(side + 1) * width] = got.astype(jnp.bfloat16)
            done += 1


def keys_and_values(features, w_key, w_value, keys):
    width = w_key.shape[1]
    count = sum(part.shape[0] for part in features)
    return pl.pallas_call(
        kv_kernel,
        out_shape=jax.ShapeDtypeStruct((count // keys, keys, 2 * width), jnp.bfloat16),
        compiler_params=params(),
        cost_estimate=pl.CostEstimate(flops=4 * count * width * width, bytes_accessed=6 * count * width, transcendentals=0),
        name="keys_and_values",
    )(w_key, w_value, *features)


def attend_kernel(rows_ref, kv_ref, out_ref, scores_ref, *, stack):
    blocks, count, width = rows_ref.shape
    head_size = width // HEADS
    factor = head_size ** (-0.5) * LOG2_E
    head_of = lax.broadcasted_iota(jnp.int32, (1, width), 1) // head_size
    firsts = list(range(0, HEADS, stack))

    def scores_of(b, first):
        rows = rows_ref[b]
        kept = [jnp.where(head_of == first + i, rows, jnp.zeros_like(rows)) for i in range(stack)]
        return lax.dot_general(
            jnp.concatenate(kept, axis=0), kv_ref[b, :, :width],
            (((1,), (1,)), ((), ())), preferred_element_type=jnp.float32)

    scores_ref[...] = scores_of(0, 0)

    @pl.loop(0, blocks // UNROLL)
    def _(step):
        scores = scores_ref[...]
        for unit in range(UNROLL):
            b = step * UNROLL + unit
            merged = None
            for at, first in enumerate(firsts):
                if at + 1 < len(firsts):
                    following = scores_of(b, firsts[at + 1])
                else:
                    following = scores_of(jnp.minimum(b + 1, blocks - 1), 0)
                peak = jnp.max(scores, axis=1, keepdims=True)
                expo = jnp.exp2((scores - peak) * factor)
                weights = (expo * (1.0 / jnp.sum(expo, axis=1, keepdims=True))).astype(jnp.bfloat16)
                got = jnp.dot(weights, kv_ref[b, :, width:], preferred_element_type=jnp.float32)
                for i in range(stack):
                    part = got[i * count:(i + 1) * count]
                    merged = part if first + i == 0 else jnp.where(head_of == first + i, part, merged)
                scores = following
            out_ref[b] = merged.astype(jnp.bfloat16)
        scores_ref[...] = scores


def attend(rows, kv, name):
    blocks, count, width = rows.shape
    keys = kv.shape[1]
    stack = 2
    pairs = blocks * count * keys
    return pl.pallas_call(
        functools.partial(attend_kernel, stack=stack),
        out_shape=jax.ShapeDtypeStruct(rows.shape, jnp.bfloat16),
        scratch_shapes=[pltpu.VMEM((stack * count, keys), jnp.float32)],
        compiler_params=params(),
        cost_estimate=pl.CostEstimate(
            flops=4 * pairs * width * HEADS, bytes_accessed=blocks * keys * width * 4,
            transcendentals=pairs * HEADS),
        name=name,
    )(rows, kv)


def gathered(codes_ref, result_refs, at):
    entries = codes_ref.shape[1]
    count = at.shape[0]
    total = None
    for base, ref in result_refs:
        slots = ref.shape[0] * ref.shape[1]
        slot = lax.broadcasted_iota(jnp.int32, (count, slots), 1) + base
        hit = slot == at[:, 0:1]
        for entry in range(1, 3):
            hit = hit | (slot == at[:, entry:entry + 1])
        pick = jnp.where(hit, 1.0, 0.0).astype(jnp.bfloat16)
        got = jnp.dot(pick, ref[...].reshape(slots, ref.shape[2]), preferred_element_type=jnp.float32)
        total = got if total is None else total + got
    return total


def columns_of(codes_ref):
    entries, count = codes_ref.shape
    spare = jnp.full((8 - entries, count), -1, jnp.int32)
    return jnp.concatenate([codes_ref[...], spare], axis=0).T


def partial_kernel(codes_ref, *refs, bases):
    out_ref = refs[-1]
    at = columns_of(codes_ref)
    tile = 256
    for step in range(out_ref.shape[0] // tile):
        rows = slice(step * tile, (step + 1) * tile)
        out_ref[rows] = gathered(codes_ref, list(zip(bases, refs[:-1])), at[rows])


def partial_sum(codes, results, bases):
    width = results[0].shape[2]
    return pl.pallas_call(
        functools.partial(partial_kernel, bases=bases),
        out_shape=jax.ShapeDtypeStruct((codes.shape[1], width), jnp.float32),
        compiler_params=params(),
        cost_estimate=pl.CostEstimate(flops=3 << 30, bytes_accessed=2 << 20, transcendentals=0),
        name="partial_sum",
    )(codes, *results)


def final_kernel(codes_ref, partial_ref, queries_ref, weight_ref, *refs, bases):
    out_ref = refs[-1]
    at = columns_of(codes_ref)
    tile = 256
    for step in range(out_ref.shape[0] // tile):
        rows = slice(step * tile, (step + 1) * tile)
        total = partial_ref[rows] + gathered(codes_ref, list(zip(bases, refs[:-1])), at[rows])
        final = jnp.dot(total.astype(jnp.bfloat16), weight_ref[...], preferred_element_type=jnp.float32)
        out_ref[rows] = (final + queries_ref[rows].astype(jnp.float32)).astype(jnp.bfloat16)


def finish(codes, partial, queries, weight, results, bases):
    return pl.pallas_call(
        functools.partial(final_kernel, bases=bases),
        out_shape=jax.ShapeDtypeStruct(queries.shape, jnp.bfloat16),
        compiler_params=params(),
        cost_estimate=pl.CostEstimate(flops=1 << 30, bytes_accessed=2 << 20, transcendentals=0),
        name="finish",
    )(codes, partial, queries, weight, *results)


def shards(queries, norm_gain, w_query, w_key, w_value, w_out, features, visible, live):
    azim_cells, range_cells, width = queries.shape
    entries = visible.shape[2]
    count = azim_cells * range_cells
    bands = lax.axis_size("band")
    local_rows = features.shape[0]
    keys = bands * local_rows // BLK_DEV
    staged = bands == 4 and local_rows == 2 * keys

    shift = (lax.axis_index("band") * local_rows // keys) * CAP
    codes = jnp.where(live != 0, visible ^ shift, -1).transpose(2, 0, 1).reshape(entries, count)
    rows_in = queries.reshape(count, width)

    if staged:
        across = swapped(features, "band", 2)
        held = [[features, swapped(features, "band", 1)]]
    else:
        whole_sector = features
        bit = 1
        while bit < bands:
            whole_sector = jnp.concatenate([whole_sector, swapped(whole_sector, "band", bit)], axis=0)
            bit *= 2
        held = [[whole_sector]]
    parts = 2 if staged else 1
    blocks = BLK_DEV // parts

    projected, *slots = project(codes, rows_in, norm_gain.reshape(1, width), w_query, parts)
    lower = [shifted(part, "sector", 1) for part in slots[:parts]]
    upper = [shifted(part, "sector", -1) for part in slots[parts:]]
    projected, *_ = lax.optimization_barrier((projected, *slots))
    own = list(scatter(codes, projected, parts))
    kv = keys_and_values(held[0], w_key, w_value, keys)
    own[0] = attend(own[0], kv, "own")

    if staged:
        across, own[0] = lax.optimization_barrier((across, own[0]))
        held.append([across, swapped(across, "band", 1)])

    def visit(part, kv, before):
        kv, first, second, before = lax.optimization_barrier((kv, lower[part], upper[part], before))
        first = attend(first, kv, "lower")
        second, first = lax.optimization_barrier((second, first))
        second = attend(second, kv, "upper")
        first, second = lax.optimization_barrier((first, second))
        return (shifted(first, "sector", -1), shifted(second, "sector", 1)), before, second

    sent, own[0], last = visit(0, kv, own[0])
    back = [sent]
    if staged:
        kv = keys_and_values(held[1], w_key, w_value, keys)
        sent, _, last = visit(1, kv, last)
        back.append(sent)
        own[1], _ = lax.optimization_barrier((own[1], last))
        own[1] = attend(own[1], kv, "own")

    def base(group, part):
        return (group * BLK_DEV + part * blocks) * CAP

    early = [(base(1, i), rows) for i, rows in enumerate(own)]
    early += [(base(2 - 2 * side, 0), back[0][side]) for side in range(2)] if staged else []
    late = [(base(2 - 2 * side, parts - 1), back[-1][side]) for side in range(2)]
    partial = partial_sum(codes, [rows for _, rows in early], tuple(at for at, _ in early))
    out = finish(codes, partial, rows_in, w_out, [rows for _, rows in late], tuple(at for at, _ in late))
    return out.reshape(azim_cells, range_cells, width)


def solution(mesh):
    return jax.shard_map(
        shards,
        mesh=mesh,
        in_specs=(
            P("sector", "band", None),
            P(),
            P(),
            P(),
            P(),
            P(),
            P(("sector", "band"), None),
            P("sector", "band", None),
            P("sector", "band", None),
        ),
        out_specs=P("sector", "band", None),
        check_vma=False,
    )
```

profile of v0, /device:TPU:0, one launch (start us, length us, event | category | flops | bytes accessed | tf_op | source)
XLA Modules:
  0.0 77.9 jit_solution(13461370624002510581)
XLA Ops:
  0.0 0.5 collective-permute-start
  0.5 2.5 %collective-permute-start.3 = (bf16[2048,256]{1,0:T(8,128)(2,1)}, bf16[2048,256]{1,0:T(8,128)(2,1)S(1)}, u32[]{:S(2)}, u32[]{:S(2)}) collective-permute-start(bf16[2048,256]{1,0:T(8,128)(2,1)} %refs_0_.1), channel_id=1, source_target_pairs={{0,2},{1,3},{2,0},{3,1},{4,6},{5,7},{6,4},{7,5},{8,10},{9,11},{10,... | collective-permute-start | bytes 3145736 | tf_op jit(solution)/shard_map/ppermute | solution.py:29
  3.0 0.8 select_bitcast_fusion
  3.8 0.1 reshape.12.codes_ref
  3.8 1.0 %copy-done.3 = bf16[16,64,256]{2,1,0:T(8,128)(2,1)S(1)} copy-done((bf16[16,64,256]{2,1,0:T(8,128)(2,1)S(1)}, bf16[16,64,256]{2,1,0:T(8,128)(2,1)}, u32[]{:S(2)}) %copy-start.3) | copy-done | bytes 524312
  4.9 0.9 %copy-done.5 = bf16[256,256]{1,0:T(8,128)(2,1)S(1)} copy-done((bf16[256,256]{1,0:T(8,128)(2,1)S(1)}, bf16[256,256]{1,0:T(8,128)(2,1)}, u32[]{:S(2)}) %copy-start.5) | copy-done | bytes 131096
  5.8 0.7 copy-done.7
  6.5 3.2 %project.1 = (bf16[1024,256]{1,0:T(8,128)(2,1)S(1)}, bf16[4,128,256]{2,1,0:T(8,128)(2,1)S(1)}, bf16[4,128,256]{2,1,0:T(8,128)(2,1)S(1)}, bf16[4,128,256]{2,1,0:T(8,128)(2,1)S(1)}, bf16[4,128,256]{2,1,0:T(8,128)(2,1)S(1)}) custom-call(s32[3,1024]{1,0:T(4,128)S(1)} %reshape.12.codes_ref, bf16[1024,256]{1,0:T(8,128)(2,1)S(1)} %bitcast.5, f32[1,256]{1,0:T(1,128)S(1)} %bitcast.7, ...), custom_call_target="tpu_custom_call" | custom-call | flops 4294967296 | bytes 2097152 | tf_op jit(solution)/shard_map/project/pallas_call | solution.py:65
  9.7 0.0 copy-start
  9.7 1.5 %collective-permute-start.1 = (bf16[4,128,256]{2,1,0:T(8,128)(2,1)S(1)}, bf16[4,128,256]{2,1,0:T(8,128)(2,1)S(1)}, u32[]{:S(2)}, u32[]{:S(2)}) collective-permute-start(bf16[4,128,256]{2,1,0:T(8,128)(2,1)S(1)} %get-tuple-element.31), channel_id=1, source_target_pairs={{0,4},{4,8},{8,12},{12,16},{16,20},{20,24},{24,28},{28,0},{1,5},{5... | collective-permute-start | bytes 786440 | tf_op jit(solution)/shard_map/ppermute | solution.py:24
  11.2 3.2 %collective-permute-start.2 = (bf16[4,128,256]{2,1,0:T(8,128)(2,1)S(1)}, bf16[4,128,256]{2,1,0:T(8,128)(2,1)S(1)}, u32[]{:S(2)}, u32[]{:S(2)}) collective-permute-start(bf16[4,128,256]{2,1,0:T(8,128)(2,1)S(1)} %get-tuple-element.32), channel_id=1, source_target_pairs={{0,28},{4,0},{8,4},{12,8},{16,12},{20,16},{24,20},{28,24},{1,29},{... | collective-permute-start | bytes 786440 | tf_op jit(solution)/shard_map/ppermute | solution.py:24
  14.5 1.5 %scatter.1 = (bf16[4,128,256]{2,1,0:T(8,128)(2,1)S(1)}, bf16[4,128,256]{2,1,0:T(8,128)(2,1)S(1)}) custom-call(s32[3,1024]{1,0:T(4,128)S(1)} %reshape.12.codes_ref, bf16[1024,256]{1,0:T(8,128)(2,1)S(1)} %get-tuple-element.33.rows_ref), custom_call_target="tpu_custom_call" | custom-call | flops 1073741824 | bytes 2097152 | tf_op jit(solution)/shard_map/scatter/pallas_call | solution.py:79
  16.0 0.0 collective-permute-done.refs_1_
  16.0 1.3 %keys_and_values.2.kv_ref = bf16[4,1024,512]{2,1,0:T(8,128)(2,1)S(1)} custom-call(bf16[256,256]{1,0:T(8,128)(2,1)S(1)} %copy-done.1, bf16[256,256]{1,0:T(8,128)(2,1)S(1)} %copy-done.2, bf16[2048,256]{1,0:T(8,128)(2,1)S(1)} %copy-done, bf16[2048,256]{1,0:T(8,128)(2,1)S(1)} %collective-permute-done.refs_1_), custom_call_target="tpu_custom_call" | custom-call | flops 1073741824 | bytes 6291456 | tf_op jit(solution)/shard_map/keys_and_values/pallas_call | solution.py:104
  17.3 6.3 %own.2.refs_0_ = bf16[4,128,256]{2,1,0:T(8,128)(2,1)S(1)} custom-call(bf16[4,128,256]{2,1,0:T(8,128)(2,1)S(1)} %get-tuple-element.34.rows_ref, bf16[4,1024,512]{2,1,0:T(8,128)(2,1)S(1)} %keys_and_values.2.kv_ref), custom_call_target="tpu_custom_call" | custom-call | flops 4294967296 | bytes 4194304 | tf_op jit(solution)/shard_map/own/pallas_call | solution.py:157
  23.5 3.5 %collective-permute-done.3.refs_0_ = bf16[2048,256]{1,0:T(8,128)(2,1)S(1)} collective-permute-done((bf16[2048,256]{1,0:T(8,128)(2,1)}, bf16[2048,256]{1,0:T(8,128)(2,1)S(1)}, u32[]{:S(2)}, u32[]{:S(2)}) %collective-permute-start.3) | collective-permute-done | bytes 1048608 | tf_op jit(solution)/shard_map/ppermute | solution.py:29
  27.0 1.7 %collective-permute-start.5 = (bf16[4,128,256]{2,1,0:T(8,128)(2,1)S(1)}, bf16[4,128,256]{2,1,0:T(8,128)(2,1)S(1)}, u32[]{:S(2)}, u32[]{:S(2)}) collective-permute-start(bf16[4,128,256]{2,1,0:T(8,128)(2,1)S(1)} %get-tuple-element.39), channel_id=1, source_target_pairs={{0,4},{4,8},{8,12},{12,16},{16,20},{20,24},{24,28},{28,0},{1,5},{5... | collective-permute-start | bytes 786440 | tf_op jit(solution)/shard_map/ppermute | solution.py:24
  28.8 3.0 %collective-permute-start.6 = (bf16[4,128,256]{2,1,0:T(8,128)(2,1)S(1)}, bf16[4,128,256]{2,1,0:T(8,128)(2,1)S(1)}, u32[]{:S(2)}, u32[]{:S(2)}) collective-permute-start(bf16[4,128,256]{2,1,0:T(8,128)(2,1)S(1)} %get-tuple-element.40), channel_id=1, source_target_pairs={{0,28},{4,0},{8,4},{12,8},{16,12},{20,16},{24,20},{28,24},{1,29},{... | collective-permute-start | bytes 786440 | tf_op jit(solution)/shard_map/ppermute | solution.py:24
  31.8 6.3 %lower.2 = bf16[4,128,256]{2,1,0:T(8,128)(2,1)S(1)} custom-call(bf16[4,128,256]{2,1,0:T(8,128)(2,1)S(1)} %collective-permute-done.1.rows_ref, bf16[4,1024,512]{2,1,0:T(8,128)(2,1)S(1)} %keys_and_values.2.kv_ref), custom_call_target="tpu_custom_call" | custom-call | flops 4294967296 | bytes 4194304 | tf_op jit(solution)/shard_map/lower/pallas_call | solution.py:157
  38.1 6.3 %upper.2 = bf16[4,128,256]{2,1,0:T(8,128)(2,1)S(1)} custom-call(bf16[4,128,256]{2,1,0:T(8,128)(2,1)S(1)} %collective-permute-done.2.rows_ref, bf16[4,1024,512]{2,1,0:T(8,128)(2,1)S(1)} %keys_and_values.2.kv_ref), custom_call_target="tpu_custom_call" | custom-call | flops 4294967296 | bytes 4194304 | tf_op jit(solution)/shard_map/upper/pallas_call | solution.py:157
  44.3 2.1 %collective-permute-start.7 = (bf16[4,128,256]{2,1,0:T(8,128)(2,1)S(1)}, bf16[4,128,256]{2,1,0:T(8,128)(2,1)S(1)}, u32[]{:S(2)}, u32[]{:S(2)}) collective-permute-start(bf16[4,128,256]{2,1,0:T(8,128)(2,1)S(1)} %lower.2), channel_id=1, source_target_pairs={{0,28},{4,0},{8,4},{12,8},{16,12},{20,16},{24,20},{28,24},{1,29},{... | collective-permute-start | bytes 786440 | tf_op jit(solution)/shard_map/ppermute | solution.py:24
  46.4 0.0 collective-permute-start.8
  46.4 1.3 %keys_and_values.3.kv_ref = bf16[4,1024,512]{2,1,0:T(8,128)(2,1)S(1)} custom-call(bf16[256,256]{1,0:T(8,128)(2,1)S(1)} %copy-done.1, bf16[256,256]{1,0:T(8,128)(2,1)S(1)} %copy-done.2, bf16[2048,256]{1,0:T(8,128)(2,1)S(1)} %collective-permute-done.3.refs_0_, bf16[2048,256]{1,0:T(8,128)(2,1)S(1)} %collective-permute-done.4.refs_1_), custom_call_target="tpu_custom_call" | custom-call | flops 1073741824 | bytes 6291456 | tf_op jit(solution)/shard_map/keys_and_values/pallas_call | solution.py:104
  47.7 6.3 %lower.3 = bf16[4,128,256]{2,1,0:T(8,128)(2,1)S(1)} custom-call(bf16[4,128,256]{2,1,0:T(8,128)(2,1)S(1)} %collective-permute-done.5.rows_ref, bf16[4,1024,512]{2,1,0:T(8,128)(2,1)S(1)} %keys_and_values.3.kv_ref), custom_call_target="tpu_custom_call" | custom-call | flops 4294967296 | bytes 4194304 | tf_op jit(solution)/shard_map/lower/pallas_call | solution.py:157
  54.0 6.3 %upper.3 = bf16[4,128,256]{2,1,0:T(8,128)(2,1)S(1)} custom-call(bf16[4,128,256]{2,1,0:T(8,128)(2,1)S(1)} %collective-permute-done.6.rows_ref, bf16[4,1024,512]{2,1,0:T(8,128)(2,1)S(1)} %keys_and_values.3.kv_ref), custom_call_target="tpu_custom_call" | custom-call | flops 4294967296 | bytes 4194304 | tf_op jit(solution)/shard_map/upper/pallas_call | solution.py:157
  60.2 0.1 collective-permute-start.10
  60.3 5.0 %collective-permute-start.9 = (bf16[4,128,256]{2,1,0:T(8,128)(2,1)S(1)}, bf16[4,128,256]{2,1,0:T(8,128)(2,1)S(1)}, u32[]{:S(2)}, u32[]{:S(2)}) collective-permute-start(bf16[4,128,256]{2,1,0:T(8,128)(2,1)S(1)} %lower.3), channel_id=1, source_target_pairs={{0,28},{4,0},{8,4},{12,8},{16,12},{20,16},{24,20},{28,24},{1,29},{... | collective-permute-start | bytes 786440 | tf_op jit(solution)/shard_map/ppermute | solution.py:24
  65.3 6.3 %own.3.refs_1_ = bf16[4,128,256]{2,1,0:T(8,128)(2,1)S(1)} custom-call(bf16[4,128,256]{2,1,0:T(8,128)(2,1)S(1)} %get-tuple-element.53.rows_ref, bf16[4,1024,512]{2,1,0:T(8,128)(2,1)S(1)} %keys_and_values.3.kv_ref), custom_call_target="tpu_custom_call" | custom-call | flops 4294967296 | bytes 4194304 | tf_op jit(solution)/shard_map/own/pallas_call | solution.py:157
  71.6 0.0 copy-start.4
  71.6 0.0 copy-start.6
  71.6 3.3 %partial_sum.1.partial_ref = f32[1024,256]{1,0:T(8,128)S(1)} custom-call(s32[3,1024]{1,0:T(4,128)S(1)} %reshape.12.codes_ref, bf16[4,128,256]{2,1,0:T(8,128)(2,1)S(1)} %own.2.refs_0_, bf16[4,128,256]{2,1,0:T(8,128)(2,1)S(1)} %own.3.refs_1_, bf16[4,128,256]{2,1,0:T(8,128)(2,1)S(1)} %collective-permute-done.7.refs_2_, ...), custom_call_target="tpu_custom_call" | custom-call | flops 3221225472 | bytes 2097152 | tf_op jit(solution)/shard_map/partial_sum/pallas_call | solution.py:202
  74.9 3.0 %finish.1 = bf16[1024,256]{1,0:T(8,128)(2,1)} custom-call(s32[3,1024]{1,0:T(4,128)S(1)} %reshape.12.codes_ref, f32[1024,256]{1,0:T(8,128)S(1)} %partial_sum.1.partial_ref, bf16[1024,256]{1,0:T(8,128)(2,1)S(1)} %bitcast.6, bf16[256,256]{1,0:T(8,128)(2,1)S(1)} %copy-done.6, bf16[4,128,256]{2,1,0:T(8,128)(2,1)S(1)} %collective-permute-done.9.refs_0_, ...), custom_call_target="tpu_custom_call" | custom-call | flops 1073741824 | bytes 2097152 | tf_op jit(solution)/shard_map/finish/pallas_call | solution.py:223
  (20 shorter events, 0.0 us)
Async XLA Ops:
  0.0 16.0 %collective-permute-start = (bf16[2048,256]{1,0:T(8,128)(2,1)}, bf16[2048,256]{1,0:T(8,128)(2,1)S(1)}, u32[]{:S(2)}, u32[]{:S(2)}) collective-permute-start(bf16[2048,256]{1,0:T(8,128)(2,1)} %refs_0_.1), channel_id=1, source_target_pairs={{0,1},{1,0},{2,3},{3,2},{4,5},{5,4},{6,7},{7,6},{8,9},{9,8},{10,11... | collective-permute-start | bytes 3145736 | tf_op jit(solution)/shard_map/ppermute | solution.py:29
  0.5 26.5 %collective-permute-start.3 = (bf16[2048,256]{1,0:T(8,128)(2,1)}, bf16[2048,256]{1,0:T(8,128)(2,1)S(1)}, u32[]{:S(2)}, u32[]{:S(2)}) collective-permute-start(bf16[2048,256]{1,0:T(8,128)(2,1)} %refs_0_.1), channel_id=1, source_target_pairs={{0,2},{1,3},{2,0},{3,1},{4,6},{5,7},{6,4},{7,5},{8,10},{9,11},{10,... | collective-permute-start | bytes 3145736 | tf_op jit(solution)/shard_map/ppermute | solution.py:29
  3.8 1.0 %copy-start.3 = (bf16[16,64,256]{2,1,0:T(8,128)(2,1)S(1)}, bf16[16,64,256]{2,1,0:T(8,128)(2,1)}, u32[]{:S(2)}) copy-start(bf16[16,64,256]{2,1,0:T(8,128)(2,1)} %param.9) | copy-start | bytes 1572868
  4.9 0.9 %copy-start.5 = (bf16[256,256]{1,0:T(8,128)(2,1)S(1)}, bf16[256,256]{1,0:T(8,128)(2,1)}, u32[]{:S(2)}) copy-start(bf16[256,256]{1,0:T(8,128)(2,1)} %weight_ref.2) | copy-start | bytes 393220
  5.8 0.7 copy-start.7
  6.5 9.5 %copy-start.1 = (bf16[256,256]{1,0:T(8,128)(2,1)S(1)}, bf16[256,256]{1,0:T(8,128)(2,1)}, u32[]{:S(2)}) copy-start(bf16[256,256]{1,0:T(8,128)(2,1)} %key_ref.3) | copy-start | bytes 393220
  6.5 9.5 %copy-start.2 = (bf16[256,256]{1,0:T(8,128)(2,1)S(1)}, bf16[256,256]{1,0:T(8,128)(2,1)}, u32[]{:S(2)}) copy-start(bf16[256,256]{1,0:T(8,128)(2,1)} %value_ref.3) | copy-start | bytes 393220
  9.7 6.3 %copy-start = (bf16[2048,256]{1,0:T(8,128)(2,1)S(1)}, bf16[2048,256]{1,0:T(8,128)(2,1)}, u32[]{:S(2)}) copy-start(bf16[2048,256]{1,0:T(8,128)(2,1)} %refs_0_.1) | copy-start | bytes 3145732
  9.7 22.1 %collective-permute-start.1 = (bf16[4,128,256]{2,1,0:T(8,128)(2,1)S(1)}, bf16[4,128,256]{2,1,0:T(8,128)(2,1)S(1)}, u32[]{:S(2)}, u32[]{:S(2)}) collective-permute-start(bf16[4,128,256]{2,1,0:T(8,128)(2,1)S(1)} %get-tuple-element.31), channel_id=1, source_target_pairs={{0,4},{4,8},{8,12},{12,16},{16,20},{20,24},{24,28},{28,0},{1,5},{5... | collective-permute-start | bytes 786440 | tf_op jit(solution)/shard_map/ppermute | solution.py:24
  11.2 20.6 %collective-permute-start.2 = (bf16[4,128,256]{2,1,0:T(8,128)(2,1)S(1)}, bf16[4,128,256]{2,1,0:T(8,128)(2,1)S(1)}, u32[]{:S(2)}, u32[]{:S(2)}) collective-permute-start(bf16[4,128,256]{2,1,0:T(8,128)(2,1)S(1)} %get-tuple-element.32), channel_id=1, source_target_pairs={{0,28},{4,0},{8,4},{12,8},{16,12},{20,16},{24,20},{28,24},{1,29},{... | collective-permute-start | bytes 786440 | tf_op jit(solution)/shard_map/ppermute | solution.py:24
  27.0 19.4 %collective-permute-start.4 = (bf16[2048,256]{1,0:T(8,128)(2,1)S(1)}, bf16[2048,256]{1,0:T(8,128)(2,1)S(1)}, u32[]{:S(2)}, u32[]{:S(2)}) collective-permute-start(bf16[2048,256]{1,0:T(8,128)(2,1)S(1)} %collective-permute-done.3.refs_0_), channel_id=1, source_target_pairs={{0,1},{1,0},{2,3},{3,2},{4,5},{5,4},{6,7},{7,6},{8,9},{9,8},{10,11... | collective-permute-start | bytes 3145736 | tf_op jit(solution)/shard_map/ppermute | solution.py:29
  27.0 20.6 %collective-permute-start.5 = (bf16[4,128,256]{2,1,0:T(8,128)(2,1)S(1)}, bf16[4,128,256]{2,1,0:T(8,128)(2,1)S(1)}, u32[]{:S(2)}, u32[]{:S(2)}) collective-permute-start(bf16[4,128,256]{2,1,0:T(8,128)(2,1)S(1)} %get-tuple-element.39), channel_id=1, source_target_pairs={{0,4},{4,8},{8,12},{12,16},{16,20},{20,24},{24,28},{28,0},{1,5},{5... | collective-permute-start | bytes 786440 | tf_op jit(solution)/shard_map/ppermute | solution.py:24
  28.8 18.9 %collective-permute-start.6 = (bf16[4,128,256]{2,1,0:T(8,128)(2,1)S(1)}, bf16[4,128,256]{2,1,0:T(8,128)(2,1)S(1)}, u32[]{:S(2)}, u32[]{:S(2)}) collective-permute-start(bf16[4,128,256]{2,1,0:T(8,128)(2,1)S(1)} %get-tuple-element.40), channel_id=1, source_target_pairs={{0,28},{4,0},{8,4},{12,8},{16,12},{20,16},{24,20},{28,24},{1,29},{... | collective-permute-start | bytes 786440 | tf_op jit(solution)/shard_map/ppermute | solution.py:24
  44.3 27.3 %collective-permute-start.7 = (bf16[4,128,256]{2,1,0:T(8,128)(2,1)S(1)}, bf16[4,128,256]{2,1,0:T(8,128)(2,1)S(1)}, u32[]{:S(2)}, u32[]{:S(2)}) collective-permute-start(bf16[4,128,256]{2,1,0:T(8,128)(2,1)S(1)} %lower.2), channel_id=1, source_target_pairs={{0,28},{4,0},{8,4},{12,8},{16,12},{20,16},{24,20},{28,24},{1,29},{... | collective-permute-start | bytes 786440 | tf_op jit(solution)/shard_map/ppermute | solution.py:24
  46.4 25.2 %collective-permute-start.8 = (bf16[4,128,256]{2,1,0:T(8,128)(2,1)S(1)}, bf16[4,128,256]{2,1,0:T(8,128)(2,1)S(1)}, u32[]{:S(2)}, u32[]{:S(2)}) collective-permute-start(bf16[4,128,256]{2,1,0:T(8,128)(2,1)S(1)} %upper.2), channel_id=1, source_target_pairs={{0,4},{4,8},{8,12},{12,16},{16,20},{20,24},{24,28},{28,0},{1,5},{5... | collective-permute-start | bytes 786440 | tf_op jit(solution)/shard_map/ppermute | solution.py:24
  60.2 14.7 %collective-permute-start.10 = (bf16[4,128,256]{2,1,0:T(8,128)(2,1)S(1)}, bf16[4,128,256]{2,1,0:T(8,128)(2,1)S(1)}, u32[]{:S(2)}, u32[]{:S(2)}) collective-permute-start(bf16[4,128,256]{2,1,0:T(8,128)(2,1)S(1)} %upper.3), channel_id=1, source_target_pairs={{0,4},{4,8},{8,12},{12,16},{16,20},{20,24},{24,28},{28,0},{1,5},{5... | collective-permute-start | bytes 786440 | tf_op jit(solution)/shard_map/ppermute | solution.py:24
  60.3 14.6 %collective-permute-start.9 = (bf16[4,128,256]{2,1,0:T(8,128)(2,1)S(1)}, bf16[4,128,256]{2,1,0:T(8,128)(2,1)S(1)}, u32[]{:S(2)}, u32[]{:S(2)}) collective-permute-start(bf16[4,128,256]{2,1,0:T(8,128)(2,1)S(1)} %lower.3), channel_id=1, source_target_pairs={{0,28},{4,0},{8,4},{12,8},{16,12},{20,16},{24,20},{28,24},{1,29},{... | collective-permute-start | bytes 786440 | tf_op jit(solution)/shard_map/ppermute | solution.py:24
  71.6 3.3 %copy-start.4 = (bf16[16,64,256]{2,1,0:T(8,128)(2,1)S(1)}, bf16[16,64,256]{2,1,0:T(8,128)(2,1)}, u32[]{:S(2)}) copy-start(bf16[16,64,256]{2,1,0:T(8,128)(2,1)} %param.9) | copy-start | bytes 1572868
  71.6 3.3 %copy-start.6 = (bf16[256,256]{1,0:T(8,128)(2,1)S(1)}, bf16[256,256]{1,0:T(8,128)(2,1)}, u32[]{:S(2)}) copy-start(bf16[256,256]{1,0:T(8,128)(2,1)} %weight_ref.3) | copy-start | bytes 393220
where the time goes:
time: 78.2 us; the launch traced here: 77.9 us
  Pallas kernels  51 us (65%)
  starting transfers between devices  19.7 us (25%)
  waiting for transfers between devices  3.53 us (5%)
  local copies, waits for them, and re-layouts  2.73 us (3%)
    pallas_call x6, Pallas kernels, attend(): pl.pallas_call(functools.partial(attend_kernel, stack=stack), out_shape=j...  37.5 us
    ppermute x8, starting transfers between devices, shifted(): lax.ppermute(block, axis, [(i, (i + distance) % count) for i in range(cou...  16.7 us
    ppermute x3, waiting for transfers between devices, swapped(): return lax.ppermute(block, axis, [(i, i ^ bit) for i in range(count)])  3.51 us
    pallas_call x1, Pallas kernels, partial_sum(): pl.pallas_call(functools.partial(partial_kernel, bases=bases), out_shape=...  3.26 us
    pallas_call x1, Pallas kernels, project(): pl.pallas_call(project_kernel, out_shape=(jax.ShapeDtypeStruct((count, wi...  3.2 us
    pallas_call x1, Pallas kernels, finish(): pl.pallas_call(functools.partial(final_kernel, bases=bases), out_shape=ja...  3 us
    ppermute x3, starting transfers between devices, swapped(): return lax.ppermute(block, axis, [(i, i ^ bit) for i in range(count)])  3 us
    unnamed x16, local copies, waits for them, and re-layouts  2.65 us
  transfers between devices with their start and end apart: 11, of which 1 were waited for; matrix products, arithmetic and copies ran while one was open for 1% of the time, Pallas kernels for 62%

commit v1 on v0

--- a/solution.py
+++ b/solution.py
@@ -7,6 +7,7 @@
 from jax.experimental.pallas import tpu as pltpu
 from jax.sharding import PartitionSpec as P
 
+
 HEADS = 8
 BLK_DEV = 8
 CAP = 128
@@ -32,18 +33,29 @@
 def fill_slots(codes_ref, rows, out_refs, group):
     blocks = out_refs[0].shape[0]
     queries = rows.shape[0]
+    codes = codes_ref[...]
+    slot = lax.broadcasted_iota(jnp.int32, (2 * CAP, queries), 0).astype(jnp.int16)
+    one, zero = jnp.ones((), jnp.bfloat16), jnp.zeros((), jnp.bfloat16)
     for step in range(0, BLK_DEV, 2):
-        slot = lax.broadcasted_iota(jnp.int32, (2 * CAP, queries), 0) + (group * BLK_DEV + step) * CAP
-        hit = slot == codes_ref[0:1, :]
-        for entry in range(1, codes_ref.shape[0]):
-            hit = hit | (slot == codes_ref[entry:entry + 1, :])
-        pick = jnp.where(hit, 1.0, 0.0).astype(jnp.bfloat16)
-        got = jnp.dot(pick, rows, preferred_element_type=jnp.float32).astype(jnp.bfloat16)
+        near = (codes - (group * BLK_DEV + step) * CAP).astype(jnp.int16)
+        hit = slot == near[0:1, :]
+        for entry in range(1, codes.shape[0]):
+            hit = hit | (slot == near[entry:entry + 1, :])
+        got = jnp.dot(jnp.where(hit, one, zero), rows, preferred_element_type=jnp.float32).astype(jnp.bfloat16)
         at = step % blocks
         out_refs[step // blocks][at:at + 2] = got.reshape(2, CAP, got.shape[1])
 
 
-def project_kernel(codes_ref, queries_ref, gain_ref, weight_ref, rows_ref, *slot_refs):
+def project_kernel(codes_ref, queries_hbm, gain_hbm, weight_hbm, rows_ref, *refs):
+    slot_refs, (queries_ref, gain_ref, weight_ref, sems) = refs[:-4], refs[-4:]
+    copies = [
+        pltpu.make_async_copy(source, target, sems.at[i])
+        for i, (source, target) in enumerate(((queries_hbm, queries_ref), (gain_hbm, gain_ref), (weight_hbm, weight_ref)))
+    ]
+    for copy in copies:
+        copy.start()
+    for copy in copies:
+        copy.wait()
     values = queries_ref[...].astype(jnp.float32)
     average = jnp.mean(values, axis=-1, keepdims=True)
     centred = values - average
@@ -62,8 +74,16 @@
 
 def project(codes, queries, gain, weight, parts):
     count, width = queries.shape
+    hbm = pl.BlockSpec(memory_space=pltpu.HBM)
     return pl.pallas_call(
         project_kernel,
+        in_specs=[pl.BlockSpec(memory_space=pltpu.VMEM), hbm, hbm, hbm],
+        scratch_shapes=[
+            pltpu.VMEM(queries.shape, queries.dtype),
+            pltpu.VMEM(gain.shape, gain.dtype),
+            pltpu.VMEM(weight.shape, weight.dtype),
+            pltpu.SemaphoreType.DMA((3,)),
+        ],
         out_shape=(jax.ShapeDtypeStruct((count, width), jnp.bfloat16),) + 2 * slot_shapes(parts, width),
         compiler_params=params(),
         cost_estimate=pl.CostEstimate(flops=4 << 30, bytes_accessed=2 << 20, transcendentals=0),
@@ -116,12 +136,14 @@
     factor = head_size ** (-0.5) * LOG2_E
     head_of = lax.broadcasted_iota(jnp.int32, (1, width), 1) // head_size
     firsts = list(range(0, HEADS, stack))
+    half = width // 2
 
     def scores_of(b, first):
-        rows = rows_ref[b]
-        kept = [jnp.where(head_of == first + i, rows, jnp.zeros_like(rows)) for i in range(stack)]
+        side = slice(half * (first >= HEADS // 2), half * (first >= HEADS // 2) + half)
+        rows = rows_ref[b, :, side]
+        kept = [jnp.where(head_of[:, side] == first + i, rows, jnp.zeros_like(rows)) for i in range(stack)]
         return lax.dot_general(
-            jnp.concatenate(kept, axis=0), kv_ref[b, :, :width],
+            jnp.concatenate(kept, axis=0), kv_ref[b, :, side],
             (((1,), (1,)), ((), ())), preferred_element_type=jnp.float32)
 
     scores_ref[...] = scores_of(0, 0)
@@ -149,7 +171,7 @@
         scores_ref[...] = scores
 
 
-def attend(rows, kv, name):
+def attend(rows, kv):
     blocks, count, width = rows.shape
     keys = kv.shape[1]
     stack = 2
@@ -162,71 +184,83 @@
         cost_estimate=pl.CostEstimate(
             flops=4 * pairs * width * HEADS, bytes_accessed=blocks * keys * width * 4,
             transcendentals=pairs * HEADS),
-        name=name,
     )(rows, kv)
 
 
-def gathered(codes_ref, result_refs, at):
-    entries = codes_ref.shape[1]
-    count = at.shape[0]
+def pick_kernel(codes_ref, *out_refs, groups):
+    entries, count = codes_ref.shape
+    spare = jnp.zeros((8 - entries, count), jnp.int32)
+    at = jnp.concatenate([codes_ref[...], spare], axis=0).T
+    lane = lax.broadcasted_iota(jnp.int32, (count, CAP), 1).astype(jnp.int16)
+    near = [jnp.broadcast_to(at[:, entry:entry + 1], (count, CAP)).astype(jnp.int16) for entry in range(entries)]
+    one, zero = jnp.ones((), jnp.bfloat16), jnp.zeros((), jnp.bfloat16)
+    for group, out_ref in zip(groups, out_refs):
+        for step in range(out_ref.shape[1] // CAP):
+            slot = lane + jnp.int16(group * BLK_DEV * CAP + step * CAP)
+            hit = slot == near[0]
+            for entry in range(1, entries):
+                hit = hit | (slot == near[entry])
+            out_ref[:, step * CAP:(step + 1) * CAP] = jnp.where(hit, one, zero)
+
+
+def picks(codes, groups):
+    shape = jax.ShapeDtypeStruct((codes.shape[1], BLK_DEV * CAP), jnp.bfloat16)
+    return pl.pallas_call(
+        functools.partial(pick_kernel, groups=groups),
+        out_shape=(shape,) * len(groups),
+        compiler_params=params(),
+        cost_estimate=pl.CostEstimate(flops=1 << 30, bytes_accessed=2 << 20, transcendentals=0),
+        name="picks",
+    )(codes)
+
+
+def gathered(pick_refs, result_refs, places, rows):
     total = None
-    for base, ref in result_refs:
+    for ref, (group, first) in zip(result_refs, places):
         slots = ref.shape[0] * ref.shape[1]
-        slot = lax.broadcasted_iota(jnp.int32, (count, slots), 1) + base
-        hit = slot == at[:, 0:1]
-        for entry in range(1, 3):
-            hit = hit | (slot == at[:, entry:entry + 1])
-        pick = jnp.where(hit, 1.0, 0.0).astype(jnp.bfloat16)
-        got = jnp.dot(pick, ref[...].reshape(slots, ref.shape[2]), preferred_element_type=jnp.float32)
+        got = jnp.dot(
+            pick_refs[group][rows, first:first + slots], ref[...].reshape(slots, ref.shape[2]),
+            preferred_element_type=jnp.float32)
         total = got if total is None else total + got
     return total
 
 
-def columns_of(codes_ref):
-    entries, count = codes_ref.shape
-    spare = jnp.full((8 - entries, count), -1, jnp.int32)
-    return jnp.concatenate([codes_ref[...], spare], axis=0).T
-
-
-def partial_kernel(codes_ref, *refs, bases):
-    out_ref = refs[-1]
-    at = columns_of(codes_ref)
+def partial_kernel(*refs, places):
+    pick_refs, result_refs, out_ref = refs[:3], refs[3:-1], refs[-1]
     tile = 256
     for step in range(out_ref.shape[0] // tile):
         rows = slice(step * tile, (step + 1) * tile)
-        out_ref[rows] = gathered(codes_ref, list(zip(bases, refs[:-1])), at[rows])
-
-
-def partial_sum(codes, results, bases):
-    width = results[0].shape[2]
-    return pl.pallas_call(
-        functools.partial(partial_kernel, bases=bases),
-        out_shape=jax.ShapeDtypeStruct((codes.shape[1], width), jnp.float32),
-        compiler_params=params(),
-        cost_estimate=pl.CostEstimate(flops=3 << 30, bytes_accessed=2 << 20, transcendentals=0),
+        out_ref[rows] = gathered(pick_refs, result_refs, places, rows)
+
+
+def partial_sum(selected, results, places):
+    return pl.pallas_call(
+        functools.partial(partial_kernel, places=places),
+        out_shape=jax.ShapeDtypeStruct((selected[0].shape[0], results[0].shape[2]), jnp.float32),
+        compiler_params=params(),
+        cost_estimate=pl.CostEstimate(flops=1 << 30, bytes_accessed=2 << 20, transcendentals=0),
         name="partial_sum",
-    )(codes, *results)
-
-
-def final_kernel(codes_ref, partial_ref, queries_ref, weight_ref, *refs, bases):
-    out_ref = refs[-1]
-    at = columns_of(codes_ref)
+    )(*selected, *results)
+
+
+def final_kernel(partial_ref, queries_ref, weight_ref, *refs, places):
+    pick_refs, result_refs, out_ref = refs[:3], refs[3:-1], refs[-1]
     tile = 256
     for step in range(out_ref.shape[0] // tile):
         rows = slice(step * tile, (step + 1) * tile)
-        total = partial_ref[rows] + gathered(codes_ref, list(zip(bases, refs[:-1])), at[rows])
+        total = partial_ref[rows] + gathered(pick_refs, result_refs, places, rows)
         final = jnp.dot(total.astype(jnp.bfloat16), weight_ref[...], preferred_element_type=jnp.float32)
         out_ref[rows] = (final + queries_ref[rows].astype(jnp.float32)).astype(jnp.bfloat16)
 
 
-def finish(codes, partial, queries, weight, results, bases):
-    return pl.pallas_call(
-        functools.partial(final_kernel, bases=bases),
+def finish(partial, queries, weight, selected, results, places):
+    return pl.pallas_call(
+        functools.partial(final_kernel, places=places),
         out_shape=jax.ShapeDtypeStruct(queries.shape, jnp.bfloat16),
         compiler_params=params(),
         cost_estimate=pl.CostEstimate(flops=1 << 30, bytes_accessed=2 << 20, transcendentals=0),
         name="finish",
-    )(codes, partial, queries, weight, *results)
+    )(partial, queries, weight, *selected, *results)
 
 
 def shards(queries, norm_gain, w_query, w_key, w_value, w_out, features, visible, live):
@@ -256,42 +290,43 @@
     blocks = BLK_DEV // parts
 
     projected, *slots = project(codes, rows_in, norm_gain.reshape(1, width), w_query, parts)
-    lower = [shifted(part, "sector", 1) for part in slots[:parts]]
-    upper = [shifted(part, "sector", -1) for part in slots[parts:]]
+    lower, upper = [], []
+    for part in range(parts):
+        lower.append(shifted(slots[part], "sector", 1))
+        upper.append(shifted(slots[parts + part], "sector", -1))
     projected, *_ = lax.optimization_barrier((projected, *slots))
     own = list(scatter(codes, projected, parts))
     kv = keys_and_values(held[0], w_key, w_value, keys)
-    own[0] = attend(own[0], kv, "own")
-
-    if staged:
-        across, own[0] = lax.optimization_barrier((across, own[0]))
-        held.append([across, swapped(across, "band", 1)])
+    own[0] = attend(own[0], kv)
+    codes, own[0] = lax.optimization_barrier((codes, own[0]))
+    selected = picks(codes, (0, 1, 2))
 
     def visit(part, kv, before):
-        kv, first, second, before = lax.optimization_barrier((kv, lower[part], upper[part], before))
-        first = attend(first, kv, "lower")
+        kv, first, before = lax.optimization_barrier((kv, lower[part], before))
+        second = upper[part]
+        first = attend(first, kv)
         second, first = lax.optimization_barrier((second, first))
-        second = attend(second, kv, "upper")
+        middle = first
+        second = attend(second, kv)
         first, second = lax.optimization_barrier((first, second))
-        return (shifted(first, "sector", -1), shifted(second, "sector", 1)), before, second
-
-    sent, own[0], last = visit(0, kv, own[0])
+        return (shifted(first, "sector", -1), shifted(second, "sector", 1)), before, middle, second
+
+    sent, selected, middle, last = visit(0, kv, selected)
     back = [sent]
     if staged:
-        kv = keys_and_values(held[1], w_key, w_value, keys)
-        sent, _, last = visit(1, kv, last)
+        across, middle = lax.optimization_barrier((across, middle))
+        kv = keys_and_values([across, swapped(across, "band", 1)], w_key, w_value, keys)
+        sent, _, _, last = visit(1, kv, last)
         back.append(sent)
         own[1], _ = lax.optimization_barrier((own[1], last))
-        own[1] = attend(own[1], kv, "own")
-
-    def base(group, part):
-        return (group * BLK_DEV + part * blocks) * CAP
-
-    early = [(base(1, i), rows) for i, rows in enumerate(own)]
-    early += [(base(2 - 2 * side, 0), back[0][side]) for side in range(2)] if staged else []
-    late = [(base(2 - 2 * side, parts - 1), back[-1][side]) for side in range(2)]
-    partial = partial_sum(codes, [rows for _, rows in early], tuple(at for at, _ in early))
-    out = finish(codes, partial, rows_in, w_out, [rows for _, rows in late], tuple(at for at, _ in late))
+        own[1] = attend(own[1], kv)
+
+    slots_of = blocks * CAP
+    early = [((1, i * slots_of), rows) for i, rows in enumerate(own)]
+    early += [((2 - 2 * side, 0), back[0][side]) for side in range(2)] if staged else []
+    late = [((2 - 2 * side, (parts - 1) * slots_of), back[-1][side]) for side in range(2)]
+    partial = partial_sum(selected, [rows for _, rows in early], tuple(at for at, _ in early))
+    out = finish(partial, rows_in, w_out, selected, [rows for _, rows in late], tuple(at for at, _ in late))
     return out.reshape(azim_cells, range_cells, width)
 
 

time: 78.2 us -> 78.2 us (level)
  Pallas kernels: 51 us -> 47.5 us
  waiting for transfers between devices: 3.53 us -> 6.23 us
  starting transfers between devices: 19.7 us -> 20.6 us
    ppermute x8, waiting for transfers between devices: 0.02 us -> 6.22 us  [shifted(): lax.ppermute(block, axis, [(i, (i + distance) % count) for i in range(cou...]
    ppermute x3, waiting for transfers between devices: 3.51 us -> 0.01 us  [swapped(): return lax.ppermute(block, axis, [(i, i ^ bit) for i in range(count)])]
    pallas_call x6, Pallas kernels: 37.5 us -> 36.1 us  [attend(): pl.pallas_call(functools.partial(attend_kernel, stack=stack), out_shape=j...]
    pallas_call x3 -> x4, Pallas kernels: 9.46 us -> 8.14 us  [the longest x1 2.51 us: finish(): pl.pallas_call(functools.partial(final_kernel, places=places), out_shape=...]
    ppermute x8, starting transfers between devices: 16.7 us -> 17.5 us  [shifted(): lax.ppermute(block, axis, [(i, (i + distance) % count) for i in range(cou...]
  transfers between devices with their start and end apart: 11 -> 11, of which waited for: 1 -> 2; matrix products, arithmetic and copies ran while one was open for 1% -> 1% of each run, Pallas kernels for 62% -> 58%
where the time goes in v1:
time: 78.2 us; the launch traced here: 78 us
  Pallas kernels  47.5 us (61%)
  starting transfers between devices  20.6 us (26%)
  waiting for transfers between devices  6.23 us (8%)
  local copies, waits for them, and re-layouts  2.74 us (4%)
    pallas_call x6, Pallas kernels, attend(): pl.pallas_call(functools.partial(attend_kernel, stack=stack), out_shape=j...  36.1 us
    ppermute x8, starting transfers between devices, shifted(): lax.ppermute(block, axis, [(i, (i + distance) % count) for i in range(cou...  17.5 us
    ppermute x8, waiting for transfers between devices, shifted(): lax.ppermute(block, axis, [(i, (i + distance) % count) for i in range(cou...  6.22 us
    ppermute x3, starting transfers between devices, swapped(): return lax.ppermute(block, axis, [(i, i ^ bit) for i in range(count)])  3.07 us
    unnamed x16, local copies, waits for them, and re-layouts  2.66 us
    pallas_call x1, Pallas kernels, finish(): pl.pallas_call(functools.partial(final_kernel, places=places), out_shape=...  2.51 us
    pallas_call x2, Pallas kernels, keys_and_values(): pl.pallas_call(kv_kernel, out_shape=jax.ShapeDtypeStruct((count // keys,...  2.51 us
    pallas_call x1, Pallas kernels, picks(): pl.pallas_call(functools.partial(pick_kernel, groups=groups), out_shape=(...  2.5 us
  transfers between devices with their start and end apart: 11, of which 2 were waited for; matrix products, arithmetic and copies ran while one was open for 1% of the time, Pallas kernels for 58%

profile of v1, /device:TPU:0, one launch (start us, length us, event | category | flops | bytes accessed | tf_op | source)
XLA Modules:
  0.0 78.0 jit_solution(6914376453207957491)
XLA Ops:
  0.0 0.5 collective-permute-start
  0.5 2.5 %collective-permute-start.3 = (bf16[2048,256]{1,0:T(8,128)(2,1)}, bf16[2048,256]{1,0:T(8,128)(2,1)S(1)}, u32[]{:S(2)}, u32[]{:S(2)}) collective-permute-start(bf16[2048,256]{1,0:T(8,128)(2,1)} %refs_0_.1), channel_id=1, source_target_pairs={{0,2},{1,3},{2,0},{3,1},{4,6},{5,7},{6,4},{7,5},{8,10},{9,11},{10,... | collective-permute-start | bytes 3145736 | tf_op jit(solution)/shard_map/ppermute | solution.py:30
  3.0 0.8 select_bitcast_fusion
  3.8 0.1 reshape.12.codes_ref
  3.8 1.0 %copy-done.1 = bf16[16,64,256]{2,1,0:T(8,128)(2,1)S(1)} copy-done((bf16[16,64,256]{2,1,0:T(8,128)(2,1)S(1)}, bf16[16,64,256]{2,1,0:T(8,128)(2,1)}, u32[]{:S(2)}) %copy-start.1) | copy-done | bytes 524312
  4.9 0.9 %copy-done.6 = bf16[256,256]{1,0:T(8,128)(2,1)S(1)} copy-done((bf16[256,256]{1,0:T(8,128)(2,1)S(1)}, bf16[256,256]{1,0:T(8,128)(2,1)}, u32[]{:S(2)}) %copy-start.6) | copy-done | bytes 131096
  5.8 0.7 copy-done.7
  6.5 1.9 %project.1 = (bf16[1024,256]{1,0:T(8,128)(2,1)S(1)}, bf16[4,128,256]{2,1,0:T(8,128)(2,1)S(1)}, bf16[4,128,256]{2,1,0:T(8,128)(2,1)S(1)}, bf16[4,128,256]{2,1,0:T(8,128)(2,1)S(1)}, bf16[4,128,256]{2,1,0:T(8,128)(2,1)S(1)}) custom-call(s32[3,1024]{1,0:T(4,128)S(1)} %reshape.12.codes_ref, bf16[1024,256]{1,0:T(8,128)(2,1)S(1)} %bitcast.5, f32[1,256]{1,0:T(1,128)S(1)} %bitcast.7, ...), custom_call_target="tpu_custom_call" | custom-call | flops 4294967296 | bytes 2097152 | tf_op jit(solution)/shard_map/project/pallas_call | solution.py:78
  8.4 0.0 copy-start
  8.4 1.5 %collective-permute-start.1 = (bf16[4,128,256]{2,1,0:T(8,128)(2,1)S(1)}, bf16[4,128,256]{2,1,0:T(8,128)(2,1)S(1)}, u32[]{:S(2)}, u32[]{:S(2)}) collective-permute-start(bf16[4,128,256]{2,1,0:T(8,128)(2,1)S(1)} %get-tuple-element.35), channel_id=1, source_target_pairs={{0,4},{4,8},{8,12},{12,16},{16,20},{20,24},{24,28},{28,0},{1,5},{5... | collective-permute-start | bytes 786440 | tf_op jit(solution)/shard_map/ppermute | solution.py:25
  10.0 3.2 %collective-permute-start.4 = (bf16[4,128,256]{2,1,0:T(8,128)(2,1)S(1)}, bf16[4,128,256]{2,1,0:T(8,128)(2,1)S(1)}, u32[]{:S(2)}, u32[]{:S(2)}) collective-permute-start(bf16[4,128,256]{2,1,0:T(8,128)(2,1)S(1)} %get-tuple-element.48), channel_id=1, source_target_pairs={{0,28},{4,0},{8,4},{12,8},{16,12},{20,16},{24,20},{28,24},{1,29},{... | collective-permute-start | bytes 786440 | tf_op jit(solution)/shard_map/ppermute | solution.py:25
  13.2 0.7 scatter.1
  14.0 1.3 %keys_and_values.2.kv_ref = bf16[4,1024,512]{2,1,0:T(8,128)(2,1)S(1)} custom-call(bf16[256,256]{1,0:T(8,128)(2,1)S(1)} %copy-done.3, bf16[256,256]{1,0:T(8,128)(2,1)S(1)} %copy-done.4, bf16[2048,256]{1,0:T(8,128)(2,1)S(1)} %copy-done, bf16[2048,256]{1,0:T(8,128)(2,1)S(1)} %collective-permute-done.refs_1_), custom_call_target="tpu_custom_call" | custom-call | flops 1073741824 | bytes 6291456 | tf_op jit(solution)/shard_map/keys_and_values/pallas_call | solution.py:124
  15.2 6.1 %shard_map.91.refs_3_ = bf16[4,128,256]{2,1,0:T(8,128)(2,1)S(1)} custom-call(bf16[4,128,256]{2,1,0:T(8,128)(2,1)S(1)} %get-tuple-element.37.rows_ref, bf16[4,1024,512]{2,1,0:T(8,128)(2,1)S(1)} %keys_and_values.2.kv_ref), custom_call_target="tpu_custom_call" | custom-call | flops 4294967296 | bytes 4194304 | tf_op jit(solution)/shard_map/pallas_call | solution.py:179
  21.3 2.5 %picks.1 = (bf16[1024,1024]{1,0:T(8,128)(2,1)S(1)}, bf16[1024,1024]{1,0:T(8,128)(2,1)S(1)}, bf16[1024,1024]{1,0:T(8,128)(2,1)S(1)}) custom-call(s32[3,1024]{1,0:T(4,128)S(1)} %reshape.12.codes_ref), custom_call_target="tpu_custom_call" | custom-call | flops 1073741824 | bytes 2097152 | tf_op jit(solution)/shard_map/picks/pallas_call | solution.py:208
  23.8 6.0 %shard_map.92 = bf16[4,128,256]{2,1,0:T(8,128)(2,1)S(1)} custom-call(bf16[4,128,256]{2,1,0:T(8,128)(2,1)S(1)} %collective-permute-done.1.rows_ref, bf16[4,1024,512]{2,1,0:T(8,128)(2,1)S(1)} %keys_and_values.2.kv_ref), custom_call_target="tpu_custom_call" | custom-call | flops 4294967296 | bytes 4194304 | tf_op jit(solution)/shard_map/pallas_call | solution.py:179
  29.8 0.1 collective-permute-start.5
  29.9 0.3 collective-permute-start.6
  30.2 4.5 %collective-permute-start.2 = (bf16[4,128,256]{2,1,0:T(8,128)(2,1)S(1)}, bf16[4,128,256]{2,1,0:T(8,128)(2,1)S(1)}, u32[]{:S(2)}, u32[]{:S(2)}) collective-permute-start(bf16[4,128,256]{2,1,0:T(8,128)(2,1)S(1)} %get-tuple-element.47), channel_id=1, source_target_pairs={{0,28},{4,0},{8,4},{12,8},{16,12},{20,16},{24,20},{28,24},{1,29},{... | collective-permute-start | bytes 786440 | tf_op jit(solution)/shard_map/ppermute | solution.py:25
  34.7 6.0 %shard_map.93 = bf16[4,128,256]{2,1,0:T(8,128)(2,1)S(1)} custom-call(bf16[4,128,256]{2,1,0:T(8,128)(2,1)S(1)} %collective-permute-done.4.rows_ref, bf16[4,1024,512]{2,1,0:T(8,128)(2,1)S(1)} %keys_and_values.2.kv_ref), custom_call_target="tpu_custom_call" | custom-call | flops 4294967296 | bytes 4194304 | tf_op jit(solution)/shard_map/pallas_call | solution.py:179
  40.7 0.6 collective-permute-start.7
  41.3 1.5 %collective-permute-start.8 = (bf16[4,128,256]{2,1,0:T(8,128)(2,1)S(1)}, bf16[4,128,256]{2,1,0:T(8,128)(2,1)S(1)}, u32[]{:S(2)}, u32[]{:S(2)}) collective-permute-start(bf16[4,128,256]{2,1,0:T(8,128)(2,1)S(1)} %shard_map.93), channel_id=1, source_target_pairs={{0,4},{4,8},{8,12},{12,16},{16,20},{20,24},{24,28},{28,0},{1,5},{5... | collective-permute-start | bytes 786440 | tf_op jit(solution)/shard_map/ppermute | solution.py:25
  42.8 1.3 %keys_and_values.3.kv_ref = bf16[4,1024,512]{2,1,0:T(8,128)(2,1)S(1)} custom-call(bf16[256,256]{1,0:T(8,128)(2,1)S(1)} %copy-done.3, bf16[256,256]{1,0:T(8,128)(2,1)S(1)} %copy-done.4, bf16[2048,256]{1,0:T(8,128)(2,1)S(1)} %collective-permute-done.3.refs_0_, bf16[2048,256]{1,0:T(8,128)(2,1)S(1)} %collective-permute-done.5.refs_1_), custom_call_target="tpu_custom_call" | custom-call | flops 1073741824 | bytes 6291456 | tf_op jit(solution)/shard_map/keys_and_values/pallas_call | solution.py:124
  44.0 4.1 %collective-permute-done.6.rows_ref = bf16[4,128,256]{2,1,0:T(8,128)(2,1)S(1)} collective-permute-done((bf16[4,128,256]{2,1,0:T(8,128)(2,1)S(1)}, bf16[4,128,256]{2,1,0:T(8,128)(2,1)S(1)}, u32[]{:S(2)}, u32[]{:S(2)}) %collective-permute-start.6) | collective-permute-done | bytes 262176 | tf_op jit(solution)/shard_map/ppermute | solution.py:25
  48.1 6.1 %shard_map.94 = bf16[4,128,256]{2,1,0:T(8,128)(2,1)S(1)} custom-call(bf16[4,128,256]{2,1,0:T(8,128)(2,1)S(1)} %collective-permute-done.6.rows_ref, bf16[4,1024,512]{2,1,0:T(8,128)(2,1)S(1)} %keys_and_values.3.kv_ref), custom_call_target="tpu_custom_call" | custom-call | flops 4294967296 | bytes 4194304 | tf_op jit(solution)/shard_map/pallas_call | solution.py:179
  54.2 6.0 %shard_map.95 = bf16[4,128,256]{2,1,0:T(8,128)(2,1)S(1)} custom-call(bf16[4,128,256]{2,1,0:T(8,128)(2,1)S(1)} %collective-permute-done.2.rows_ref, bf16[4,1024,512]{2,1,0:T(8,128)(2,1)S(1)} %keys_and_values.3.kv_ref), custom_call_target="tpu_custom_call" | custom-call | flops 4294967296 | bytes 4194304 | tf_op jit(solution)/shard_map/pallas_call | solution.py:179
  60.2 2.5 %collective-permute-start.10 = (bf16[4,128,256]{2,1,0:T(8,128)(2,1)S(1)}, bf16[4,128,256]{2,1,0:T(8,128)(2,1)S(1)}, u32[]{:S(2)}, u32[]{:S(2)}) collective-permute-start(bf16[4,128,256]{2,1,0:T(8,128)(2,1)S(1)} %shard_map.95), channel_id=1, source_target_pairs={{0,4},{4,8},{8,12},{12,16},{16,20},{20,24},{24,28},{28,0},{1,5},{5... | collective-permute-start | bytes 786440 | tf_op jit(solution)/shard_map/ppermute | solution.py:25
  62.7 3.3 %collective-permute-start.9 = (bf16[4,128,256]{2,1,0:T(8,128)(2,1)S(1)}, bf16[4,128,256]{2,1,0:T(8,128)(2,1)S(1)}, u32[]{:S(2)}, u32[]{:S(2)}) collective-permute-start(bf16[4,128,256]{2,1,0:T(8,128)(2,1)S(1)} %shard_map.94), channel_id=1, source_target_pairs={{0,28},{4,0},{8,4},{12,8},{16,12},{20,16},{24,20},{28,24},{1,29},{... | collective-permute-start | bytes 786440 | tf_op jit(solution)/shard_map/ppermute | solution.py:25
  66.0 6.0 %shard_map.96.refs_4_ = bf16[4,128,256]{2,1,0:T(8,128)(2,1)S(1)} custom-call(bf16[4,128,256]{2,1,0:T(8,128)(2,1)S(1)} %get-tuple-element.61.rows_ref, bf16[4,1024,512]{2,1,0:T(8,128)(2,1)S(1)} %keys_and_values.3.kv_ref), custom_call_target="tpu_custom_call" | custom-call | flops 4294967296 | bytes 4194304 | tf_op jit(solution)/shard_map/pallas_call | solution.py:179
  72.1 1.2 %partial_sum.1.partial_ref = f32[1024,256]{1,0:T(8,128)S(1)} custom-call(bf16[1024,1024]{1,0:T(8,128)(2,1)S(1)} %get-tuple-element.42.refs_0_, bf16[1024,1024]{1,0:T(8,128)(2,1)S(1)} %get-tuple-element.43.refs_1_, bf16[1024,1024]{1,0:T(8,128)(2,1)S(1)} %get-tuple-element.44.refs_2_, bf16[4,128,256]{2,1,0:T(8,128)(2,1)S(1)} %shard_map.91.refs_3_, ...), custom_call_target="tpu_custom_call" | custom-call | flops 1073741824 | bytes 2097152 | tf_op jit(solution)/shard_map/partial_sum/pallas_call | solution.py:237
  73.3 2.1 %collective-permute-done.9.refs_3_ = bf16[4,128,256]{2,1,0:T(8,128)(2,1)S(1)} collective-permute-done((bf16[4,128,256]{2,1,0:T(8,128)(2,1)S(1)}, bf16[4,128,256]{2,1,0:T(8,128)(2,1)S(1)}, u32[]{:S(2)}, u32[]{:S(2)}) %collective-permute-start.9) | collective-permute-done | bytes 262176 | tf_op jit(solution)/shard_map/ppermute | solution.py:25
  75.5 2.5 %finish.1 = bf16[1024,256]{1,0:T(8,128)(2,1)} custom-call(f32[1024,256]{1,0:T(8,128)S(1)} %partial_sum.1.partial_ref, bf16[1024,256]{1,0:T(8,128)(2,1)S(1)} %bitcast.6, bf16[256,256]{1,0:T(8,128)(2,1)S(1)} %copy-done.5, bf16[1024,1024]{1,0:T(8,128)(2,1)S(1)} %get-tuple-element.42.refs_0_, bf16[1024,1024]{1,0:T(8,128)(2,1)S(1)} %get-tuple-element.43.refs_1_, ...), custom_call_target="tpu_custom_call" | custom-call | flops 1073741824 | bytes 2097152 | tf_op jit(solution)/shard_map/finish/pallas_call | solution.py:257
  (21 shorter events, 0.1 us)
Async XLA Ops:
  0.0 13.9 %collective-permute-start = (bf16[2048,256]{1,0:T(8,128)(2,1)}, bf16[2048,256]{1,0:T(8,128)(2,1)S(1)}, u32[]{:S(2)}, u32[]{:S(2)}) collective-permute-start(bf16[2048,256]{1,0:T(8,128)(2,1)} %refs_0_.1), channel_id=1, source_target_pairs={{0,1},{1,0},{2,3},{3,2},{4,5},{5,4},{6,7},{7,6},{8,9},{9,8},{10,11... | collective-permute-start | bytes 3145736 | tf_op jit(solution)/shard_map/ppermute | solution.py:30
  0.5 29.3 %collective-permute-start.3 = (bf16[2048,256]{1,0:T(8,128)(2,1)}, bf16[2048,256]{1,0:T(8,128)(2,1)S(1)}, u32[]{:S(2)}, u32[]{:S(2)}) collective-permute-start(bf16[2048,256]{1,0:T(8,128)(2,1)} %refs_0_.1), channel_id=1, source_target_pairs={{0,2},{1,3},{2,0},{3,1},{4,6},{5,7},{6,4},{7,5},{8,10},{9,11},{10,... | collective-permute-start | bytes 3145736 | tf_op jit(solution)/shard_map/ppermute | solution.py:30
  3.8 1.0 %copy-start.1 = (bf16[16,64,256]{2,1,0:T(8,128)(2,1)S(1)}, bf16[16,64,256]{2,1,0:T(8,128)(2,1)}, u32[]{:S(2)}) copy-start(bf16[16,64,256]{2,1,0:T(8,128)(2,1)} %param.9) | copy-start | bytes 1572868
  4.9 0.9 %copy-start.6 = (bf16[256,256]{1,0:T(8,128)(2,1)S(1)}, bf16[256,256]{1,0:T(8,128)(2,1)}, u32[]{:S(2)}) copy-start(bf16[256,256]{1,0:T(8,128)(2,1)} %weight_hbm.1) | copy-start | bytes 393220
  5.8 0.7 copy-start.7
  8.4 5.6 %copy-start = (bf16[2048,256]{1,0:T(8,128)(2,1)S(1)}, bf16[2048,256]{1,0:T(8,128)(2,1)}, u32[]{:S(2)}) copy-start(bf16[2048,256]{1,0:T(8,128)(2,1)} %refs_0_.1) | copy-start | bytes 3145732
  8.4 5.5 %copy-start.3 = (bf16[256,256]{1,0:T(8,128)(2,1)S(1)}, bf16[256,256]{1,0:T(8,128)(2,1)}, u32[]{:S(2)}) copy-start(bf16[256,256]{1,0:T(8,128)(2,1)} %key_ref.3) | copy-start | bytes 393220
  8.4 5.5 %copy-start.4 = (bf16[256,256]{1,0:T(8,128)(2,1)S(1)}, bf16[256,256]{1,0:T(8,128)(2,1)}, u32[]{:S(2)}) copy-start(bf16[256,256]{1,0:T(8,128)(2,1)} %value_ref.3) | copy-start | bytes 393220
  8.4 15.4 %collective-permute-start.1 = (bf16[4,128,256]{2,1,0:T(8,128)(2,1)S(1)}, bf16[4,128,256]{2,1,0:T(8,128)(2,1)S(1)}, u32[]{:S(2)}, u32[]{:S(2)}) collective-permute-start(bf16[4,128,256]{2,1,0:T(8,128)(2,1)S(1)} %get-tuple-element.35), channel_id=1, source_target_pairs={{0,4},{4,8},{8,12},{12,16},{16,20},{20,24},{24,28},{28,0},{1,5},{5... | collective-permute-start | bytes 786440 | tf_op jit(solution)/shard_map/ppermute | solution.py:25
  10.0 19.8 %collective-permute-start.4 = (bf16[4,128,256]{2,1,0:T(8,128)(2,1)S(1)}, bf16[4,128,256]{2,1,0:T(8,128)(2,1)S(1)}, u32[]{:S(2)}, u32[]{:S(2)}) collective-permute-start(bf16[4,128,256]{2,1,0:T(8,128)(2,1)S(1)} %get-tuple-element.48), channel_id=1, source_target_pairs={{0,28},{4,0},{8,4},{12,8},{16,12},{20,16},{24,20},{28,24},{1,29},{... | collective-permute-start | bytes 786440 | tf_op jit(solution)/shard_map/ppermute | solution.py:25
  29.8 12.9 %collective-permute-start.5 = (bf16[2048,256]{1,0:T(8,128)(2,1)S(1)}, bf16[2048,256]{1,0:T(8,128)(2,1)S(1)}, u32[]{:S(2)}, u32[]{:S(2)}) collective-permute-start(bf16[2048,256]{1,0:T(8,128)(2,1)S(1)} %collective-permute-done.3.refs_0_), channel_id=1, source_target_pairs={{0,1},{1,0},{2,3},{3,2},{4,5},{5,4},{6,7},{7,6},{8,9},{9,8},{10,11... | collective-permute-start | bytes 3145736 | tf_op jit(solution)/shard_map/ppermute | solution.py:30
  29.9 18.2 %collective-permute-start.6 = (bf16[4,128,256]{2,1,0:T(8,128)(2,1)S(1)}, bf16[4,128,256]{2,1,0:T(8,128)(2,1)S(1)}, u32[]{:S(2)}, u32[]{:S(2)}) collective-permute-start(bf16[4,128,256]{2,1,0:T(8,128)(2,1)S(1)} %get-tuple-element.53), channel_id=1, source_target_pairs={{0,4},{4,8},{8,12},{12,16},{16,20},{20,24},{24,28},{28,0},{1,5},{5... | collective-permute-start | bytes 786440 | tf_op jit(solution)/shard_map/ppermute | solution.py:25
  30.2 24.0 %collective-permute-start.2 = (bf16[4,128,256]{2,1,0:T(8,128)(2,1)S(1)}, bf16[4,128,256]{2,1,0:T(8,128)(2,1)S(1)}, u32[]{:S(2)}, u32[]{:S(2)}) collective-permute-start(bf16[4,128,256]{2,1,0:T(8,128)(2,1)S(1)} %get-tuple-element.47), channel_id=1, source_target_pairs={{0,28},{4,0},{8,4},{12,8},{16,12},{20,16},{24,20},{28,24},{1,29},{... | collective-permute-start | bytes 786440 | tf_op jit(solution)/shard_map/ppermute | solution.py:25
  40.7 31.4 %collective-permute-start.7 = (bf16[4,128,256]{2,1,0:T(8,128)(2,1)S(1)}, bf16[4,128,256]{2,1,0:T(8,128)(2,1)S(1)}, u32[]{:S(2)}, u32[]{:S(2)}) collective-permute-start(bf16[4,128,256]{2,1,0:T(8,128)(2,1)S(1)} %shard_map.92), channel_id=1, source_target_pairs={{0,28},{4,0},{8,4},{12,8},{16,12},{20,16},{24,20},{28,24},{1,29},{... | collective-permute-start | bytes 786440 | tf_op jit(solution)/shard_map/ppermute | solution.py:25
  41.3 30.8 %collective-permute-start.8 = (bf16[4,128,256]{2,1,0:T(8,128)(2,1)S(1)}, bf16[4,128,256]{2,1,0:T(8,128)(2,1)S(1)}, u32[]{:S(2)}, u32[]{:S(2)}) collective-permute-start(bf16[4,128,256]{2,1,0:T(8,128)(2,1)S(1)} %shard_map.93), channel_id=1, source_target_pairs={{0,4},{4,8},{8,12},{12,16},{16,20},{20,24},{24,28},{28,0},{1,5},{5... | collective-permute-start | bytes 786440 | tf_op jit(solution)/shard_map/ppermute | solution.py:25
  60.2 13.2 %collective-permute-start.10 = (bf16[4,128,256]{2,1,0:T(8,128)(2,1)S(1)}, bf16[4,128,256]{2,1,0:T(8,128)(2,1)S(1)}, u32[]{:S(2)}, u32[]{:S(2)}) collective-permute-start(bf16[4,128,256]{2,1,0:T(8,128)(2,1)S(1)} %shard_map.95), channel_id=1, source_target_pairs={{0,4},{4,8},{8,12},{12,16},{16,20},{20,24},{24,28},{28,0},{1,5},{5... | collective-permute-start | bytes 786440 | tf_op jit(solution)/shard_map/ppermute | solution.py:25
  62.7 12.8 %collective-permute-start.9 = (bf16[4,128,256]{2,1,0:T(8,128)(2,1)S(1)}, bf16[4,128,256]{2,1,0:T(8,128)(2,1)S(1)}, u32[]{:S(2)}, u32[]{:S(2)}) collective-permute-start(bf16[4,128,256]{2,1,0:T(8,128)(2,1)S(1)} %shard_map.94), channel_id=1, source_target_pairs={{0,28},{4,0},{8,4},{12,8},{16,12},{20,16},{24,20},{28,24},{1,29},{... | collective-permute-start | bytes 786440 | tf_op jit(solution)/shard_map/ppermute | solution.py:25
  72.0 3.4 %copy-start.2 = (bf16[16,64,256]{2,1,0:T(8,128)(2,1)S(1)}, bf16[16,64,256]{2,1,0:T(8,128)(2,1)}, u32[]{:S(2)}) copy-start(bf16[16,64,256]{2,1,0:T(8,128)(2,1)} %param.9) | copy-start | bytes 1572868
  72.0 3.4 %copy-start.5 = (bf16[256,256]{1,0:T(8,128)(2,1)S(1)}, bf16[256,256]{1,0:T(8,128)(2,1)}, u32[]{:S(2)}) copy-start(bf16[256,256]{1,0:T(8,128)(2,1)} %weight_ref.1) | copy-start | bytes 393220

commit v2 on v1

--- a/solution.py
+++ b/solution.py
@@ -30,8 +30,7 @@
     return lax.ppermute(block, axis, [(i, i ^ bit) for i in range(count)])
 
 
-def fill_slots(codes_ref, rows, out_refs, group):
-    blocks = out_refs[0].shape[0]
+def fill_slots(codes_ref, rows, out_ref, group):
     queries = rows.shape[0]
     codes = codes_ref[...]
     slot = lax.broadcasted_iota(jnp.int32, (2 * CAP, queries), 0).astype(jnp.int16)
@@ -42,12 +41,11 @@
         for entry in range(1, codes.shape[0]):
             hit = hit | (slot == near[entry:entry + 1, :])
         got = jnp.dot(jnp.where(hit, one, zero), rows, preferred_element_type=jnp.float32).astype(jnp.bfloat16)
-        at = step % blocks
-        out_refs[step // blocks][at:at + 2] = got.reshape(2, CAP, got.shape[1])
+        out_ref[step:step + 2] = got.reshape(2, CAP, got.shape[1])
 
 
 def project_kernel(codes_ref, queries_hbm, gain_hbm, weight_hbm, rows_ref, *refs):
-    slot_refs, (queries_ref, gain_ref, weight_ref, sems) = refs[:-4], refs[-4:]
+    slots_ref, queries_ref, gain_ref, weight_ref, sems = refs
     copies = [
         pltpu.make_async_copy(source, target, sems.at[i])
         for i, (source, target) in enumerate(((queries_hbm, queries_ref), (gain_hbm, gain_ref), (weight_hbm, weight_ref)))
@@ -63,16 +61,14 @@
     normed = (centred * lax.rsqrt(spread + 1e-05) * gain_ref[...]).astype(jnp.bfloat16)
     rows = jnp.dot(normed, weight_ref[...], preferred_element_type=jnp.float32).astype(jnp.bfloat16)
     rows_ref[...] = rows
-    parts = len(slot_refs) // 2
-    fill_slots(codes_ref, rows, slot_refs[:parts], 2)
-    fill_slots(codes_ref, rows, slot_refs[parts:], 0)
-
-
-def slot_shapes(parts, width):
-    return (jax.ShapeDtypeStruct((BLK_DEV // parts, CAP, width), jnp.bfloat16),) * parts
-
-
-def project(codes, queries, gain, weight, parts):
+    fill_slots(codes_ref, rows, slots_ref, 2)
+
+
+def slot_shape(width):
+    return jax.ShapeDtypeStruct((BLK_DEV, CAP, width), jnp.bfloat16)
+
+
+def project(codes, queries, gain, weight):
     count, width = queries.shape
     hbm = pl.BlockSpec(memory_space=pltpu.HBM)
     return pl.pallas_call(
@@ -84,21 +80,23 @@
             pltpu.VMEM(weight.shape, weight.dtype),
             pltpu.SemaphoreType.DMA((3,)),
         ],
-        out_shape=(jax.ShapeDtypeStruct((count, width), jnp.bfloat16),) + 2 * slot_shapes(parts, width),
+        out_shape=(jax.ShapeDtypeStruct((count, width), jnp.bfloat16), slot_shape(width)),
         compiler_params=params(),
         cost_estimate=pl.CostEstimate(flops=4 << 30, bytes_accessed=2 << 20, transcendentals=0),
         name="project",
     )(codes, queries, gain, weight)
 
 
-def scatter_kernel(codes_ref, rows_ref, *slot_refs):
-    fill_slots(codes_ref, rows_ref[...], slot_refs, 1)
-
-
-def scatter(codes, rows, parts):
+def scatter_kernel(codes_ref, rows_ref, prev_ref, own_ref):
+    rows = rows_ref[...]
+    fill_slots(codes_ref, rows, prev_ref, 0)
+    fill_slots(codes_ref, rows, own_ref, 1)
+
+
+def scatter(codes, rows):
     return pl.pallas_call(
         scatter_kernel,
-        out_shape=slot_shapes(parts, rows.shape[1]),
+        out_shape=(slot_shape(rows.shape[1]),) * 2,
         compiler_params=params(),
         cost_estimate=pl.CostEstimate(flops=1 << 30, bytes_accessed=2 << 20, transcendentals=0),
         name="scatter",
@@ -130,8 +128,12 @@
     )(w_key, w_value, *features)
 
 
-def attend_kernel(rows_ref, kv_ref, out_ref, scores_ref, *, stack):
-    blocks, count, width = rows_ref.shape
+def attend_kernel(rows_ref, kv_ref, *refs, stack, start):
+    out_ref, scores_ref = refs[-2:]
+    blocks, (_, count, width) = kv_ref.shape[0], rows_ref.shape
+    if len(refs) > 2:
+        out_ref[:start] = refs[0][...]
+    base = out_ref.shape[0] - blocks
     head_size = width // HEADS
     factor = head_size ** (-0.5) * LOG2_E
     head_of = lax.broadcasted_iota(jnp.int32, (1, width), 1) // head_size
@@ -140,7 +142,7 @@
 
     def scores_of(b, first):
         side = slice(half * (first >= HEADS // 2), half * (first >= HEADS // 2) + half)
-        rows = rows_ref[b, :, side]
+        rows = rows_ref[start + b, :, side]
         kept = [jnp.where(head_of[:, side] == first + i, rows, jnp.zeros_like(rows)) for i in range(stack)]
         return lax.dot_general(
             jnp.concatenate(kept, axis=0), kv_ref[b, :, side],
@@ -167,24 +169,26 @@
                     part = got[i * count:(i + 1) * count]
                     merged = part if first + i == 0 else jnp.where(head_of == first + i, part, merged)
                 scores = following
-            out_ref[b] = merged.astype(jnp.bfloat16)
+            out_ref[base + b] = merged.astype(jnp.bfloat16)
         scores_ref[...] = scores
 
 
-def attend(rows, kv):
-    blocks, count, width = rows.shape
-    keys = kv.shape[1]
+def attend(rows, kv, start, before=None):
+    _, count, width = rows.shape
+    blocks, keys = kv.shape[:2]
     stack = 2
     pairs = blocks * count * keys
-    return pl.pallas_call(
-        functools.partial(attend_kernel, stack=stack),
-        out_shape=jax.ShapeDtypeStruct(rows.shape, jnp.bfloat16),
+    done = 0 if before is None else start
+    return pl.pallas_call(
+        functools.partial(attend_kernel, stack=stack, start=start),
+        out_shape=jax.ShapeDtypeStruct((done + blocks, count, width), jnp.bfloat16),
         scratch_shapes=[pltpu.VMEM((stack * count, keys), jnp.float32)],
         compiler_params=params(),
         cost_estimate=pl.CostEstimate(
             flops=4 * pairs * width * HEADS, bytes_accessed=blocks * keys * width * 4,
             transcendentals=pairs * HEADS),
-    )(rows, kv)
+        name="attend",
+    )(rows, kv, *([] if before is None else [before]))
 
 
 def pick_kernel(codes_ref, *out_refs, groups):
@@ -286,47 +290,40 @@
             whole_sector = jnp.concatenate([whole_sector, swapped(whole_sector, "band", bit)], axis=0)
             bit *= 2
         held = [[whole_sector]]
-    parts = 2 if staged else 1
-    blocks = BLK_DEV // parts
-
-    projected, *slots = project(codes, rows_in, norm_gain.reshape(1, width), w_query, parts)
-    lower, upper = [], []
-    for part in range(parts):
-        lower.append(shifted(slots[part], "sector", 1))
-        upper.append(shifted(slots[parts + part], "sector", -1))
-    projected, *_ = lax.optimization_barrier((projected, *slots))
-    own = list(scatter(codes, projected, parts))
+    selected = picks(codes, (0, 1, 2))
+    codes, *selected = lax.optimization_barrier((codes, *selected))
+    projected, slots_next = project(codes, rows_in, norm_gain.reshape(1, width), w_query)
+    lower = shifted(slots_next, "sector", 1)
+    projected, _ = lax.optimization_barrier((projected, slots_next))
+    slots_prev, slots_own = scatter(codes, projected)
     kv = keys_and_values(held[0], w_key, w_value, keys)
-    own[0] = attend(own[0], kv)
-    codes, own[0] = lax.optimization_barrier((codes, own[0]))
-    selected = picks(codes, (0, 1, 2))
-
-    def visit(part, kv, before):
-        kv, first, before = lax.optimization_barrier((kv, lower[part], before))
-        second = upper[part]
-        first = attend(first, kv)
-        second, first = lax.optimization_barrier((second, first))
-        middle = first
-        second = attend(second, kv)
-        first, second = lax.optimization_barrier((first, second))
-        return (shifted(first, "sector", -1), shifted(second, "sector", 1)), before, middle, second
-
-    sent, selected, middle, last = visit(0, kv, selected)
-    back = [sent]
+    half = kv.shape[0]
+    own = [attend(slots_own, kv, 0)]
+    slots_prev, own[0] = lax.optimization_barrier((slots_prev, own[0]))
+    upper = shifted(slots_prev, "sector", -1)
+    kv, lower, own[0] = lax.optimization_barrier((kv, lower, own[0]))
+    from_lower = attend(lower, kv, 0)
+    kvs = [kv]
     if staged:
-        across, middle = lax.optimization_barrier((across, middle))
-        kv = keys_and_values([across, swapped(across, "band", 1)], w_key, w_value, keys)
-        sent, _, _, last = visit(1, kv, last)
-        back.append(sent)
-        own[1], _ = lax.optimization_barrier((own[1], last))
-        own[1] = attend(own[1], kv)
-
-    slots_of = blocks * CAP
-    early = [((1, i * slots_of), rows) for i, rows in enumerate(own)]
-    early += [((2 - 2 * side, 0), back[0][side]) for side in range(2)] if staged else []
-    late = [((2 - 2 * side, (parts - 1) * slots_of), back[-1][side]) for side in range(2)]
+        across, from_lower = lax.optimization_barrier((across, from_lower))
+        kvs.append(keys_and_values([across, swapped(across, "band", 1)], w_key, w_value, keys))
+        from_lower = attend(lower, kvs[1], half, from_lower)
+    back_lower = shifted(from_lower, "sector", -1)
+    back_upper = []
+    last = from_lower
+    for part, kv in enumerate(kvs):
+        turn, last = lax.optimization_barrier((upper, last))
+        last = attend(turn, kv, part * half)
+        back_upper.append(shifted(last, "sector", 1))
+    if staged:
+        turn, last = lax.optimization_barrier((slots_own, last))
+        own.append(attend(turn, kvs[1], half))
+
+    cuts = [i * half * CAP for i in range(len(kvs))]
+    early = [((1, at), rows) for at, rows in zip(cuts, own)] + [((2, 0), back_lower)]
+    early += [((0, at), rows) for at, rows in zip(cuts[:-1], back_upper)]
     partial = partial_sum(selected, [rows for _, rows in early], tuple(at for at, _ in early))
-    out = finish(partial, rows_in, w_out, selected, [rows for _, rows in late], tuple(at for at, _ in late))
+    out = finish(partial, rows_in, w_out, selected, back_upper[-1:], ((0, cuts[-1]),))
     return out.reshape(azim_cells, range_cells, width)
 
 

time: 78.2 us -> 77 us (0.985)
  waiting for transfers between devices: 6.23 us -> 18.7 us
  starting transfers between devices: 20.6 us -> 9.93 us
  local copies, waits for them, and re-layouts: 2.74 us -> 0.12 us
    ppermute x8 -> x5, waiting for transfers between devices: 6.22 us -> 18 us  [shifted(): lax.ppermute(block, axis, [(i, (i + distance) % count) for i in range(cou...]
    ppermute x8 -> x5, starting transfers between devices: 17.5 us -> 6.72 us  [shifted(): lax.ppermute(block, axis, [(i, (i + distance) % count) for i in range(cou...]
    unnamed x16 -> x14, local copies, waits for them, and re-layouts: 2.66 us -> 0.04 us
  transfers between devices with their start and end apart: 11 -> 8, of which waited for: 2 -> 4; matrix products, arithmetic and copies ran while one was open for 1% -> 1% of each run, Pallas kernels for 58% -> 59%
where the time goes in v2:
time: 77 us; the launch traced here: 76.8 us
  Pallas kernels  47.1 us (61%)
  waiting for transfers between devices  18.7 us (24%)
  starting transfers between devices  9.93 us (13%)
    pallas_call x6, Pallas kernels, attend(): pl.pallas_call(functools.partial(attend_kernel, stack=stack, start=start)...  36 us
    ppermute x5, waiting for transfers between devices, shifted(): lax.ppermute(block, axis, [(i, (i + distance) % count) for i in range(cou...  18 us
    ppermute x5, starting transfers between devices, shifted(): lax.ppermute(block, axis, [(i, (i + distance) % count) for i in range(cou...  6.72 us
    ppermute x3, starting transfers between devices, swapped(): return lax.ppermute(block, axis, [(i, i ^ bit) for i in range(count)])  3.21 us
    pallas_call x2, Pallas kernels, keys_and_values(): pl.pallas_call(kv_kernel, out_shape=jax.ShapeDtypeStruct((count // keys,...  2.51 us
    pallas_call x1, Pallas kernels, picks(): pl.pallas_call(functools.partial(pick_kernel, groups=groups), out_shape=(...  2.5 us
    pallas_call x1, Pallas kernels, finish(): pl.pallas_call(functools.partial(final_kernel, places=places), out_shape=...  1.98 us
  transfers between devices with their start and end apart: 8, of which 4 were waited for; matrix products, arithmetic and copies ran while one was open for 1% of the time, Pallas kernels for 59%

profile of v2, /device:TPU:0, one launch (start us, length us, event | category | flops | bytes accessed | tf_op | source)
XLA Modules:
  0.0 76.8 jit_solution(12137020591601465364)
XLA Ops:
  0.0 0.6 collective-permute-start
  0.6 2.6 %collective-permute-start.3 = (bf16[2048,256]{1,0:T(8,128)(2,1)}, bf16[2048,256]{1,0:T(8,128)(2,1)S(1)}, u32[]{:S(2)}, u32[]{:S(2)}) collective-permute-start(bf16[2048,256]{1,0:T(8,128)(2,1)} %refs_0_.1), channel_id=1, source_target_pairs={{0,2},{1,3},{2,0},{3,1},{4,6},{5,7},{6,4},{7,5},{8,10},{9,11},{10,... | collective-permute-start | bytes 3145736 | tf_op jit(solution)/shard_map/ppermute | solution.py:30
  3.2 0.8 select_bitcast_fusion
  3.9 0.1 reshape.12.codes_ref
  4.0 2.5 %picks.1 = (bf16[1024,1024]{1,0:T(8,128)(2,1)S(1)}, bf16[1024,1024]{1,0:T(8,128)(2,1)S(1)}, bf16[1024,1024]{1,0:T(8,128)(2,1)S(1)}) custom-call(s32[3,1024]{1,0:T(4,128)S(1)} %reshape.12.codes_ref), custom_call_target="tpu_custom_call" | custom-call | flops 1073741824 | bytes 2097152 | tf_op jit(solution)/shard_map/picks/pallas_call | solution.py:212
  6.5 1.4 %project.1 = (bf16[1024,256]{1,0:T(8,128)(2,1)S(1)}, bf16[8,128,256]{2,1,0:T(8,128)(2,1)S(1)}) custom-call(s32[3,1024]{1,0:T(4,128)S(1)} %reshape.12.codes_ref, bf16[1024,256]{1,0:T(8,128)(2,1)S(1)} %bitcast.5, f32[1,256]{1,0:T(1,128)S(1)} %bitcast.7, bf16[256,256]{1,0:T(8,128)(2,1)S(1)} %copy-done.5), custom_call_target="tpu_custom_call" | custom-call | flops 4294967296 | bytes 2097152 | tf_op jit(solution)/shard_map/project/pallas_call | solution.py:74
  7.9 0.0 copy-start
  7.9 0.0 copy-start.2
  7.9 0.0 copy-start.3
  7.9 1.7 %collective-permute-start.1 = (bf16[8,128,256]{2,1,0:T(8,128)(2,1)S(1)}, bf16[8,128,256]{2,1,0:T(8,128)(2,1)S(1)}, u32[]{:S(2)}, u32[]{:S(2)}) collective-permute-start(bf16[8,128,256]{2,1,0:T(8,128)(2,1)S(1)} %get-tuple-element.34), channel_id=1, source_target_pairs={{0,4},{4,8},{8,12},{12,16},{16,20},{20,24},{24,28},{28,0},{1,5},{5... | collective-permute-start | bytes 1572872 | tf_op jit(solution)/shard_map/ppermute | solution.py:25
  9.7 1.3 %scatter.1 = (bf16[8,128,256]{2,1,0:T(8,128)(2,1)S(1)}, bf16[8,128,256]{2,1,0:T(8,128)(2,1)S(1)}) custom-call(s32[3,1024]{1,0:T(4,128)S(1)} %reshape.12.codes_ref, bf16[1024,256]{1,0:T(8,128)(2,1)S(1)} %get-tuple-element.35.rows_ref), custom_call_target="tpu_custom_call" | custom-call | flops 1073741824 | bytes 2097152 | tf_op jit(solution)/shard_map/scatter/pallas_call | solution.py:97
  10.9 0.0 collective-permute-done.refs_1_
  11.0 1.3 %keys_and_values.2.kv_ref = bf16[4,1024,512]{2,1,0:T(8,128)(2,1)S(1)} custom-call(bf16[256,256]{1,0:T(8,128)(2,1)S(1)} %copy-done.2, bf16[256,256]{1,0:T(8,128)(2,1)S(1)} %copy-done.3, bf16[2048,256]{1,0:T(8,128)(2,1)S(1)} %copy-done, bf16[2048,256]{1,0:T(8,128)(2,1)S(1)} %collective-permute-done.refs_1_), custom_call_target="tpu_custom_call" | custom-call | flops 1073741824 | bytes 6291456 | tf_op jit(solution)/shard_map/keys_and_values/pallas_call | solution.py:122
  12.2 6.0 %attend.6.refs_3_ = bf16[4,128,256]{2,1,0:T(8,128)(2,1)S(1)} custom-call(bf16[8,128,256]{2,1,0:T(8,128)(2,1)S(1)} %get-tuple-element.47.rows_ref, bf16[4,1024,512]{2,1,0:T(8,128)(2,1)S(1)} %keys_and_values.2.kv_ref), custom_call_target="tpu_custom_call" | custom-call | flops 4294967296 | bytes 4194304 | tf_op jit(solution)/shard_map/attend/pallas_call | solution.py:182
  18.2 6.7 %collective-permute-done.1.rows_ref = bf16[8,128,256]{2,1,0:T(8,128)(2,1)S(1)} collective-permute-done((bf16[8,128,256]{2,1,0:T(8,128)(2,1)S(1)}, bf16[8,128,256]{2,1,0:T(8,128)(2,1)S(1)}, u32[]{:S(2)}, u32[]{:S(2)}) %collective-permute-start.1) | collective-permute-done | bytes 524320 | tf_op jit(solution)/shard_map/ppermute | solution.py:25
  24.9 6.0 %attend.7.refs_0_ = bf16[4,128,256]{2,1,0:T(8,128)(2,1)S(1)} custom-call(bf16[8,128,256]{2,1,0:T(8,128)(2,1)S(1)} %collective-permute-done.1.rows_ref, bf16[4,1024,512]{2,1,0:T(8,128)(2,1)S(1)} %keys_and_values.2.kv_ref), custom_call_target="tpu_custom_call" | custom-call | flops 4294967296 | bytes 4194304 | tf_op jit(solution)/shard_map/attend/pallas_call | solution.py:182
  30.9 0.1 collective-permute-start.4
  31.0 2.0 %collective-permute-start.2 = (bf16[8,128,256]{2,1,0:T(8,128)(2,1)S(1)}, bf16[8,128,256]{2,1,0:T(8,128)(2,1)S(1)}, u32[]{:S(2)}, u32[]{:S(2)}) collective-permute-start(bf16[8,128,256]{2,1,0:T(8,128)(2,1)S(1)} %get-tuple-element.40), channel_id=1, source_target_pairs={{0,28},{4,0},{8,4},{12,8},{16,12},{20,16},{24,20},{28,24},{1,29},{... | collective-permute-start | bytes 1572872 | tf_op jit(solution)/shard_map/ppermute | solution.py:25
  33.0 0.6 collective-permute-done.4.refs_1_
  33.7 1.3 %keys_and_values.3.kv_ref = bf16[4,1024,512]{2,1,0:T(8,128)(2,1)S(1)} custom-call(bf16[256,256]{1,0:T(8,128)(2,1)S(1)} %copy-done.2, bf16[256,256]{1,0:T(8,128)(2,1)S(1)} %copy-done.3, bf16[2048,256]{1,0:T(8,128)(2,1)S(1)} %collective-permute-done.3.refs_0_, bf16[2048,256]{1,0:T(8,128)(2,1)S(1)} %collective-permute-done.4.refs_1_), custom_call_target="tpu_custom_call" | custom-call | flops 1073741824 | bytes 6291456 | tf_op jit(solution)/shard_map/keys_and_values/pallas_call | solution.py:122
  34.9 6.0 %attend.8 = bf16[8,128,256]{2,1,0:T(8,128)(2,1)S(1)} custom-call(bf16[8,128,256]{2,1,0:T(8,128)(2,1)S(1)} %collective-permute-done.1.rows_ref, bf16[4,1024,512]{2,1,0:T(8,128)(2,1)S(1)} %keys_and_values.3.kv_ref, bf16[4,128,256]{2,1,0:T(8,128)(2,1)S(1)} %attend.7.refs_0_), custom_call_target="tpu_custom_call" | custom-call | flops 4294967296 | bytes 4194304 | tf_op jit(solution)/shard_map/attend/pallas_call | solution.py:182
  40.9 1.8 %collective-permute-start.5 = (bf16[8,128,256]{2,1,0:T(8,128)(2,1)S(1)}, bf16[8,128,256]{2,1,0:T(8,128)(2,1)S(1)}, u32[]{:S(2)}, u32[]{:S(2)}) collective-permute-start(bf16[8,128,256]{2,1,0:T(8,128)(2,1)S(1)} %attend.8), channel_id=1, source_target_pairs={{0,28},{4,0},{8,4},{12,8},{16,12},{20,16},{24,20},{28,24},{1,29},{... | collective-permute-start | bytes 1572872 | tf_op jit(solution)/shard_map/ppermute | solution.py:25
  42.7 3.3 %collective-permute-done.2.rows_ref = bf16[8,128,256]{2,1,0:T(8,128)(2,1)S(1)} collective-permute-done((bf16[8,128,256]{2,1,0:T(8,128)(2,1)S(1)}, bf16[8,128,256]{2,1,0:T(8,128)(2,1)S(1)}, u32[]{:S(2)}, u32[]{:S(2)}) %collective-permute-start.2) | collective-permute-done | bytes 524320 | tf_op jit(solution)/shard_map/ppermute | solution.py:25
  46.1 6.0 %attend.9 = bf16[4,128,256]{2,1,0:T(8,128)(2,1)S(1)} custom-call(bf16[8,128,256]{2,1,0:T(8,128)(2,1)S(1)} %collective-permute-done.2.rows_ref, bf16[4,1024,512]{2,1,0:T(8,128)(2,1)S(1)} %keys_and_values.2.kv_ref), custom_call_target="tpu_custom_call" | custom-call | flops 4294967296 | bytes 4194304 | tf_op jit(solution)/shard_map/attend/pallas_call | solution.py:182
  52.1 6.0 %attend.10 = bf16[4,128,256]{2,1,0:T(8,128)(2,1)S(1)} custom-call(bf16[8,128,256]{2,1,0:T(8,128)(2,1)S(1)} %collective-permute-done.2.rows_ref, bf16[4,1024,512]{2,1,0:T(8,128)(2,1)S(1)} %keys_and_values.3.kv_ref), custom_call_target="tpu_custom_call" | custom-call | flops 4294967296 | bytes 4194304 | tf_op jit(solution)/shard_map/attend/pallas_call | solution.py:182
  58.1 0.1 collective-permute-start.7
  58.2 1.1 %collective-permute-start.6 = (bf16[4,128,256]{2,1,0:T(8,128)(2,1)S(1)}, bf16[4,128,256]{2,1,0:T(8,128)(2,1)S(1)}, u32[]{:S(2)}, u32[]{:S(2)}) collective-permute-start(bf16[4,128,256]{2,1,0:T(8,128)(2,1)S(1)} %attend.9), channel_id=1, source_target_pairs={{0,4},{4,8},{8,12},{12,16},{16,20},{20,24},{24,28},{28,0},{1,5},{5... | collective-permute-start | bytes 786440 | tf_op jit(solution)/shard_map/ppermute | solution.py:25
  59.3 6.0 %attend.11.refs_4_ = bf16[4,128,256]{2,1,0:T(8,128)(2,1)S(1)} custom-call(bf16[8,128,256]{2,1,0:T(8,128)(2,1)S(1)} %get-tuple-element.47.rows_ref, bf16[4,1024,512]{2,1,0:T(8,128)(2,1)S(1)} %keys_and_values.3.kv_ref), custom_call_target="tpu_custom_call" | custom-call | flops 4294967296 | bytes 4194304 | tf_op jit(solution)/shard_map/attend/pallas_call | solution.py:182
  65.3 0.0 copy-start.4
  65.3 8.0 %collective-permute-done.6.refs_6_ = bf16[4,128,256]{2,1,0:T(8,128)(2,1)S(1)} collective-permute-done((bf16[4,128,256]{2,1,0:T(8,128)(2,1)S(1)}, bf16[4,128,256]{2,1,0:T(8,128)(2,1)S(1)}, u32[]{:S(2)}, u32[]{:S(2)}) %collective-permute-start.6) | collective-permute-done | bytes 262176 | tf_op jit(solution)/shard_map/ppermute | solution.py:25
  73.3 1.5 %partial_sum.1.partial_ref = f32[1024,256]{1,0:T(8,128)S(1)} custom-call(bf16[1024,1024]{1,0:T(8,128)(2,1)S(1)} %get-tuple-element.30.refs_0_, bf16[1024,1024]{1,0:T(8,128)(2,1)S(1)} %get-tuple-element.31.refs_1_, bf16[1024,1024]{1,0:T(8,128)(2,1)S(1)} %get-tuple-element.32.refs_2_, bf16[4,128,256]{2,1,0:T(8,128)(2,1)S(1)} %attend.6.refs_3_, ...), custom_call_target="tpu_custom_call" | custom-call | flops 1073741824 | bytes 2097152 | tf_op jit(solution)/shard_map/partial_sum/pallas_call | solution.py:241
  74.8 2.0 %finish.1 = bf16[1024,256]{1,0:T(8,128)(2,1)} custom-call(f32[1024,256]{1,0:T(8,128)S(1)} %partial_sum.1.partial_ref, bf16[1024,256]{1,0:T(8,128)(2,1)S(1)} %bitcast.6, bf16[256,256]{1,0:T(8,128)(2,1)S(1)} %copy-done.4, bf16[1024,1024]{1,0:T(8,128)(2,1)S(1)} %get-tuple-element.30.refs_0_, bf16[1024,1024]{1,0:T(8,128)(2,1)S(1)} %get-tuple-element.31.refs_1_, ...), custom_call_target="tpu_custom_call" | custom-call | flops 1073741824 | bytes 2097152 | tf_op jit(solution)/shard_map/finish/pallas_call | solution.py:261
  (13 shorter events, 0.0 us)
Async XLA Ops:
  0.0 6.5 %copy-start.5 = (bf16[256,256]{1,0:T(8,128)(2,1)S(1)}, bf16[256,256]{1,0:T(8,128)(2,1)}, u32[]{:S(2)}) copy-start(bf16[256,256]{1,0:T(8,128)(2,1)} %weight_hbm.1) | copy-start | bytes 393220
  0.0 6.5 %copy-start.6 = (f32[256]{0:T(256)S(1)}, f32[256]{0:T(256)}, u32[]{:S(2)}) copy-start(f32[256]{0:T(256)} %param.10) | copy-start | bytes 3076
  0.0 6.5 %copy-start.1 = (bf16[16,64,256]{2,1,0:T(8,128)(2,1)S(1)}, bf16[16,64,256]{2,1,0:T(8,128)(2,1)}, u32[]{:S(2)}) copy-start(bf16[16,64,256]{2,1,0:T(8,128)(2,1)} %param.9) | copy-start | bytes 1572868
  0.0 10.9 %collective-permute-start = (bf16[2048,256]{1,0:T(8,128)(2,1)}, bf16[2048,256]{1,0:T(8,128)(2,1)S(1)}, u32[]{:S(2)}, u32[]{:S(2)}) collective-permute-start(bf16[2048,256]{1,0:T(8,128)(2,1)} %refs_0_.1), channel_id=1, source_target_pairs={{0,1},{1,0},{2,3},{3,2},{4,5},{5,4},{6,7},{7,6},{8,9},{9,8},{10,11... | collective-permute-start | bytes 3145736 | tf_op jit(solution)/shard_map/ppermute | solution.py:30
  0.6 30.4 %collective-permute-start.3 = (bf16[2048,256]{1,0:T(8,128)(2,1)}, bf16[2048,256]{1,0:T(8,128)(2,1)S(1)}, u32[]{:S(2)}, u32[]{:S(2)}) collective-permute-start(bf16[2048,256]{1,0:T(8,128)(2,1)} %refs_0_.1), channel_id=1, source_target_pairs={{0,2},{1,3},{2,0},{3,1},{4,6},{5,7},{6,4},{7,5},{8,10},{9,11},{10,... | collective-permute-start | bytes 3145736 | tf_op jit(solution)/shard_map/ppermute | solution.py:30
  7.9 3.0 %copy-start = (bf16[2048,256]{1,0:T(8,128)(2,1)S(1)}, bf16[2048,256]{1,0:T(8,128)(2,1)}, u32[]{:S(2)}) copy-start(bf16[2048,256]{1,0:T(8,128)(2,1)} %refs_0_.1) | copy-start | bytes 3145732
  7.9 3.0 %copy-start.2 = (bf16[256,256]{1,0:T(8,128)(2,1)S(1)}, bf16[256,256]{1,0:T(8,128)(2,1)}, u32[]{:S(2)}) copy-start(bf16[256,256]{1,0:T(8,128)(2,1)} %key_ref.3) | copy-start | bytes 393220
  7.9 3.0 %copy-start.3 = (bf16[256,256]{1,0:T(8,128)(2,1)S(1)}, bf16[256,256]{1,0:T(8,128)(2,1)}, u32[]{:S(2)}) copy-start(bf16[256,256]{1,0:T(8,128)(2,1)} %value_ref.3) | copy-start | bytes 393220
  7.9 17.0 %collective-permute-start.1 = (bf16[8,128,256]{2,1,0:T(8,128)(2,1)S(1)}, bf16[8,128,256]{2,1,0:T(8,128)(2,1)S(1)}, u32[]{:S(2)}, u32[]{:S(2)}) collective-permute-start(bf16[8,128,256]{2,1,0:T(8,128)(2,1)S(1)} %get-tuple-element.34), channel_id=1, source_target_pairs={{0,4},{4,8},{8,12},{12,16},{16,20},{20,24},{24,28},{28,0},{1,5},{5... | collective-permute-start | bytes 1572872 | tf_op jit(solution)/shard_map/ppermute | solution.py:25
  30.9 2.7 %collective-permute-start.4 = (bf16[2048,256]{1,0:T(8,128)(2,1)S(1)}, bf16[2048,256]{1,0:T(8,128)(2,1)S(1)}, u32[]{:S(2)}, u32[]{:S(2)}) collective-permute-start(bf16[2048,256]{1,0:T(8,128)(2,1)S(1)} %collective-permute-done.3.refs_0_), channel_id=1, source_target_pairs={{0,1},{1,0},{2,3},{3,2},{4,5},{5,4},{6,7},{7,6},{8,9},{9,8},{10,11... | collective-permute-start | bytes 3145736 | tf_op jit(solution)/shard_map/ppermute | solution.py:30
  31.0 15.1 %collective-permute-start.2 = (bf16[8,128,256]{2,1,0:T(8,128)(2,1)S(1)}, bf16[8,128,256]{2,1,0:T(8,128)(2,1)S(1)}, u32[]{:S(2)}, u32[]{:S(2)}) collective-permute-start(bf16[8,128,256]{2,1,0:T(8,128)(2,1)S(1)} %get-tuple-element.40), channel_id=1, source_target_pairs={{0,28},{4,0},{8,4},{12,8},{16,12},{20,16},{24,20},{28,24},{1,29},{... | collective-permute-start | bytes 1572872 | tf_op jit(solution)/shard_map/ppermute | solution.py:25
  40.9 32.4 %collective-permute-start.5 = (bf16[8,128,256]{2,1,0:T(8,128)(2,1)S(1)}, bf16[8,128,256]{2,1,0:T(8,128)(2,1)S(1)}, u32[]{:S(2)}, u32[]{:S(2)}) collective-permute-start(bf16[8,128,256]{2,1,0:T(8,128)(2,1)S(1)} %attend.8), channel_id=1, source_target_pairs={{0,28},{4,0},{8,4},{12,8},{16,12},{20,16},{24,20},{28,24},{1,29},{... | collective-permute-start | bytes 1572872 | tf_op jit(solution)/shard_map/ppermute | solution.py:25
  58.1 16.7 %collective-permute-start.7 = (bf16[4,128,256]{2,1,0:T(8,128)(2,1)S(1)}, bf16[4,128,256]{2,1,0:T(8,128)(2,1)S(1)}, u32[]{:S(2)}, u32[]{:S(2)}) collective-permute-start(bf16[4,128,256]{2,1,0:T(8,128)(2,1)S(1)} %attend.10), channel_id=1, source_target_pairs={{0,4},{4,8},{8,12},{12,16},{16,20},{20,24},{24,28},{28,0},{1,5},{5... | collective-permute-start | bytes 786440 | tf_op jit(solution)/shard_map/ppermute | solution.py:25
  58.2 15.1 %collective-permute-start.6 = (bf16[4,128,256]{2,1,0:T(8,128)(2,1)S(1)}, bf16[4,128,256]{2,1,0:T(8,128)(2,1)S(1)}, u32[]{:S(2)}, u32[]{:S(2)}) collective-permute-start(bf16[4,128,256]{2,1,0:T(8,128)(2,1)S(1)} %attend.9), channel_id=1, source_target_pairs={{0,4},{4,8},{8,12},{12,16},{16,20},{20,24},{24,28},{28,0},{1,5},{5... | collective-permute-start | bytes 786440 | tf_op jit(solution)/shard_map/ppermute | solution.py:25
  65.3 9.5 %copy-start.4 = (bf16[256,256]{1,0:T(8,128)(2,1)S(1)}, bf16[256,256]{1,0:T(8,128)(2,1)}, u32[]{:S(2)}) copy-start(bf16[256,256]{1,0:T(8,128)(2,1)} %weight_ref.1) | copy-start | bytes 393220

commit v3 on v2

--- a/solution.py
+++ b/solution.py
@@ -30,13 +30,13 @@
     return lax.ppermute(block, axis, [(i, i ^ bit) for i in range(count)])
 
 
-def fill_slots(codes_ref, rows, out_ref, group):
+def fill_slots(codes_ref, rows, out_ref, first):
     queries = rows.shape[0]
     codes = codes_ref[...]
     slot = lax.broadcasted_iota(jnp.int32, (2 * CAP, queries), 0).astype(jnp.int16)
     one, zero = jnp.ones((), jnp.bfloat16), jnp.zeros((), jnp.bfloat16)
-    for step in range(0, BLK_DEV, 2):
-        near = (codes - (group * BLK_DEV + step) * CAP).astype(jnp.int16)
+    for step in range(0, out_ref.shape[0], 2):
+        near = (codes - (first + step) * CAP).astype(jnp.int16)
         hit = slot == near[0:1, :]
         for entry in range(1, codes.shape[0]):
             hit = hit | (slot == near[entry:entry + 1, :])
@@ -45,7 +45,7 @@
 
 
 def project_kernel(codes_ref, queries_hbm, gain_hbm, weight_hbm, rows_ref, *refs):
-    slots_ref, queries_ref, gain_ref, weight_ref, sems = refs
+    lower_ref, upper_ref, queries_ref, gain_ref, weight_ref, sems = refs
     copies = [
         pltpu.make_async_copy(source, target, sems.at[i])
         for i, (source, target) in enumerate(((queries_hbm, queries_ref), (gain_hbm, gain_ref), (weight_hbm, weight_ref)))
@@ -61,14 +61,15 @@
     normed = (centred * lax.rsqrt(spread + 1e-05) * gain_ref[...]).astype(jnp.bfloat16)
     rows = jnp.dot(normed, weight_ref[...], preferred_element_type=jnp.float32).astype(jnp.bfloat16)
     rows_ref[...] = rows
-    fill_slots(codes_ref, rows, slots_ref, 2)
-
-
-def slot_shape(width):
-    return jax.ShapeDtypeStruct((BLK_DEV, CAP, width), jnp.bfloat16)
-
-
-def project(codes, queries, gain, weight):
+    fill_slots(codes_ref, rows, lower_ref, 2 * BLK_DEV)
+    fill_slots(codes_ref, rows, upper_ref, 0)
+
+
+def slot_shape(blocks, width):
+    return jax.ShapeDtypeStruct((blocks, CAP, width), jnp.bfloat16)
+
+
+def project(codes, queries, gain, weight, blocks):
     count, width = queries.shape
     hbm = pl.BlockSpec(memory_space=pltpu.HBM)
     return pl.pallas_call(
@@ -80,23 +81,26 @@
             pltpu.VMEM(weight.shape, weight.dtype),
             pltpu.SemaphoreType.DMA((3,)),
         ],
-        out_shape=(jax.ShapeDtypeStruct((count, width), jnp.bfloat16), slot_shape(width)),
+        out_shape=(jax.ShapeDtypeStruct((count, width), jnp.bfloat16),) + (slot_shape(blocks, width),) * 2,
         compiler_params=params(),
         cost_estimate=pl.CostEstimate(flops=4 << 30, bytes_accessed=2 << 20, transcendentals=0),
         name="project",
     )(codes, queries, gain, weight)
 
 
-def scatter_kernel(codes_ref, rows_ref, prev_ref, own_ref):
+def scatter_kernel(codes_ref, rows_ref, own_ref, *refs, blocks):
     rows = rows_ref[...]
-    fill_slots(codes_ref, rows, prev_ref, 0)
-    fill_slots(codes_ref, rows, own_ref, 1)
-
-
-def scatter(codes, rows):
-    return pl.pallas_call(
-        scatter_kernel,
-        out_shape=(slot_shape(rows.shape[1]),) * 2,
+    for ref, first in zip(refs, (2 * BLK_DEV + blocks, blocks)):
+        fill_slots(codes_ref, rows, ref, first)
+    fill_slots(codes_ref, rows, own_ref, BLK_DEV)
+
+
+def scatter(codes, rows, blocks):
+    width = rows.shape[1]
+    rest = BLK_DEV - blocks
+    return pl.pallas_call(
+        functools.partial(scatter_kernel, blocks=blocks),
+        out_shape=(slot_shape(BLK_DEV, width),) + ((slot_shape(rest, width),) * 2 if rest else ()),
         compiler_params=params(),
         cost_estimate=pl.CostEstimate(flops=1 << 30, bytes_accessed=2 << 20, transcendentals=0),
         name="scatter",
@@ -128,12 +132,8 @@
     )(w_key, w_value, *features)
 
 
-def attend_kernel(rows_ref, kv_ref, *refs, stack, start):
-    out_ref, scores_ref = refs[-2:]
+def attend_kernel(rows_ref, kv_ref, out_ref, scores_ref, *, stack, start):
     blocks, (_, count, width) = kv_ref.shape[0], rows_ref.shape
-    if len(refs) > 2:
-        out_ref[:start] = refs[0][...]
-    base = out_ref.shape[0] - blocks
     head_size = width // HEADS
     factor = head_size ** (-0.5) * LOG2_E
     head_of = lax.broadcasted_iota(jnp.int32, (1, width), 1) // head_size
@@ -169,26 +169,25 @@
                     part = got[i * count:(i + 1) * count]
                     merged = part if first + i == 0 else jnp.where(head_of == first + i, part, merged)
                 scores = following
-            out_ref[base + b] = merged.astype(jnp.bfloat16)
+            out_ref[b] = merged.astype(jnp.bfloat16)
         scores_ref[...] = scores
 
 
-def attend(rows, kv, start, before=None):
+def attend(rows, kv, start=0):
     _, count, width = rows.shape
     blocks, keys = kv.shape[:2]
     stack = 2
     pairs = blocks * count * keys
-    done = 0 if before is None else start
     return pl.pallas_call(
         functools.partial(attend_kernel, stack=stack, start=start),
-        out_shape=jax.ShapeDtypeStruct((done + blocks, count, width), jnp.bfloat16),
+        out_shape=jax.ShapeDtypeStruct((blocks, count, width), jnp.bfloat16),
         scratch_shapes=[pltpu.VMEM((stack * count, keys), jnp.float32)],
         compiler_params=params(),
         cost_estimate=pl.CostEstimate(
             flops=4 * pairs * width * HEADS, bytes_accessed=blocks * keys * width * 4,
             transcendentals=pairs * HEADS),
         name="attend",
-    )(rows, kv, *([] if before is None else [before]))
+    )(rows, kv)
 
 
 def pick_kernel(codes_ref, *out_refs, groups):
@@ -292,38 +291,47 @@
         held = [[whole_sector]]
     selected = picks(codes, (0, 1, 2))
     codes, *selected = lax.optimization_barrier((codes, *selected))
-    projected, slots_next = project(codes, rows_in, norm_gain.reshape(1, width), w_query)
-    lower = shifted(slots_next, "sector", 1)
-    projected, _ = lax.optimization_barrier((projected, slots_next))
-    slots_prev, slots_own = scatter(codes, projected)
-    kv = keys_and_values(held[0], w_key, w_value, keys)
-    half = kv.shape[0]
-    own = [attend(slots_own, kv, 0)]
-    slots_prev, own[0] = lax.optimization_barrier((slots_prev, own[0]))
-    upper = shifted(slots_prev, "sector", -1)
-    kv, lower, own[0] = lax.optimization_barrier((kv, lower, own[0]))
-    from_lower = attend(lower, kv, 0)
-    kvs = [kv]
+    blocks = BLK_DEV // 2 if staged else BLK_DEV
+    projected, *ready = project(codes, rows_in, norm_gain.reshape(1, width), w_query, blocks)
+
+    def send(lower, upper):
+        lower = shifted(lower, "sector", 1)
+        return lower, shifted(upper, "sector", -1)
+
+    visits = [send(*ready)]
+    projected, *_ = lax.optimization_barrier((projected, *ready))
+    slots_own, *ready = scatter(codes, projected, blocks)
+    kvs = [keys_and_values(held[0], w_key, w_value, keys)]
+    own = [attend(slots_own, kvs[0])]
+    last = own[0]
     if staged:
-        across, from_lower = lax.optimization_barrier((across, from_lower))
-        kvs.append(keys_and_values([across, swapped(across, "band", 1)], w_key, w_value, keys))
-        from_lower = attend(lower, kvs[1], half, from_lower)
-    back_lower = shifted(from_lower, "sector", -1)
-    back_upper = []
-    last = from_lower
-    for part, kv in enumerate(kvs):
-        turn, last = lax.optimization_barrier((upper, last))
-        last = attend(turn, kv, part * half)
-        back_upper.append(shifted(last, "sector", 1))
+        *ready, last = lax.optimization_barrier((*ready, last))
+        visits.append(send(*ready))
+    back = []
+    for part, (lower, upper) in enumerate(visits):
+        if part:
+            kvs.append(keys_and_values([across, beyond], w_key, w_value, keys))
+        lower, last = lax.optimization_barrier((lower, last))
+        lower = attend(lower, kvs[part])
+        if staged and not part:
+            across, lower = lax.optimization_barrier((across, lower))
+            beyond = swapped(across, "band", 1)
+        upper, lower = lax.optimization_barrier((upper, lower))
+        upper = attend(upper, kvs[part])
+        lower, upper = lax.optimization_barrier((lower, upper))
+        back.append((shifted(lower, "sector", -1), shifted(upper, "sector", 1)))
+        last = upper
     if staged:
         turn, last = lax.optimization_barrier((slots_own, last))
-        own.append(attend(turn, kvs[1], half))
-
-    cuts = [i * half * CAP for i in range(len(kvs))]
-    early = [((1, at), rows) for at, rows in zip(cuts, own)] + [((2, 0), back_lower)]
-    early += [((0, at), rows) for at, rows in zip(cuts[:-1], back_upper)]
+        own.append(attend(turn, kvs[1], blocks))
+
+    cuts = [i * blocks * CAP for i in range(len(kvs))]
+    early = [((1, at), rows) for at, rows in zip(cuts, own)]
+    pairs = [[((2, at), lower), ((0, at), upper)] for at, (lower, upper) in zip(cuts, back)]
+    early += [pair for group in pairs[:-1] for pair in group]
     partial = partial_sum(selected, [rows for _, rows in early], tuple(at for at, _ in early))
-    out = finish(partial, rows_in, w_out, selected, back_upper[-1:], ((0, cuts[-1]),))
+    late = pairs[-1]
+    out = finish(partial, rows_in, w_out, selected, [rows for _, rows in late], tuple(at for at, _ in late))
     return out.reshape(azim_cells, range_cells, width)
 
 

time: 77 us -> 88.3 us (1.15)
  starting transfers between devices: 9.93 us -> 23.4 us
  waiting for transfers between devices: 18.7 us -> 16.2 us
    ppermute x5 -> x8, starting transfers between devices: 6.72 us -> 20.2 us  [shifted(): lax.ppermute(block, axis, [(i, (i + distance) % count) for i in range(cou...]
    ppermute x5 -> x8, waiting for transfers between devices: 18 us -> 16.2 us  [shifted(): lax.ppermute(block, axis, [(i, (i + distance) % count) for i in range(cou...]
  transfers between devices with their start and end apart: 8 -> 11, of which waited for: 4 -> 3; matrix products, arithmetic and copies ran while one was open for 1% -> 1% of each run, Pallas kernels for 59% -> 51%
where the time goes in v3:
time: 88.3 us; the launch traced here: 88.1 us
  Pallas kernels  47.4 us (54%)
  starting transfers between devices  23.4 us (27%)
  waiting for transfers between devices  16.2 us (18%)
    pallas_call x6, Pallas kernels, attend(): pl.pallas_call(functools.partial(attend_kernel, stack=stack, start=start)...  36 us
    ppermute x8, starting transfers between devices, shifted(): lax.ppermute(block, axis, [(i, (i + distance) % count) for i in range(cou...  20.2 us
    ppermute x8, waiting for transfers between devices, shifted(): lax.ppermute(block, axis, [(i, (i + distance) % count) for i in range(cou...  16.2 us
    ppermute x3, starting transfers between devices, swapped(): return lax.ppermute(block, axis, [(i, i ^ bit) for i in range(count)])  3.21 us
    pallas_call x2, Pallas kernels, keys_and_values(): pl.pallas_call(kv_kernel, out_shape=jax.ShapeDtypeStruct((count // keys,...  2.51 us
    pallas_call x1, Pallas kernels, finish(): pl.pallas_call(functools.partial(final_kernel, places=places), out_shape=...  2.51 us
    pallas_call x1, Pallas kernels, picks(): pl.pallas_call(functools.partial(pick_kernel, groups=groups), out_shape=(...  2.5 us
  transfers between devices with their start and end apart: 11, of which 3 were waited for; matrix products, arithmetic and copies ran while one was open for 1% of the time, Pallas kernels for 51%

profile of v3, /device:TPU:0, one launch (start us, length us, event | category | flops | bytes accessed | tf_op | source)
XLA Modules:
  0.0 88.1 jit_solution(5190743617722551115)
XLA Ops:
  0.0 0.6 collective-permute-start
  0.6 2.6 %collective-permute-start.4 = (bf16[2048,256]{1,0:T(8,128)(2,1)}, bf16[2048,256]{1,0:T(8,128)(2,1)S(1)}, u32[]{:S(2)}, u32[]{:S(2)}) collective-permute-start(bf16[2048,256]{1,0:T(8,128)(2,1)} %refs_0_.1), channel_id=1, source_target_pairs={{0,2},{1,3},{2,0},{3,1},{4,6},{5,7},{6,4},{7,5},{8,10},{9,11},{10,... | collective-permute-start | bytes 3145736 | tf_op jit(solution)/shard_map/ppermute | solution.py:30
  3.2 0.8 select_bitcast_fusion
  3.9 0.1 reshape.12.codes_ref
  4.0 2.5 %picks.1 = (bf16[1024,1024]{1,0:T(8,128)(2,1)S(1)}, bf16[1024,1024]{1,0:T(8,128)(2,1)S(1)}, bf16[1024,1024]{1,0:T(8,128)(2,1)S(1)}) custom-call(s32[3,1024]{1,0:T(4,128)S(1)} %reshape.12.codes_ref), custom_call_target="tpu_custom_call" | custom-call | flops 1073741824 | bytes 2097152 | tf_op jit(solution)/shard_map/picks/pallas_call | solution.py:211
  6.5 0.0 copy-start
  6.5 0.0 copy-start.2
  6.6 0.0 copy-start.3
  6.6 1.4 %project.1 = (bf16[1024,256]{1,0:T(8,128)(2,1)S(1)}, bf16[4,128,256]{2,1,0:T(8,128)(2,1)S(1)}, bf16[4,128,256]{2,1,0:T(8,128)(2,1)S(1)}) custom-call(s32[3,1024]{1,0:T(4,128)S(1)} %reshape.12.codes_ref, bf16[1024,256]{1,0:T(8,128)(2,1)S(1)} %bitcast.5, f32[1,256]{1,0:T(1,128)S(1)} %bitcast.7, bf16[256,256]{1,0:T(8,128)(2,1)S(1)} %copy-done.5), custom_call_target="tpu_custom_call" | custom-call | flops 4294967296 | bytes 2097152 | tf_op jit(solution)/shard_map/project/pallas_call | solution.py:75
  7.9 1.5 %collective-permute-start.5 = (bf16[4,128,256]{2,1,0:T(8,128)(2,1)S(1)}, bf16[4,128,256]{2,1,0:T(8,128)(2,1)S(1)}, u32[]{:S(2)}, u32[]{:S(2)}) collective-permute-start(bf16[4,128,256]{2,1,0:T(8,128)(2,1)S(1)} %get-tuple-element.47), channel_id=1, source_target_pairs={{0,4},{4,8},{8,12},{12,16},{16,20},{20,24},{24,28},{28,0},{1,5},{5... | collective-permute-start | bytes 786440 | tf_op jit(solution)/shard_map/ppermute | solution.py:25
  9.5 3.3 %collective-permute-start.3 = (bf16[4,128,256]{2,1,0:T(8,128)(2,1)S(1)}, bf16[4,128,256]{2,1,0:T(8,128)(2,1)S(1)}, u32[]{:S(2)}, u32[]{:S(2)}) collective-permute-start(bf16[4,128,256]{2,1,0:T(8,128)(2,1)S(1)} %get-tuple-element.46), channel_id=1, source_target_pairs={{0,28},{4,0},{8,4},{12,8},{16,12},{20,16},{24,20},{28,24},{1,29},{... | collective-permute-start | bytes 786440 | tf_op jit(solution)/shard_map/ppermute | solution.py:25
  12.8 8.2 %collective-permute-done.5.rows_ref = bf16[4,128,256]{2,1,0:T(8,128)(2,1)S(1)} collective-permute-done((bf16[4,128,256]{2,1,0:T(8,128)(2,1)S(1)}, bf16[4,128,256]{2,1,0:T(8,128)(2,1)S(1)}, u32[]{:S(2)}, u32[]{:S(2)}) %collective-permute-start.5) | collective-permute-done | bytes 262176 | tf_op jit(solution)/shard_map/ppermute | solution.py:25
  21.0 1.3 %keys_and_values.2.kv_ref = bf16[4,1024,512]{2,1,0:T(8,128)(2,1)S(1)} custom-call(bf16[256,256]{1,0:T(8,128)(2,1)S(1)} %copy-done.2, bf16[256,256]{1,0:T(8,128)(2,1)S(1)} %copy-done.3, bf16[2048,256]{1,0:T(8,128)(2,1)S(1)} %copy-done, bf16[2048,256]{1,0:T(8,128)(2,1)S(1)} %collective-permute-done.refs_1_), custom_call_target="tpu_custom_call" | custom-call | flops 1073741824 | bytes 6291456 | tf_op jit(solution)/shard_map/keys_and_values/pallas_call | solution.py:126
  22.3 6.1 %attend.7 = bf16[4,128,256]{2,1,0:T(8,128)(2,1)S(1)} custom-call(bf16[4,128,256]{2,1,0:T(8,128)(2,1)S(1)} %collective-permute-done.5.rows_ref, bf16[4,1024,512]{2,1,0:T(8,128)(2,1)S(1)} %keys_and_values.2.kv_ref), custom_call_target="tpu_custom_call" | custom-call | flops 4294967296 | bytes 4194304 | tf_op jit(solution)/shard_map/attend/pallas_call | solution.py:181
  28.3 0.1 collective-permute-start.6
  28.4 1.3 %scatter.1 = (bf16[8,128,256]{2,1,0:T(8,128)(2,1)S(1)}, bf16[4,128,256]{2,1,0:T(8,128)(2,1)S(1)}, bf16[4,128,256]{2,1,0:T(8,128)(2,1)S(1)}) custom-call(s32[3,1024]{1,0:T(4,128)S(1)} %reshape.12.codes_ref, bf16[1024,256]{1,0:T(8,128)(2,1)S(1)} %get-tuple-element.40.rows_ref), custom_call_target="tpu_custom_call" | custom-call | flops 1073741824 | bytes 2097152 | tf_op jit(solution)/shard_map/scatter/pallas_call | solution.py:101
  29.7 6.0 %attend.6.refs_3_ = bf16[4,128,256]{2,1,0:T(8,128)(2,1)S(1)} custom-call(bf16[8,128,256]{2,1,0:T(8,128)(2,1)S(1)} %get-tuple-element.57.rows_ref, bf16[4,1024,512]{2,1,0:T(8,128)(2,1)S(1)} %keys_and_values.2.kv_ref), custom_call_target="tpu_custom_call" | custom-call | flops 4294967296 | bytes 4194304 | tf_op jit(solution)/shard_map/attend/pallas_call | solution.py:181
  35.7 2.8 %collective-permute-start.2 = (bf16[4,128,256]{2,1,0:T(8,128)(2,1)S(1)}, bf16[4,128,256]{2,1,0:T(8,128)(2,1)S(1)}, u32[]{:S(2)}, u32[]{:S(2)}) collective-permute-start(bf16[4,128,256]{2,1,0:T(8,128)(2,1)S(1)} %get-tuple-element.45), channel_id=1, source_target_pairs={{0,4},{4,8},{8,12},{12,16},{16,20},{20,24},{24,28},{28,0},{1,5},{5... | collective-permute-start | bytes 786440 | tf_op jit(solution)/shard_map/ppermute | solution.py:25
  38.5 6.0 %attend.8 = bf16[4,128,256]{2,1,0:T(8,128)(2,1)S(1)} custom-call(bf16[4,128,256]{2,1,0:T(8,128)(2,1)S(1)} %collective-permute-done.3.rows_ref, bf16[4,1024,512]{2,1,0:T(8,128)(2,1)S(1)} %keys_and_values.2.kv_ref), custom_call_target="tpu_custom_call" | custom-call | flops 4294967296 | bytes 4194304 | tf_op jit(solution)/shard_map/attend/pallas_call | solution.py:181
  44.5 3.1 %collective-permute-start.7 = (bf16[4,128,256]{2,1,0:T(8,128)(2,1)S(1)}, bf16[4,128,256]{2,1,0:T(8,128)(2,1)S(1)}, u32[]{:S(2)}, u32[]{:S(2)}) collective-permute-start(bf16[4,128,256]{2,1,0:T(8,128)(2,1)S(1)} %attend.7), channel_id=1, source_target_pairs={{0,28},{4,0},{8,4},{12,8},{16,12},{20,16},{24,20},{28,24},{1,29},{... | collective-permute-start | bytes 786440 | tf_op jit(solution)/shard_map/ppermute | solution.py:25
  47.6 4.7 %collective-permute-start.1 = (bf16[4,128,256]{2,1,0:T(8,128)(2,1)S(1)}, bf16[4,128,256]{2,1,0:T(8,128)(2,1)S(1)}, u32[]{:S(2)}, u32[]{:S(2)}) collective-permute-start(bf16[4,128,256]{2,1,0:T(8,128)(2,1)S(1)} %get-tuple-element.44), channel_id=1, source_target_pairs={{0,28},{4,0},{8,4},{12,8},{16,12},{20,16},{24,20},{28,24},{1,29},{... | collective-permute-start | bytes 786440 | tf_op jit(solution)/shard_map/ppermute | solution.py:25
  52.3 1.3 %keys_and_values.3.kv_ref = bf16[4,1024,512]{2,1,0:T(8,128)(2,1)S(1)} custom-call(bf16[256,256]{1,0:T(8,128)(2,1)S(1)} %copy-done.2, bf16[256,256]{1,0:T(8,128)(2,1)S(1)} %copy-done.3, bf16[2048,256]{1,0:T(8,128)(2,1)S(1)} %collective-permute-done.4.refs_0_, bf16[2048,256]{1,0:T(8,128)(2,1)S(1)} %collective-permute-done.6.refs_1_), custom_call_target="tpu_custom_call" | custom-call | flops 1073741824 | bytes 6291456 | tf_op jit(solution)/shard_map/keys_and_values/pallas_call | solution.py:126
  53.6 6.0 %attend.9 = bf16[4,128,256]{2,1,0:T(8,128)(2,1)S(1)} custom-call(bf16[4,128,256]{2,1,0:T(8,128)(2,1)S(1)} %collective-permute-done.2.rows_ref, bf16[4,1024,512]{2,1,0:T(8,128)(2,1)S(1)} %keys_and_values.3.kv_ref), custom_call_target="tpu_custom_call" | custom-call | flops 4294967296 | bytes 4194304 | tf_op jit(solution)/shard_map/attend/pallas_call | solution.py:181
  59.6 5.8 %collective-permute-done.1.rows_ref = bf16[4,128,256]{2,1,0:T(8,128)(2,1)S(1)} collective-permute-done((bf16[4,128,256]{2,1,0:T(8,128)(2,1)S(1)}, bf16[4,128,256]{2,1,0:T(8,128)(2,1)S(1)}, u32[]{:S(2)}, u32[]{:S(2)}) %collective-permute-start.1) | collective-permute-done | bytes 262176 | tf_op jit(solution)/shard_map/ppermute | solution.py:25
  65.3 6.0 %attend.10 = bf16[4,128,256]{2,1,0:T(8,128)(2,1)S(1)} custom-call(bf16[4,128,256]{2,1,0:T(8,128)(2,1)S(1)} %collective-permute-done.1.rows_ref, bf16[4,1024,512]{2,1,0:T(8,128)(2,1)S(1)} %keys_and_values.3.kv_ref), custom_call_target="tpu_custom_call" | custom-call | flops 4294967296 | bytes 4194304 | tf_op jit(solution)/shard_map/attend/pallas_call | solution.py:181
  71.3 0.1 collective-permute-start.10
  71.4 4.7 %collective-permute-start.9 = (bf16[4,128,256]{2,1,0:T(8,128)(2,1)S(1)}, bf16[4,128,256]{2,1,0:T(8,128)(2,1)S(1)}, u32[]{:S(2)}, u32[]{:S(2)}) collective-permute-start(bf16[4,128,256]{2,1,0:T(8,128)(2,1)S(1)} %attend.9), channel_id=1, source_target_pairs={{0,28},{4,0},{8,4},{12,8},{16,12},{20,16},{24,20},{28,24},{1,29},{... | collective-permute-start | bytes 786440 | tf_op jit(solution)/shard_map/ppermute | solution.py:25
  76.1 6.0 %attend.11.refs_4_ = bf16[4,128,256]{2,1,0:T(8,128)(2,1)S(1)} custom-call(bf16[8,128,256]{2,1,0:T(8,128)(2,1)S(1)} %get-tuple-element.57.rows_ref, bf16[4,1024,512]{2,1,0:T(8,128)(2,1)S(1)} %keys_and_values.3.kv_ref), custom_call_target="tpu_custom_call" | custom-call | flops 4294967296 | bytes 4194304 | tf_op jit(solution)/shard_map/attend/pallas_call | solution.py:181
  82.1 0.0 copy-start.4
  82.1 1.2 %partial_sum.1.partial_ref = f32[1024,256]{1,0:T(8,128)S(1)} custom-call(bf16[1024,1024]{1,0:T(8,128)(2,1)S(1)} %get-tuple-element.36.refs_0_, bf16[1024,1024]{1,0:T(8,128)(2,1)S(1)} %get-tuple-element.37.refs_1_, bf16[1024,1024]{1,0:T(8,128)(2,1)S(1)} %get-tuple-element.38.refs_2_, bf16[4,128,256]{2,1,0:T(8,128)(2,1)S(1)} %attend.6.refs_3_, ...), custom_call_target="tpu_custom_call" | custom-call | flops 1073741824 | bytes 2097152 | tf_op jit(solution)/shard_map/partial_sum/pallas_call | solution.py:240
  83.4 2.2 %collective-permute-done.9.refs_3_ = bf16[4,128,256]{2,1,0:T(8,128)(2,1)S(1)} collective-permute-done((bf16[4,128,256]{2,1,0:T(8,128)(2,1)S(1)}, bf16[4,128,256]{2,1,0:T(8,128)(2,1)S(1)}, u32[]{:S(2)}, u32[]{:S(2)}) %collective-permute-start.9) | collective-permute-done | bytes 262176 | tf_op jit(solution)/shard_map/ppermute | solution.py:25
  85.6 2.5 %finish.1 = bf16[1024,256]{1,0:T(8,128)(2,1)} custom-call(f32[1024,256]{1,0:T(8,128)S(1)} %partial_sum.1.partial_ref, bf16[1024,256]{1,0:T(8,128)(2,1)S(1)} %bitcast.6, bf16[256,256]{1,0:T(8,128)(2,1)S(1)} %copy-done.4, bf16[1024,1024]{1,0:T(8,128)(2,1)S(1)} %get-tuple-element.36.refs_0_, bf16[1024,1024]{1,0:T(8,128)(2,1)S(1)} %get-tuple-element.37.refs_1_, ...), custom_call_target="tpu_custom_call" | custom-call | flops 1073741824 | bytes 2097152 | tf_op jit(solution)/shard_map/finish/pallas_call | solution.py:260
  (19 shorter events, 0.0 us)
Async XLA Ops:
  0.0 6.5 %copy-start.5 = (bf16[256,256]{1,0:T(8,128)(2,1)S(1)}, bf16[256,256]{1,0:T(8,128)(2,1)}, u32[]{:S(2)}) copy-start(bf16[256,256]{1,0:T(8,128)(2,1)} %weight_hbm.1) | copy-start | bytes 393220
  0.0 6.5 %copy-start.6 = (f32[256]{0:T(256)S(1)}, f32[256]{0:T(256)}, u32[]{:S(2)}) copy-start(f32[256]{0:T(256)} %param.10) | copy-start | bytes 3076
  0.0 6.5 %copy-start.1 = (bf16[16,64,256]{2,1,0:T(8,128)(2,1)S(1)}, bf16[16,64,256]{2,1,0:T(8,128)(2,1)}, u32[]{:S(2)}) copy-start(bf16[16,64,256]{2,1,0:T(8,128)(2,1)} %param.9) | copy-start | bytes 1572868
  0.0 21.0 %collective-permute-start = (bf16[2048,256]{1,0:T(8,128)(2,1)}, bf16[2048,256]{1,0:T(8,128)(2,1)S(1)}, u32[]{:S(2)}, u32[]{:S(2)}) collective-permute-start(bf16[2048,256]{1,0:T(8,128)(2,1)} %refs_0_.1), channel_id=1, source_target_pairs={{0,1},{1,0},{2,3},{3,2},{4,5},{5,4},{6,7},{7,6},{8,9},{9,8},{10,11... | collective-permute-start | bytes 3145736 | tf_op jit(solution)/shard_map/ppermute | solution.py:30
  0.6 27.8 %collective-permute-start.4 = (bf16[2048,256]{1,0:T(8,128)(2,1)}, bf16[2048,256]{1,0:T(8,128)(2,1)S(1)}, u32[]{:S(2)}, u32[]{:S(2)}) collective-permute-start(bf16[2048,256]{1,0:T(8,128)(2,1)} %refs_0_.1), channel_id=1, source_target_pairs={{0,2},{1,3},{2,0},{3,1},{4,6},{5,7},{6,4},{7,5},{8,10},{9,11},{10,... | collective-permute-start | bytes 3145736 | tf_op jit(solution)/shard_map/ppermute | solution.py:30
  6.5 14.4 %copy-start = (bf16[2048,256]{1,0:T(8,128)(2,1)S(1)}, bf16[2048,256]{1,0:T(8,128)(2,1)}, u32[]{:S(2)}) copy-start(bf16[2048,256]{1,0:T(8,128)(2,1)} %refs_0_.1) | copy-start | bytes 3145732
  6.5 14.4 %copy-start.2 = (bf16[256,256]{1,0:T(8,128)(2,1)S(1)}, bf16[256,256]{1,0:T(8,128)(2,1)}, u32[]{:S(2)}) copy-start(bf16[256,256]{1,0:T(8,128)(2,1)} %key_ref.3) | copy-start | bytes 393220
  6.6 14.4 %copy-start.3 = (bf16[256,256]{1,0:T(8,128)(2,1)S(1)}, bf16[256,256]{1,0:T(8,128)(2,1)}, u32[]{:S(2)}) copy-start(bf16[256,256]{1,0:T(8,128)(2,1)} %value_ref.3) | copy-start | bytes 393220
  7.9 13.0 %collective-permute-start.5 = (bf16[4,128,256]{2,1,0:T(8,128)(2,1)S(1)}, bf16[4,128,256]{2,1,0:T(8,128)(2,1)S(1)}, u32[]{:S(2)}, u32[]{:S(2)}) collective-permute-start(bf16[4,128,256]{2,1,0:T(8,128)(2,1)S(1)} %get-tuple-element.47), channel_id=1, source_target_pairs={{0,4},{4,8},{8,12},{12,16},{16,20},{20,24},{24,28},{28,0},{1,5},{5... | collective-permute-start | bytes 786440 | tf_op jit(solution)/shard_map/ppermute | solution.py:25
  9.5 20.2 %collective-permute-start.3 = (bf16[4,128,256]{2,1,0:T(8,128)(2,1)S(1)}, bf16[4,128,256]{2,1,0:T(8,128)(2,1)S(1)}, u32[]{:S(2)}, u32[]{:S(2)}) collective-permute-start(bf16[4,128,256]{2,1,0:T(8,128)(2,1)S(1)} %get-tuple-element.46), channel_id=1, source_target_pairs={{0,28},{4,0},{8,4},{12,8},{16,12},{20,16},{24,20},{28,24},{1,29},{... | collective-permute-start | bytes 786440 | tf_op jit(solution)/shard_map/ppermute | solution.py:25
  28.3 24.0 %collective-permute-start.6 = (bf16[2048,256]{1,0:T(8,128)(2,1)S(1)}, bf16[2048,256]{1,0:T(8,128)(2,1)S(1)}, u32[]{:S(2)}, u32[]{:S(2)}) collective-permute-start(bf16[2048,256]{1,0:T(8,128)(2,1)S(1)} %collective-permute-done.4.refs_0_), channel_id=1, source_target_pairs={{0,1},{1,0},{2,3},{3,2},{4,5},{5,4},{6,7},{7,6},{8,9},{9,8},{10,11... | collective-permute-start | bytes 3145736 | tf_op jit(solution)/shard_map/ppermute | solution.py:30
  35.7 16.6 %collective-permute-start.2 = (bf16[4,128,256]{2,1,0:T(8,128)(2,1)S(1)}, bf16[4,128,256]{2,1,0:T(8,128)(2,1)S(1)}, u32[]{:S(2)}, u32[]{:S(2)}) collective-permute-start(bf16[4,128,256]{2,1,0:T(8,128)(2,1)S(1)} %get-tuple-element.45), channel_id=1, source_target_pairs={{0,4},{4,8},{8,12},{12,16},{16,20},{20,24},{24,28},{28,0},{1,5},{5... | collective-permute-start | bytes 786440 | tf_op jit(solution)/shard_map/ppermute | solution.py:25
  44.5 37.7 %collective-permute-start.7 = (bf16[4,128,256]{2,1,0:T(8,128)(2,1)S(1)}, bf16[4,128,256]{2,1,0:T(8,128)(2,1)S(1)}, u32[]{:S(2)}, u32[]{:S(2)}) collective-permute-start(bf16[4,128,256]{2,1,0:T(8,128)(2,1)S(1)} %attend.7), channel_id=1, source_target_pairs={{0,28},{4,0},{8,4},{12,8},{16,12},{20,16},{24,20},{28,24},{1,29},{... | collective-permute-start | bytes 786440 | tf_op jit(solution)/shard_map/ppermute | solution.py:25
  47.6 34.6 %collective-permute-start.8 = (bf16[4,128,256]{2,1,0:T(8,128)(2,1)S(1)}, bf16[4,128,256]{2,1,0:T(8,128)(2,1)S(1)}, u32[]{:S(2)}, u32[]{:S(2)}) collective-permute-start(bf16[4,128,256]{2,1,0:T(8,128)(2,1)S(1)} %attend.8), channel_id=1, source_target_pairs={{0,4},{4,8},{8,12},{12,16},{16,20},{20,24},{24,28},{28,0},{1,5},{5... | collective-permute-start | bytes 786440 | tf_op jit(solution)/shard_map/ppermute | solution.py:25
  47.6 17.8 %collective-permute-start.1 = (bf16[4,128,256]{2,1,0:T(8,128)(2,1)S(1)}, bf16[4,128,256]{2,1,0:T(8,128)(2,1)S(1)}, u32[]{:S(2)}, u32[]{:S(2)}) collective-permute-start(bf16[4,128,256]{2,1,0:T(8,128)(2,1)S(1)} %get-tuple-element.44), channel_id=1, source_target_pairs={{0,28},{4,0},{8,4},{12,8},{16,12},{20,16},{24,20},{28,24},{1,29},{... | collective-permute-start | bytes 786440 | tf_op jit(solution)/shard_map/ppermute | solution.py:25
  71.3 14.3 %collective-permute-start.10 = (bf16[4,128,256]{2,1,0:T(8,128)(2,1)S(1)}, bf16[4,128,256]{2,1,0:T(8,128)(2,1)S(1)}, u32[]{:S(2)}, u32[]{:S(2)}) collective-permute-start(bf16[4,128,256]{2,1,0:T(8,128)(2,1)S(1)} %attend.10), channel_id=1, source_target_pairs={{0,4},{4,8},{8,12},{12,16},{16,20},{20,24},{24,28},{28,0},{1,5},{5... | collective-permute-start | bytes 786440 | tf_op jit(solution)/shard_map/ppermute | solution.py:25
  71.4 14.2 %collective-permute-start.9 = (bf16[4,128,256]{2,1,0:T(8,128)(2,1)S(1)}, bf16[4,128,256]{2,1,0:T(8,128)(2,1)S(1)}, u32[]{:S(2)}, u32[]{:S(2)}) collective-permute-start(bf16[4,128,256]{2,1,0:T(8,128)(2,1)S(1)} %attend.9), channel_id=1, source_target_pairs={{0,28},{4,0},{8,4},{12,8},{16,12},{20,16},{24,20},{28,24},{1,29},{... | collective-permute-start | bytes 786440 | tf_op jit(solution)/shard_map/ppermute | solution.py:25
  82.1 3.5 %copy-start.4 = (bf16[256,256]{1,0:T(8,128)(2,1)S(1)}, bf16[256,256]{1,0:T(8,128)(2,1)}, u32[]{:S(2)}) copy-start(bf16[256,256]{1,0:T(8,128)(2,1)} %weight_ref.1) | copy-start | bytes 393220

commit v4 on v3

--- a/solution.py
+++ b/solution.py
@@ -313,24 +313,26 @@
             kvs.append(keys_and_values([across, beyond], w_key, w_value, keys))
         lower, last = lax.optimization_barrier((lower, last))
         lower = attend(lower, kvs[part])
-        if staged and not part:
-            across, lower = lax.optimization_barrier((across, lower))
-            beyond = swapped(across, "band", 1)
         upper, lower = lax.optimization_barrier((upper, lower))
         upper = attend(upper, kvs[part])
-        lower, upper = lax.optimization_barrier((lower, upper))
-        back.append((shifted(lower, "sector", -1), shifted(upper, "sector", 1)))
+        if staged and not part:
+            lower, upper, across = lax.optimization_barrier((lower, upper, across))
+            beyond = swapped(across, "band", 1)
+        lower = shifted(lower, "sector", -1)
         last = upper
+        upper = shifted(upper, "sector", 1)
+        back.append((lower, upper))
     if staged:
         turn, last = lax.optimization_barrier((slots_own, last))
         own.append(attend(turn, kvs[1], blocks))
 
     cuts = [i * blocks * CAP for i in range(len(kvs))]
     early = [((1, at), rows) for at, rows in zip(cuts, own)]
-    pairs = [[((2, at), lower), ((0, at), upper)] for at, (lower, upper) in zip(cuts, back)]
-    early += [pair for group in pairs[:-1] for pair in group]
+    returned = [((2, at), lower) for at, (lower, _) in zip(cuts, back)]
+    returned += [((0, at), upper) for at, (_, upper) in zip(cuts, back)]
+    early += returned[:-1]
     partial = partial_sum(selected, [rows for _, rows in early], tuple(at for at, _ in early))
-    late = pairs[-1]
+    late = returned[-1:]
     out = finish(partial, rows_in, w_out, selected, [rows for _, rows in late], tuple(at for at, _ in late))
     return out.reshape(azim_cells, range_cells, width)
 

time: 88.3 us -> 93.3 us (1.057)
  waiting for transfers between devices: 16.2 us -> 20.6 us
  starting transfers between devices: 23.4 us -> 24.4 us
    ppermute x8, waiting for transfers between devices: 16.2 us -> 20.5 us  [shifted(): lax.ppermute(block, axis, [(i, (i + distance) % count) for i in range(cou...]
    ppermute x8, starting transfers between devices: 20.2 us -> 22.3 us  [shifted(): lax.ppermute(block, axis, [(i, (i + distance) % count) for i in range(cou...]
    ppermute x3, starting transfers between devices: 3.21 us -> 2.08 us  [swapped(): return lax.ppermute(block, axis, [(i, i ^ bit) for i in range(count)])]
  transfers between devices with their start and end apart: 11 -> 11, of which waited for: 3 -> 5; matrix products, arithmetic and copies ran while one was open for 1% -> 1% of each run, Pallas kernels for 51% -> 48%
where the time goes in v4:
time: 93.3 us; the launch traced here: 93.2 us
  Pallas kernels  47.2 us (51%)
  starting transfers between devices  24.4 us (26%)
  waiting for transfers between devices  20.6 us (22%)
    pallas_call x6, Pallas kernels, attend(): pl.pallas_call(functools.partial(attend_kernel, stack=stack, start=start)...  36 us
    ppermute x8, starting transfers between devices, shifted(): lax.ppermute(block, axis, [(i, (i + distance) % count) for i in range(cou...  22.3 us
    ppermute x8, waiting for transfers between devices, shifted(): lax.ppermute(block, axis, [(i, (i + distance) % count) for i in range(cou...  20.5 us
    pallas_call x2, Pallas kernels, keys_and_values(): pl.pallas_call(kv_kernel, out_shape=jax.ShapeDtypeStruct((count // keys,...  2.51 us
    pallas_call x1, Pallas kernels, picks(): pl.pallas_call(functools.partial(pick_kernel, groups=groups), out_shape=(...  2.5 us
    ppermute x3, starting transfers between devices, swapped(): return lax.ppermute(block, axis, [(i, i ^ bit) for i in range(count)])  2.08 us
    pallas_call x1, Pallas kernels, finish(): pl.pallas_call(functools.partial(final_kernel, places=places), out_shape=...  1.97 us
  transfers between devices with their start and end apart: 11, of which 5 were waited for; matrix products, arithmetic and copies ran while one was open for 1% of the time, Pallas kernels for 48%

profile of v4, /device:TPU:0, one launch (start us, length us, event | category | flops | bytes accessed | tf_op | source)
XLA Modules:
  0.0 93.2 jit_solution(3613583008530174237)
XLA Ops:
  0.0 0.6 collective-permute-start
  0.6 0.8 select_bitcast_fusion
  1.3 0.1 reshape.12.codes_ref
  1.4 2.5 %picks.1 = (bf16[1024,1024]{1,0:T(8,128)(2,1)S(1)}, bf16[1024,1024]{1,0:T(8,128)(2,1)S(1)}, bf16[1024,1024]{1,0:T(8,128)(2,1)S(1)}) custom-call(s32[3,1024]{1,0:T(4,128)S(1)} %reshape.12.codes_ref), custom_call_target="tpu_custom_call" | custom-call | flops 1073741824 | bytes 2097152 | tf_op jit(solution)/shard_map/picks/pallas_call | solution.py:211
  3.9 0.0 copy-start
  4.0 0.0 copy-start.2
  4.0 0.0 copy-start.3
  4.0 1.4 %project.1 = (bf16[1024,256]{1,0:T(8,128)(2,1)S(1)}, bf16[4,128,256]{2,1,0:T(8,128)(2,1)S(1)}, bf16[4,128,256]{2,1,0:T(8,128)(2,1)S(1)}) custom-call(s32[3,1024]{1,0:T(4,128)S(1)} %reshape.12.codes_ref, bf16[1024,256]{1,0:T(8,128)(2,1)S(1)} %bitcast.5, f32[1,256]{1,0:T(1,128)S(1)} %bitcast.7, bf16[256,256]{1,0:T(8,128)(2,1)S(1)} %copy-done.5), custom_call_target="tpu_custom_call" | custom-call | flops 4294967296 | bytes 2097152 | tf_op jit(solution)/shard_map/project/pallas_call | solution.py:75
  5.4 2.6 %collective-permute-start.4 = (bf16[4,128,256]{2,1,0:T(8,128)(2,1)S(1)}, bf16[4,128,256]{2,1,0:T(8,128)(2,1)S(1)}, u32[]{:S(2)}, u32[]{:S(2)}) collective-permute-start(bf16[4,128,256]{2,1,0:T(8,128)(2,1)S(1)} %get-tuple-element.44), channel_id=1, source_target_pairs={{0,4},{4,8},{8,12},{12,16},{16,20},{20,24},{24,28},{28,0},{1,5},{5... | collective-permute-start | bytes 786440 | tf_op jit(solution)/shard_map/ppermute | solution.py:25
  8.0 1.5 %collective-permute-start.5 = (bf16[2048,256]{1,0:T(8,128)(2,1)S(1)}, bf16[2048,256]{1,0:T(8,128)(2,1)S(1)}, u32[]{:S(2)}, u32[]{:S(2)}) collective-permute-start(bf16[2048,256]{1,0:T(8,128)(2,1)S(1)} %copy-done), channel_id=1, source_target_pairs={{0,2},{1,3},{2,0},{3,1},{4,6},{5,7},{6,4},{7,5},{8,10},{9,11},{10,... | collective-permute-start | bytes 3145736 | tf_op jit(solution)/shard_map/ppermute | solution.py:30
  9.5 3.2 %collective-permute-start.3 = (bf16[4,128,256]{2,1,0:T(8,128)(2,1)S(1)}, bf16[4,128,256]{2,1,0:T(8,128)(2,1)S(1)}, u32[]{:S(2)}, u32[]{:S(2)}) collective-permute-start(bf16[4,128,256]{2,1,0:T(8,128)(2,1)S(1)} %get-tuple-element.43), channel_id=1, source_target_pairs={{0,28},{4,0},{8,4},{12,8},{16,12},{20,16},{24,20},{28,24},{1,29},{... | collective-permute-start | bytes 786440 | tf_op jit(solution)/shard_map/ppermute | solution.py:25
  12.8 7.0 %collective-permute-done.4.rows_ref = bf16[4,128,256]{2,1,0:T(8,128)(2,1)S(1)} collective-permute-done((bf16[4,128,256]{2,1,0:T(8,128)(2,1)S(1)}, bf16[4,128,256]{2,1,0:T(8,128)(2,1)S(1)}, u32[]{:S(2)}, u32[]{:S(2)}) %collective-permute-start.4) | collective-permute-done | bytes 262176 | tf_op jit(solution)/shard_map/ppermute | solution.py:25
  19.7 1.3 %keys_and_values.2.kv_ref = bf16[4,1024,512]{2,1,0:T(8,128)(2,1)S(1)} custom-call(bf16[256,256]{1,0:T(8,128)(2,1)S(1)} %copy-done.2, bf16[256,256]{1,0:T(8,128)(2,1)S(1)} %copy-done.3, bf16[2048,256]{1,0:T(8,128)(2,1)S(1)} %copy-done, bf16[2048,256]{1,0:T(8,128)(2,1)S(1)} %collective-permute-done.refs_1_), custom_call_target="tpu_custom_call" | custom-call | flops 1073741824 | bytes 6291456 | tf_op jit(solution)/shard_map/keys_and_values/pallas_call | solution.py:126
  21.0 6.0 %attend.7 = bf16[4,128,256]{2,1,0:T(8,128)(2,1)S(1)} custom-call(bf16[4,128,256]{2,1,0:T(8,128)(2,1)S(1)} %collective-permute-done.4.rows_ref, bf16[4,1024,512]{2,1,0:T(8,128)(2,1)S(1)} %keys_and_values.2.kv_ref), custom_call_target="tpu_custom_call" | custom-call | flops 4294967296 | bytes 4194304 | tf_op jit(solution)/shard_map/attend/pallas_call | solution.py:181
  27.0 6.1 %attend.8 = bf16[4,128,256]{2,1,0:T(8,128)(2,1)S(1)} custom-call(bf16[4,128,256]{2,1,0:T(8,128)(2,1)S(1)} %collective-permute-done.3.rows_ref, bf16[4,1024,512]{2,1,0:T(8,128)(2,1)S(1)} %keys_and_values.2.kv_ref), custom_call_target="tpu_custom_call" | custom-call | flops 4294967296 | bytes 4194304 | tf_op jit(solution)/shard_map/attend/pallas_call | solution.py:181
  33.1 0.1 collective-permute-done.5.refs_0_
  33.2 1.3 %scatter.1 = (bf16[8,128,256]{2,1,0:T(8,128)(2,1)S(1)}, bf16[4,128,256]{2,1,0:T(8,128)(2,1)S(1)}, bf16[4,128,256]{2,1,0:T(8,128)(2,1)S(1)}) custom-call(s32[3,1024]{1,0:T(4,128)S(1)} %reshape.12.codes_ref, bf16[1024,256]{1,0:T(8,128)(2,1)S(1)} %get-tuple-element.37.rows_ref), custom_call_target="tpu_custom_call" | custom-call | flops 1073741824 | bytes 2097152 | tf_op jit(solution)/shard_map/scatter/pallas_call | solution.py:101
  34.5 6.0 %attend.6.refs_3_ = bf16[4,128,256]{2,1,0:T(8,128)(2,1)S(1)} custom-call(bf16[8,128,256]{2,1,0:T(8,128)(2,1)S(1)} %get-tuple-element.51.rows_ref, bf16[4,1024,512]{2,1,0:T(8,128)(2,1)S(1)} %keys_and_values.2.kv_ref), custom_call_target="tpu_custom_call" | custom-call | flops 4294967296 | bytes 4194304 | tf_op jit(solution)/shard_map/attend/pallas_call | solution.py:181
  40.5 2.8 %collective-permute-start.2 = (bf16[4,128,256]{2,1,0:T(8,128)(2,1)S(1)}, bf16[4,128,256]{2,1,0:T(8,128)(2,1)S(1)}, u32[]{:S(2)}, u32[]{:S(2)}) collective-permute-start(bf16[4,128,256]{2,1,0:T(8,128)(2,1)S(1)} %get-tuple-element.42), channel_id=1, source_target_pairs={{0,4},{4,8},{8,12},{12,16},{16,20},{20,24},{24,28},{28,0},{1,5},{5... | collective-permute-start | bytes 786440 | tf_op jit(solution)/shard_map/ppermute | solution.py:25
  43.2 3.1 %collective-permute-start.7 = (bf16[4,128,256]{2,1,0:T(8,128)(2,1)S(1)}, bf16[4,128,256]{2,1,0:T(8,128)(2,1)S(1)}, u32[]{:S(2)}, u32[]{:S(2)}) collective-permute-start(bf16[4,128,256]{2,1,0:T(8,128)(2,1)S(1)} %attend.7), channel_id=1, source_target_pairs={{0,28},{4,0},{8,4},{12,8},{16,12},{20,16},{24,20},{28,24},{1,29},{... | collective-permute-start | bytes 786440 | tf_op jit(solution)/shard_map/ppermute | solution.py:25
  46.3 4.7 %collective-permute-start.1 = (bf16[4,128,256]{2,1,0:T(8,128)(2,1)S(1)}, bf16[4,128,256]{2,1,0:T(8,128)(2,1)S(1)}, u32[]{:S(2)}, u32[]{:S(2)}) collective-permute-start(bf16[4,128,256]{2,1,0:T(8,128)(2,1)S(1)} %get-tuple-element.41), channel_id=1, source_target_pairs={{0,28},{4,0},{8,4},{12,8},{16,12},{20,16},{24,20},{28,24},{1,29},{... | collective-permute-start | bytes 786440 | tf_op jit(solution)/shard_map/ppermute | solution.py:25
  51.0 10.1 %collective-permute-done.2.rows_ref = bf16[4,128,256]{2,1,0:T(8,128)(2,1)S(1)} collective-permute-done((bf16[4,128,256]{2,1,0:T(8,128)(2,1)S(1)}, bf16[4,128,256]{2,1,0:T(8,128)(2,1)S(1)}, u32[]{:S(2)}, u32[]{:S(2)}) %collective-permute-start.2) | collective-permute-done | bytes 262176 | tf_op jit(solution)/shard_map/ppermute | solution.py:25
  61.2 1.3 %keys_and_values.3.kv_ref = bf16[4,1024,512]{2,1,0:T(8,128)(2,1)S(1)} custom-call(bf16[256,256]{1,0:T(8,128)(2,1)S(1)} %copy-done.2, bf16[256,256]{1,0:T(8,128)(2,1)S(1)} %copy-done.3, bf16[2048,256]{1,0:T(8,128)(2,1)S(1)} %collective-permute-done.5.refs_0_, bf16[2048,256]{1,0:T(8,128)(2,1)S(1)} %collective-permute-done.6.refs_1_), custom_call_target="tpu_custom_call" | custom-call | flops 1073741824 | bytes 6291456 | tf_op jit(solution)/shard_map/keys_and_values/pallas_call | solution.py:126
  62.4 6.0 %attend.9 = bf16[4,128,256]{2,1,0:T(8,128)(2,1)S(1)} custom-call(bf16[4,128,256]{2,1,0:T(8,128)(2,1)S(1)} %collective-permute-done.2.rows_ref, bf16[4,1024,512]{2,1,0:T(8,128)(2,1)S(1)} %keys_and_values.3.kv_ref), custom_call_target="tpu_custom_call" | custom-call | flops 4294967296 | bytes 4194304 | tf_op jit(solution)/shard_map/attend/pallas_call | solution.py:181
  68.4 0.1 collective-permute-done.1.rows_ref
  68.5 6.0 %attend.10 = bf16[4,128,256]{2,1,0:T(8,128)(2,1)S(1)} custom-call(bf16[4,128,256]{2,1,0:T(8,128)(2,1)S(1)} %collective-permute-done.1.rows_ref, bf16[4,1024,512]{2,1,0:T(8,128)(2,1)S(1)} %keys_and_values.3.kv_ref), custom_call_target="tpu_custom_call" | custom-call | flops 4294967296 | bytes 4194304 | tf_op jit(solution)/shard_map/attend/pallas_call | solution.py:181
  74.5 2.5 %collective-permute-start.10 = (bf16[4,128,256]{2,1,0:T(8,128)(2,1)S(1)}, bf16[4,128,256]{2,1,0:T(8,128)(2,1)S(1)}, u32[]{:S(2)}, u32[]{:S(2)}) collective-permute-start(bf16[4,128,256]{2,1,0:T(8,128)(2,1)S(1)} %attend.10), channel_id=1, source_target_pairs={{0,4},{4,8},{8,12},{12,16},{16,20},{20,24},{24,28},{28,0},{1,5},{5... | collective-permute-start | bytes 786440 | tf_op jit(solution)/shard_map/ppermute | solution.py:25
  77.0 3.4 %collective-permute-start.8 = (bf16[4,128,256]{2,1,0:T(8,128)(2,1)S(1)}, bf16[4,128,256]{2,1,0:T(8,128)(2,1)S(1)}, u32[]{:S(2)}, u32[]{:S(2)}) collective-permute-start(bf16[4,128,256]{2,1,0:T(8,128)(2,1)S(1)} %attend.9), channel_id=1, source_target_pairs={{0,28},{4,0},{8,4},{12,8},{16,12},{20,16},{24,20},{28,24},{1,29},{... | collective-permute-start | bytes 786440 | tf_op jit(solution)/shard_map/ppermute | solution.py:25
  80.3 6.0 %attend.11.refs_4_ = bf16[4,128,256]{2,1,0:T(8,128)(2,1)S(1)} custom-call(bf16[8,128,256]{2,1,0:T(8,128)(2,1)S(1)} %get-tuple-element.51.rows_ref, bf16[4,1024,512]{2,1,0:T(8,128)(2,1)S(1)} %keys_and_values.3.kv_ref), custom_call_target="tpu_custom_call" | custom-call | flops 4294967296 | bytes 4194304 | tf_op jit(solution)/shard_map/attend/pallas_call | solution.py:181
  86.4 3.3 %collective-permute-done.8.refs_6_ = bf16[4,128,256]{2,1,0:T(8,128)(2,1)S(1)} collective-permute-done((bf16[4,128,256]{2,1,0:T(8,128)(2,1)S(1)}, bf16[4,128,256]{2,1,0:T(8,128)(2,1)S(1)}, u32[]{:S(2)}, u32[]{:S(2)}) %collective-permute-start.8) | collective-permute-done | bytes 262176 | tf_op jit(solution)/shard_map/ppermute | solution.py:25
  89.7 1.5 %partial_sum.1.partial_ref = f32[1024,256]{1,0:T(8,128)S(1)} custom-call(bf16[1024,1024]{1,0:T(8,128)(2,1)S(1)} %get-tuple-element.33.refs_0_, bf16[1024,1024]{1,0:T(8,128)(2,1)S(1)} %get-tuple-element.34.refs_1_, bf16[1024,1024]{1,0:T(8,128)(2,1)S(1)} %get-tuple-element.35.refs_2_, bf16[4,128,256]{2,1,0:T(8,128)(2,1)S(1)} %attend.6.refs_3_, ...), custom_call_target="tpu_custom_call" | custom-call | flops 1073741824 | bytes 2097152 | tf_op jit(solution)/shard_map/partial_sum/pallas_call | solution.py:240
  91.2 2.0 %finish.1 = bf16[1024,256]{1,0:T(8,128)(2,1)} custom-call(f32[1024,256]{1,0:T(8,128)S(1)} %partial_sum.1.partial_ref, bf16[1024,256]{1,0:T(8,128)(2,1)S(1)} %bitcast.6, bf16[256,256]{1,0:T(8,128)(2,1)S(1)} %copy-done.4, bf16[1024,1024]{1,0:T(8,128)(2,1)S(1)} %get-tuple-element.33.refs_0_, bf16[1024,1024]{1,0:T(8,128)(2,1)S(1)} %get-tuple-element.34.refs_1_, ...), custom_call_target="tpu_custom_call" | custom-call | flops 1073741824 | bytes 2097152 | tf_op jit(solution)/shard_map/finish/pallas_call | solution.py:260
  (19 shorter events, 0.0 us)
Async XLA Ops:
  0.0 3.9 %copy-start.5 = (bf16[256,256]{1,0:T(8,128)(2,1)S(1)}, bf16[256,256]{1,0:T(8,128)(2,1)}, u32[]{:S(2)}) copy-start(bf16[256,256]{1,0:T(8,128)(2,1)} %weight_hbm.1) | copy-start | bytes 393220
  0.0 3.9 %copy-start.6 = (f32[256]{0:T(256)S(1)}, f32[256]{0:T(256)}, u32[]{:S(2)}) copy-start(f32[256]{0:T(256)} %param.10) | copy-start | bytes 3076
  0.0 3.9 %copy-start.1 = (bf16[16,64,256]{2,1,0:T(8,128)(2,1)S(1)}, bf16[16,64,256]{2,1,0:T(8,128)(2,1)}, u32[]{:S(2)}) copy-start(bf16[16,64,256]{2,1,0:T(8,128)(2,1)} %param.9) | copy-start | bytes 1572868
  0.0 19.7 %collective-permute-start = (bf16[2048,256]{1,0:T(8,128)(2,1)}, bf16[2048,256]{1,0:T(8,128)(2,1)S(1)}, u32[]{:S(2)}, u32[]{:S(2)}) collective-permute-start(bf16[2048,256]{1,0:T(8,128)(2,1)} %refs_0_.1), channel_id=1, source_target_pairs={{0,1},{1,0},{2,3},{3,2},{4,5},{5,4},{6,7},{7,6},{8,9},{9,8},{10,11... | collective-permute-start | bytes 3145736 | tf_op jit(solution)/shard_map/ppermute | solution.py:30
  3.9 4.1 %copy-start = (bf16[2048,256]{1,0:T(8,128)(2,1)S(1)}, bf16[2048,256]{1,0:T(8,128)(2,1)}, u32[]{:S(2)}) copy-start(bf16[2048,256]{1,0:T(8,128)(2,1)} %refs_0_.1) | copy-start | bytes 3145732
  4.0 15.8 %copy-start.2 = (bf16[256,256]{1,0:T(8,128)(2,1)S(1)}, bf16[256,256]{1,0:T(8,128)(2,1)}, u32[]{:S(2)}) copy-start(bf16[256,256]{1,0:T(8,128)(2,1)} %key_ref.3) | copy-start | bytes 393220
  4.0 15.8 %copy-start.3 = (bf16[256,256]{1,0:T(8,128)(2,1)S(1)}, bf16[256,256]{1,0:T(8,128)(2,1)}, u32[]{:S(2)}) copy-start(bf16[256,256]{1,0:T(8,128)(2,1)} %value_ref.3) | copy-start | bytes 393220
  5.4 14.4 %collective-permute-start.4 = (bf16[4,128,256]{2,1,0:T(8,128)(2,1)S(1)}, bf16[4,128,256]{2,1,0:T(8,128)(2,1)S(1)}, u32[]{:S(2)}, u32[]{:S(2)}) collective-permute-start(bf16[4,128,256]{2,1,0:T(8,128)(2,1)S(1)} %get-tuple-element.44), channel_id=1, source_target_pairs={{0,4},{4,8},{8,12},{12,16},{16,20},{20,24},{24,28},{28,0},{1,5},{5... | collective-permute-start | bytes 786440 | tf_op jit(solution)/shard_map/ppermute | solution.py:25
  8.0 25.2 %collective-permute-start.5 = (bf16[2048,256]{1,0:T(8,128)(2,1)S(1)}, bf16[2048,256]{1,0:T(8,128)(2,1)S(1)}, u32[]{:S(2)}, u32[]{:S(2)}) collective-permute-start(bf16[2048,256]{1,0:T(8,128)(2,1)S(1)} %copy-done), channel_id=1, source_target_pairs={{0,2},{1,3},{2,0},{3,1},{4,6},{5,7},{6,4},{7,5},{8,10},{9,11},{10,... | collective-permute-start | bytes 3145736 | tf_op jit(solution)/shard_map/ppermute | solution.py:30
  9.5 17.5 %collective-permute-start.3 = (bf16[4,128,256]{2,1,0:T(8,128)(2,1)S(1)}, bf16[4,128,256]{2,1,0:T(8,128)(2,1)S(1)}, u32[]{:S(2)}, u32[]{:S(2)}) collective-permute-start(bf16[4,128,256]{2,1,0:T(8,128)(2,1)S(1)} %get-tuple-element.43), channel_id=1, source_target_pairs={{0,28},{4,0},{8,4},{12,8},{16,12},{20,16},{24,20},{28,24},{1,29},{... | collective-permute-start | bytes 786440 | tf_op jit(solution)/shard_map/ppermute | solution.py:25
  33.2 28.0 %collective-permute-start.6 = (bf16[2048,256]{1,0:T(8,128)(2,1)S(1)}, bf16[2048,256]{1,0:T(8,128)(2,1)S(1)}, u32[]{:S(2)}, u32[]{:S(2)}) collective-permute-start(bf16[2048,256]{1,0:T(8,128)(2,1)S(1)} %collective-permute-done.5.refs_0_), channel_id=1, source_target_pairs={{0,1},{1,0},{2,3},{3,2},{4,5},{5,4},{6,7},{7,6},{8,9},{9,8},{10,11... | collective-permute-start | bytes 3145736 | tf_op jit(solution)/shard_map/ppermute | solution.py:30
  40.5 20.7 %collective-permute-start.2 = (bf16[4,128,256]{2,1,0:T(8,128)(2,1)S(1)}, bf16[4,128,256]{2,1,0:T(8,128)(2,1)S(1)}, u32[]{:S(2)}, u32[]{:S(2)}) collective-permute-start(bf16[4,128,256]{2,1,0:T(8,128)(2,1)S(1)} %get-tuple-element.42), channel_id=1, source_target_pairs={{0,4},{4,8},{8,12},{12,16},{16,20},{20,24},{24,28},{28,0},{1,5},{5... | collective-permute-start | bytes 786440 | tf_op jit(solution)/shard_map/ppermute | solution.py:25
  43.2 43.1 %collective-permute-start.7 = (bf16[4,128,256]{2,1,0:T(8,128)(2,1)S(1)}, bf16[4,128,256]{2,1,0:T(8,128)(2,1)S(1)}, u32[]{:S(2)}, u32[]{:S(2)}) collective-permute-start(bf16[4,128,256]{2,1,0:T(8,128)(2,1)S(1)} %attend.7), channel_id=1, source_target_pairs={{0,28},{4,0},{8,4},{12,8},{16,12},{20,16},{24,20},{28,24},{1,29},{... | collective-permute-start | bytes 786440 | tf_op jit(solution)/shard_map/ppermute | solution.py:25
  46.3 40.0 %collective-permute-start.9 = (bf16[4,128,256]{2,1,0:T(8,128)(2,1)S(1)}, bf16[4,128,256]{2,1,0:T(8,128)(2,1)S(1)}, u32[]{:S(2)}, u32[]{:S(2)}) collective-permute-start(bf16[4,128,256]{2,1,0:T(8,128)(2,1)S(1)} %attend.8), channel_id=1, source_target_pairs={{0,4},{4,8},{8,12},{12,16},{16,20},{20,24},{24,28},{28,0},{1,5},{5... | collective-permute-start | bytes 786440 | tf_op jit(solution)/shard_map/ppermute | solution.py:25
  46.3 22.2 %collective-permute-start.1 = (bf16[4,128,256]{2,1,0:T(8,128)(2,1)S(1)}, bf16[4,128,256]{2,1,0:T(8,128)(2,1)S(1)}, u32[]{:S(2)}, u32[]{:S(2)}) collective-permute-start(bf16[4,128,256]{2,1,0:T(8,128)(2,1)S(1)} %get-tuple-element.41), channel_id=1, source_target_pairs={{0,28},{4,0},{8,4},{12,8},{16,12},{20,16},{24,20},{28,24},{1,29},{... | collective-permute-start | bytes 786440 | tf_op jit(solution)/shard_map/ppermute | solution.py:25
  74.5 16.7 %collective-permute-start.10 = (bf16[4,128,256]{2,1,0:T(8,128)(2,1)S(1)}, bf16[4,128,256]{2,1,0:T(8,128)(2,1)S(1)}, u32[]{:S(2)}, u32[]{:S(2)}) collective-permute-start(bf16[4,128,256]{2,1,0:T(8,128)(2,1)S(1)} %attend.10), channel_id=1, source_target_pairs={{0,4},{4,8},{8,12},{12,16},{16,20},{20,24},{24,28},{28,0},{1,5},{5... | collective-permute-start | bytes 786440 | tf_op jit(solution)/shard_map/ppermute | solution.py:25
  77.0 12.7 %collective-permute-start.8 = (bf16[4,128,256]{2,1,0:T(8,128)(2,1)S(1)}, bf16[4,128,256]{2,1,0:T(8,128)(2,1)S(1)}, u32[]{:S(2)}, u32[]{:S(2)}) collective-permute-start(bf16[4,128,256]{2,1,0:T(8,128)(2,1)S(1)} %attend.9), channel_id=1, source_target_pairs={{0,28},{4,0},{8,4},{12,8},{16,12},{20,16},{24,20},{28,24},{1,29},{... | collective-permute-start | bytes 786440 | tf_op jit(solution)/shard_map/ppermute | solution.py:25
  86.3 4.9 %copy-start.4 = (bf16[256,256]{1,0:T(8,128)(2,1)S(1)}, bf16[256,256]{1,0:T(8,128)(2,1)}, u32[]{:S(2)}) copy-start(bf16[256,256]{1,0:T(8,128)(2,1)} %weight_ref.1) | copy-start | bytes 393220

commit v5 on v4

--- a/solution.py
+++ b/solution.py
@@ -20,9 +20,9 @@
     return pltpu.CompilerParams(vmem_limit_bytes=VMEM_BYTES)
 
 
-def shifted(block, axis, distance):
-    count = lax.axis_size(axis)
-    return lax.ppermute(block, axis, [(i, (i + distance) % count) for i in range(count)])
+def exchanged(block, side):
+    count = lax.axis_size("sector")
+    return lax.ppermute(block, "sector", [(i, (((i + side) ^ 1) - side) % count) for i in range(count)])
 
 
 def swapped(block, axis, bit):
@@ -276,7 +276,10 @@
     staged = bands == 4 and local_rows == 2 * keys
 
     shift = (lax.axis_index("band") * local_rows // keys) * CAP
-    codes = jnp.where(live != 0, visible ^ shift, -1).transpose(2, 0, 1).reshape(entries, count)
+    span = BLK_DEV * CAP
+    turned = visible + (2 - 2 * lax.div(visible, span)) * span
+    named = jnp.where(lax.axis_index("sector") % 2 == 1, turned, visible)
+    codes = jnp.where(live != 0, named ^ shift, -1).transpose(2, 0, 1).reshape(entries, count)
     rows_in = queries.reshape(count, width)
 
     if staged:
@@ -295,8 +298,8 @@
     projected, *ready = project(codes, rows_in, norm_gain.reshape(1, width), w_query, blocks)
 
     def send(lower, upper):
-        lower = shifted(lower, "sector", 1)
-        return lower, shifted(upper, "sector", -1)
+        lower = exchanged(lower, 0)
+        return lower, exchanged(upper, 1)
 
     visits = [send(*ready)]
     projected, *_ = lax.optimization_barrier((projected, *ready))
@@ -311,25 +314,27 @@
     for part, (lower, upper) in enumerate(visits):
         if part:
             kvs.append(keys_and_values([across, beyond], w_key, w_value, keys))
-        lower, last = lax.optimization_barrier((lower, last))
-        lower = attend(lower, kvs[part])
-        upper, lower = lax.optimization_barrier((upper, lower))
-        upper = attend(upper, kvs[part])
+        arrived = {"lower": lower, "upper": upper}
+        turns = ("upper", "lower") if part else ("lower", "upper")
+        for name in turns:
+            rows, last = lax.optimization_barrier((arrived[name], last))
+            last = arrived[name] = attend(rows, kvs[part])
+            if staged and part == 0 and name == turns[0]:
+                across, last = lax.optimization_barrier((across, last))
+                beyond = swapped(across, "band", 1)
         if staged and not part:
-            lower, upper, across = lax.optimization_barrier((lower, upper, across))
-            beyond = swapped(across, "band", 1)
-        lower = shifted(lower, "sector", -1)
-        last = upper
-        upper = shifted(upper, "sector", 1)
-        back.append((lower, upper))
+            arrived = dict(zip(arrived, lax.optimization_barrier(tuple(arrived.values()))))
+        for side, name in enumerate(("lower", "upper")):
+            arrived[name] = exchanged(arrived[name], side)
+        back.append((arrived["lower"], arrived["upper"]))
     if staged:
         turn, last = lax.optimization_barrier((slots_own, last))
         own.append(attend(turn, kvs[1], blocks))
 
     cuts = [i * blocks * CAP for i in range(len(kvs))]
     early = [((1, at), rows) for at, rows in zip(cuts, own)]
-    returned = [((2, at), lower) for at, (lower, _) in zip(cuts, back)]
-    returned += [((0, at), upper) for at, (_, upper) in zip(cuts, back)]
+    returned = [((0, at), upper) for at, (_, upper) in zip(cuts, back)]
+    returned += [((2, at), lower) for at, (lower, _) in zip(cuts, back)]
     early += returned[:-1]
     partial = partial_sum(selected, [rows for _, rows in early], tuple(at for at, _ in early))
     late = returned[-1:]

time: 93.3 us -> 88.7 us (0.951)
  starting transfers between devices: 24.4 us -> 18.3 us
    ppermute x8, starting transfers between devices: 22.3 us -> 15.1 us  [exchanged(): lax.ppermute(block, 'sector', [(i, ((i + side ^ 1) - side) % count) for i...]
    ppermute x3, starting transfers between devices: 2.08 us -> 3.21 us  [swapped(): return lax.ppermute(block, axis, [(i, i ^ bit) for i in range(count)])]
    ppermute x8, waiting for transfers between devices: 20.5 us -> 21.4 us  [exchanged(): lax.ppermute(block, 'sector', [(i, ((i + side ^ 1) - side) % count) for i...]
  transfers between devices with their start and end apart: 11 -> 11, of which waited for: 5 -> 4; matrix products, arithmetic and copies ran while one was open for 1% -> 1% of each run, Pallas kernels for 48% -> 52%
where the time goes in v5:
time: 88.7 us; the launch traced here: 88.6 us
  Pallas kernels  47.7 us (54%)
  waiting for transfers between devices  21.5 us (24%)
  starting transfers between devices  18.3 us (21%)
    pallas_call x6, Pallas kernels, attend(): pl.pallas_call(functools.partial(attend_kernel, stack=stack, start=start)...  36.4 us
    ppermute x8, waiting for transfers between devices, exchanged(): lax.ppermute(block, 'sector', [(i, ((i + side ^ 1) - side) % count) for i...  21.4 us
    ppermute x8, starting transfers between devices, exchanged(): lax.ppermute(block, 'sector', [(i, ((i + side ^ 1) - side) % count) for i...  15.1 us
    ppermute x3, starting transfers between devices, swapped(): return lax.ppermute(block, axis, [(i, i ^ bit) for i in range(count)])  3.21 us
    pallas_call x2, Pallas kernels, keys_and_values(): pl.pallas_call(kv_kernel, out_shape=jax.ShapeDtypeStruct((count // keys,...  2.51 us
    pallas_call x1, Pallas kernels, picks(): pl.pallas_call(functools.partial(pick_kernel, groups=groups), out_shape=(...  2.5 us
    pallas_call x1, Pallas kernels, finish(): pl.pallas_call(functools.partial(final_kernel, places=places), out_shape=...  1.97 us
  transfers between devices with their start and end apart: 11, of which 4 were waited for; matrix products, arithmetic and copies ran while one was open for 1% of the time, Pallas kernels for 52%

profile of v5, /device:TPU:0, one launch (start us, length us, event | category | flops | bytes accessed | tf_op | source)
XLA Modules:
  0.0 88.6 jit_solution(11261020030552606200)
XLA Ops:
  0.0 0.6 collective-permute-start
  0.6 2.6 %collective-permute-start.4 = (bf16[2048,256]{1,0:T(8,128)(2,1)}, bf16[2048,256]{1,0:T(8,128)(2,1)S(1)}, u32[]{:S(2)}, u32[]{:S(2)}) collective-permute-start(bf16[2048,256]{1,0:T(8,128)(2,1)} %refs_0_.1), channel_id=1, source_target_pairs={{0,2},{1,3},{2,0},{3,1},{4,6},{5,7},{6,4},{7,5},{8,10},{9,11},{10,... | collective-permute-start | bytes 3145736 | tf_op jit(solution)/shard_map/ppermute | solution.py:30
  3.2 0.8 fusion.6
  3.9 0.1 reshape.12.codes_ref
  4.0 2.5 %picks.1 = (bf16[1024,1024]{1,0:T(8,128)(2,1)S(1)}, bf16[1024,1024]{1,0:T(8,128)(2,1)S(1)}, bf16[1024,1024]{1,0:T(8,128)(2,1)S(1)}) custom-call(s32[3,1024]{1,0:T(4,128)S(1)} %reshape.12.codes_ref), custom_call_target="tpu_custom_call" | custom-call | flops 1073741824 | bytes 2097152 | tf_op jit(solution)/shard_map/picks/pallas_call | solution.py:211
  6.5 0.0 copy-start
  6.6 0.0 copy-start.2
  6.6 0.0 copy-start.3
  6.6 1.5 %project.1 = (bf16[1024,256]{1,0:T(8,128)(2,1)S(1)}, bf16[4,128,256]{2,1,0:T(8,128)(2,1)S(1)}, bf16[4,128,256]{2,1,0:T(8,128)(2,1)S(1)}) custom-call(s32[3,1024]{1,0:T(4,128)S(1)} %reshape.12.codes_ref, bf16[1024,256]{1,0:T(8,128)(2,1)S(1)} %bitcast.5, f32[1,256]{1,0:T(1,128)S(1)} %bitcast.7, bf16[256,256]{1,0:T(8,128)(2,1)S(1)} %copy-done.5), custom_call_target="tpu_custom_call" | custom-call | flops 4294967296 | bytes 2097152 | tf_op jit(solution)/shard_map/project/pallas_call | solution.py:75
  8.1 1.6 %collective-permute-start.5 = (bf16[4,128,256]{2,1,0:T(8,128)(2,1)S(1)}, bf16[4,128,256]{2,1,0:T(8,128)(2,1)S(1)}, u32[]{:S(2)}, u32[]{:S(2)}) collective-permute-start(bf16[4,128,256]{2,1,0:T(8,128)(2,1)S(1)} %get-tuple-element.42), channel_id=1, source_target_pairs={{0,4},{4,0},{8,12},{12,8},{16,20},{20,16},{24,28},{28,24},{1,5},{5... | collective-permute-start | bytes 786440 | tf_op jit(solution)/shard_map/ppermute | solution.py:25
  9.7 3.6 %collective-permute-start.3 = (bf16[4,128,256]{2,1,0:T(8,128)(2,1)S(1)}, bf16[4,128,256]{2,1,0:T(8,128)(2,1)S(1)}, u32[]{:S(2)}, u32[]{:S(2)}) collective-permute-start(bf16[4,128,256]{2,1,0:T(8,128)(2,1)S(1)} %get-tuple-element.40), channel_id=1, source_target_pairs={{0,28},{4,8},{8,4},{12,16},{16,12},{20,24},{24,20},{28,0},{1,29},{... | collective-permute-start | bytes 786440 | tf_op jit(solution)/shard_map/ppermute | solution.py:25
  13.3 8.9 %collective-permute-done.5.rows_ref = bf16[4,128,256]{2,1,0:T(8,128)(2,1)S(1)} collective-permute-done((bf16[4,128,256]{2,1,0:T(8,128)(2,1)S(1)}, bf16[4,128,256]{2,1,0:T(8,128)(2,1)S(1)}, u32[]{:S(2)}, u32[]{:S(2)}) %collective-permute-start.5) | collective-permute-done | bytes 262176 | tf_op jit(solution)/shard_map/ppermute | solution.py:25
  22.2 1.3 %keys_and_values.2.kv_ref = bf16[4,1024,512]{2,1,0:T(8,128)(2,1)S(1)} custom-call(bf16[256,256]{1,0:T(8,128)(2,1)S(1)} %copy-done.2, bf16[256,256]{1,0:T(8,128)(2,1)S(1)} %copy-done.3, bf16[2048,256]{1,0:T(8,128)(2,1)S(1)} %copy-done, bf16[2048,256]{1,0:T(8,128)(2,1)S(1)} %collective-permute-done.refs_1_), custom_call_target="tpu_custom_call" | custom-call | flops 1073741824 | bytes 6291456 | tf_op jit(solution)/shard_map/keys_and_values/pallas_call | solution.py:126
  23.5 6.0 %attend.8 = bf16[4,128,256]{2,1,0:T(8,128)(2,1)S(1)} custom-call(bf16[4,128,256]{2,1,0:T(8,128)(2,1)S(1)} %collective-permute-done.5.rows_ref, bf16[4,1024,512]{2,1,0:T(8,128)(2,1)S(1)} %keys_and_values.2.kv_ref), custom_call_target="tpu_custom_call" | custom-call | flops 4294967296 | bytes 4194304 | tf_op jit(solution)/shard_map/attend/pallas_call | solution.py:181
  29.5 0.1 collective-permute-start.6
  29.5 1.3 %scatter.1 = (bf16[8,128,256]{2,1,0:T(8,128)(2,1)S(1)}, bf16[4,128,256]{2,1,0:T(8,128)(2,1)S(1)}, bf16[4,128,256]{2,1,0:T(8,128)(2,1)S(1)}) custom-call(s32[3,1024]{1,0:T(4,128)S(1)} %reshape.12.codes_ref, bf16[1024,256]{1,0:T(8,128)(2,1)S(1)} %get-tuple-element.34.rows_ref), custom_call_target="tpu_custom_call" | custom-call | flops 1073741824 | bytes 2097152 | tf_op jit(solution)/shard_map/scatter/pallas_call | solution.py:101
  30.8 6.0 %attend.6.refs_3_ = bf16[4,128,256]{2,1,0:T(8,128)(2,1)S(1)} custom-call(bf16[8,128,256]{2,1,0:T(8,128)(2,1)S(1)} %get-tuple-element.45.rows_ref, bf16[4,1024,512]{2,1,0:T(8,128)(2,1)S(1)} %keys_and_values.2.kv_ref), custom_call_target="tpu_custom_call" | custom-call | flops 4294967296 | bytes 4194304 | tf_op jit(solution)/shard_map/attend/pallas_call | solution.py:181
  36.8 4.6 %collective-permute-start.2 = (bf16[4,128,256]{2,1,0:T(8,128)(2,1)S(1)}, bf16[4,128,256]{2,1,0:T(8,128)(2,1)S(1)}, u32[]{:S(2)}, u32[]{:S(2)}) collective-permute-start(bf16[4,128,256]{2,1,0:T(8,128)(2,1)S(1)} %get-tuple-element.39), channel_id=1, source_target_pairs={{0,28},{4,8},{8,4},{12,16},{16,12},{20,24},{24,20},{28,0},{1,29},{... | collective-permute-start | bytes 786440 | tf_op jit(solution)/shard_map/ppermute | solution.py:25
  41.4 6.2 %attend.7 = bf16[4,128,256]{2,1,0:T(8,128)(2,1)S(1)} custom-call(bf16[4,128,256]{2,1,0:T(8,128)(2,1)S(1)} %collective-permute-done.3.rows_ref, bf16[4,1024,512]{2,1,0:T(8,128)(2,1)S(1)} %keys_and_values.2.kv_ref), custom_call_target="tpu_custom_call" | custom-call | flops 4294967296 | bytes 4194304 | tf_op jit(solution)/shard_map/attend/pallas_call | solution.py:181
  47.6 0.3 collective-permute-start.7
  47.9 2.0 %collective-permute-start.1 = (bf16[4,128,256]{2,1,0:T(8,128)(2,1)S(1)}, bf16[4,128,256]{2,1,0:T(8,128)(2,1)S(1)}, u32[]{:S(2)}, u32[]{:S(2)}) collective-permute-start(bf16[4,128,256]{2,1,0:T(8,128)(2,1)S(1)} %get-tuple-element.38), channel_id=1, source_target_pairs={{0,4},{4,0},{8,12},{12,8},{16,20},{20,16},{24,28},{28,24},{1,5},{5... | collective-permute-start | bytes 786440 | tf_op jit(solution)/shard_map/ppermute | solution.py:25
  49.9 1.3 %keys_and_values.3.kv_ref = bf16[4,1024,512]{2,1,0:T(8,128)(2,1)S(1)} custom-call(bf16[256,256]{1,0:T(8,128)(2,1)S(1)} %copy-done.2, bf16[256,256]{1,0:T(8,128)(2,1)S(1)} %copy-done.3, bf16[2048,256]{1,0:T(8,128)(2,1)S(1)} %collective-permute-done.4.refs_0_, bf16[2048,256]{1,0:T(8,128)(2,1)S(1)} %collective-permute-done.6.refs_1_), custom_call_target="tpu_custom_call" | custom-call | flops 1073741824 | bytes 6291456 | tf_op jit(solution)/shard_map/keys_and_values/pallas_call | solution.py:126
  51.2 6.0 %attend.9 = bf16[4,128,256]{2,1,0:T(8,128)(2,1)S(1)} custom-call(bf16[4,128,256]{2,1,0:T(8,128)(2,1)S(1)} %collective-permute-done.2.rows_ref, bf16[4,1024,512]{2,1,0:T(8,128)(2,1)S(1)} %keys_and_values.3.kv_ref), custom_call_target="tpu_custom_call" | custom-call | flops 4294967296 | bytes 4194304 | tf_op jit(solution)/shard_map/attend/pallas_call | solution.py:181
  57.2 10.2 %collective-permute-done.1.rows_ref = bf16[4,128,256]{2,1,0:T(8,128)(2,1)S(1)} collective-permute-done((bf16[4,128,256]{2,1,0:T(8,128)(2,1)S(1)}, bf16[4,128,256]{2,1,0:T(8,128)(2,1)S(1)}, u32[]{:S(2)}, u32[]{:S(2)}) %collective-permute-start.1) | collective-permute-done | bytes 262176 | tf_op jit(solution)/shard_map/ppermute | solution.py:25
  67.4 6.0 %attend.10 = bf16[4,128,256]{2,1,0:T(8,128)(2,1)S(1)} custom-call(bf16[4,128,256]{2,1,0:T(8,128)(2,1)S(1)} %collective-permute-done.1.rows_ref, bf16[4,1024,512]{2,1,0:T(8,128)(2,1)S(1)} %keys_and_values.3.kv_ref), custom_call_target="tpu_custom_call" | custom-call | flops 4294967296 | bytes 4194304 | tf_op jit(solution)/shard_map/attend/pallas_call | solution.py:181
  73.4 0.1 collective-permute-start.10
  73.5 3.0 %collective-permute-start.8 = (bf16[4,128,256]{2,1,0:T(8,128)(2,1)S(1)}, bf16[4,128,256]{2,1,0:T(8,128)(2,1)S(1)}, u32[]{:S(2)}, u32[]{:S(2)}) collective-permute-start(bf16[4,128,256]{2,1,0:T(8,128)(2,1)S(1)} %attend.9), channel_id=1, source_target_pairs={{0,28},{4,8},{8,4},{12,16},{16,12},{20,24},{24,20},{28,0},{1,29},{... | collective-permute-start | bytes 786440 | tf_op jit(solution)/shard_map/ppermute | solution.py:25
  76.5 6.2 %attend.11.refs_4_ = bf16[4,128,256]{2,1,0:T(8,128)(2,1)S(1)} custom-call(bf16[8,128,256]{2,1,0:T(8,128)(2,1)S(1)} %get-tuple-element.45.rows_ref, bf16[4,1024,512]{2,1,0:T(8,128)(2,1)S(1)} %keys_and_values.3.kv_ref), custom_call_target="tpu_custom_call" | custom-call | flops 4294967296 | bytes 4194304 | tf_op jit(solution)/shard_map/attend/pallas_call | solution.py:181
  82.8 1.1 %collective-permute-done.8.refs_6_ = bf16[4,128,256]{2,1,0:T(8,128)(2,1)S(1)} collective-permute-done((bf16[4,128,256]{2,1,0:T(8,128)(2,1)S(1)}, bf16[4,128,256]{2,1,0:T(8,128)(2,1)S(1)}, u32[]{:S(2)}, u32[]{:S(2)}) %collective-permute-start.8) | collective-permute-done | bytes 262176 | tf_op jit(solution)/shard_map/ppermute | solution.py:25
  83.8 1.5 %partial_sum.1.partial_ref = f32[1024,256]{1,0:T(8,128)S(1)} custom-call(bf16[1024,1024]{1,0:T(8,128)(2,1)S(1)} %get-tuple-element.30.refs_0_, bf16[1024,1024]{1,0:T(8,128)(2,1)S(1)} %get-tuple-element.31.refs_1_, bf16[1024,1024]{1,0:T(8,128)(2,1)S(1)} %get-tuple-element.32.refs_2_, bf16[4,128,256]{2,1,0:T(8,128)(2,1)S(1)} %attend.6.refs_3_, ...), custom_call_target="tpu_custom_call" | custom-call | flops 1073741824 | bytes 2097152 | tf_op jit(solution)/shard_map/partial_sum/pallas_call | solution.py:240
  85.4 1.2 %collective-permute-done.10.refs_3_ = bf16[4,128,256]{2,1,0:T(8,128)(2,1)S(1)} collective-permute-done((bf16[4,128,256]{2,1,0:T(8,128)(2,1)S(1)}, bf16[4,128,256]{2,1,0:T(8,128)(2,1)S(1)}, u32[]{:S(2)}, u32[]{:S(2)}) %collective-permute-start.10) | collective-permute-done | bytes 262176 | tf_op jit(solution)/shard_map/ppermute | solution.py:25
  86.6 2.0 %finish.1 = bf16[1024,256]{1,0:T(8,128)(2,1)} custom-call(f32[1024,256]{1,0:T(8,128)S(1)} %partial_sum.1.partial_ref, bf16[1024,256]{1,0:T(8,128)(2,1)S(1)} %bitcast.6, bf16[256,256]{1,0:T(8,128)(2,1)S(1)} %copy-done.4, bf16[1024,1024]{1,0:T(8,128)(2,1)S(1)} %get-tuple-element.30.refs_0_, bf16[1024,1024]{1,0:T(8,128)(2,1)S(1)} %get-tuple-element.31.refs_1_, ...), custom_call_target="tpu_custom_call" | custom-call | flops 1073741824 | bytes 2097152 | tf_op jit(solution)/shard_map/finish/pallas_call | solution.py:260
  (19 shorter events, 0.0 us)
Async XLA Ops:
  0.0 6.5 %copy-start.5 = (bf16[256,256]{1,0:T(8,128)(2,1)S(1)}, bf16[256,256]{1,0:T(8,128)(2,1)}, u32[]{:S(2)}) copy-start(bf16[256,256]{1,0:T(8,128)(2,1)} %weight_hbm.1) | copy-start | bytes 393220
  0.0 6.5 %copy-start.6 = (f32[256]{0:T(256)S(1)}, f32[256]{0:T(256)}, u32[]{:S(2)}) copy-start(f32[256]{0:T(256)} %param.10) | copy-start | bytes 3076
  0.0 6.5 %copy-start.1 = (bf16[16,64,256]{2,1,0:T(8,128)(2,1)S(1)}, bf16[16,64,256]{2,1,0:T(8,128)(2,1)}, u32[]{:S(2)}) copy-start(bf16[16,64,256]{2,1,0:T(8,128)(2,1)} %param.9) | copy-start | bytes 1572868
  0.0 22.2 %collective-permute-start = (bf16[2048,256]{1,0:T(8,128)(2,1)}, bf16[2048,256]{1,0:T(8,128)(2,1)S(1)}, u32[]{:S(2)}, u32[]{:S(2)}) collective-permute-start(bf16[2048,256]{1,0:T(8,128)(2,1)} %refs_0_.1), channel_id=1, source_target_pairs={{0,1},{1,0},{2,3},{3,2},{4,5},{5,4},{6,7},{7,6},{8,9},{9,8},{10,11... | collective-permute-start | bytes 3145736 | tf_op jit(solution)/shard_map/ppermute | solution.py:30
  0.6 28.9 %collective-permute-start.4 = (bf16[2048,256]{1,0:T(8,128)(2,1)}, bf16[2048,256]{1,0:T(8,128)(2,1)S(1)}, u32[]{:S(2)}, u32[]{:S(2)}) collective-permute-start(bf16[2048,256]{1,0:T(8,128)(2,1)} %refs_0_.1), channel_id=1, source_target_pairs={{0,2},{1,3},{2,0},{3,1},{4,6},{5,7},{6,4},{7,5},{8,10},{9,11},{10,... | collective-permute-start | bytes 3145736 | tf_op jit(solution)/shard_map/ppermute | solution.py:30
  6.5 15.6 %copy-start = (bf16[2048,256]{1,0:T(8,128)(2,1)S(1)}, bf16[2048,256]{1,0:T(8,128)(2,1)}, u32[]{:S(2)}) copy-start(bf16[2048,256]{1,0:T(8,128)(2,1)} %refs_0_.1) | copy-start | bytes 3145732
  6.6 15.6 %copy-start.2 = (bf16[256,256]{1,0:T(8,128)(2,1)S(1)}, bf16[256,256]{1,0:T(8,128)(2,1)}, u32[]{:S(2)}) copy-start(bf16[256,256]{1,0:T(8,128)(2,1)} %key_ref.3) | copy-start | bytes 393220
  6.6 15.6 %copy-start.3 = (bf16[256,256]{1,0:T(8,128)(2,1)S(1)}, bf16[256,256]{1,0:T(8,128)(2,1)}, u32[]{:S(2)}) copy-start(bf16[256,256]{1,0:T(8,128)(2,1)} %value_ref.3) | copy-start | bytes 393220
  8.1 14.0 %collective-permute-start.5 = (bf16[4,128,256]{2,1,0:T(8,128)(2,1)S(1)}, bf16[4,128,256]{2,1,0:T(8,128)(2,1)S(1)}, u32[]{:S(2)}, u32[]{:S(2)}) collective-permute-start(bf16[4,128,256]{2,1,0:T(8,128)(2,1)S(1)} %get-tuple-element.42), channel_id=1, source_target_pairs={{0,4},{4,0},{8,12},{12,8},{16,20},{20,16},{24,28},{28,24},{1,5},{5... | collective-permute-start | bytes 786440 | tf_op jit(solution)/shard_map/ppermute | solution.py:25
  9.7 21.1 %collective-permute-start.3 = (bf16[4,128,256]{2,1,0:T(8,128)(2,1)S(1)}, bf16[4,128,256]{2,1,0:T(8,128)(2,1)S(1)}, u32[]{:S(2)}, u32[]{:S(2)}) collective-permute-start(bf16[4,128,256]{2,1,0:T(8,128)(2,1)S(1)} %get-tuple-element.40), channel_id=1, source_target_pairs={{0,28},{4,8},{8,4},{12,16},{16,12},{20,24},{24,20},{28,0},{1,29},{... | collective-permute-start | bytes 786440 | tf_op jit(solution)/shard_map/ppermute | solution.py:25
  29.5 20.5 %collective-permute-start.6 = (bf16[2048,256]{1,0:T(8,128)(2,1)S(1)}, bf16[2048,256]{1,0:T(8,128)(2,1)S(1)}, u32[]{:S(2)}, u32[]{:S(2)}) collective-permute-start(bf16[2048,256]{1,0:T(8,128)(2,1)S(1)} %collective-permute-done.4.refs_0_), channel_id=1, source_target_pairs={{0,1},{1,0},{2,3},{3,2},{4,5},{5,4},{6,7},{7,6},{8,9},{9,8},{10,11... | collective-permute-start | bytes 3145736 | tf_op jit(solution)/shard_map/ppermute | solution.py:30
  36.8 13.1 %collective-permute-start.2 = (bf16[4,128,256]{2,1,0:T(8,128)(2,1)S(1)}, bf16[4,128,256]{2,1,0:T(8,128)(2,1)S(1)}, u32[]{:S(2)}, u32[]{:S(2)}) collective-permute-start(bf16[4,128,256]{2,1,0:T(8,128)(2,1)S(1)} %get-tuple-element.39), channel_id=1, source_target_pairs={{0,28},{4,8},{8,4},{12,16},{16,12},{20,24},{24,20},{28,0},{1,29},{... | collective-permute-start | bytes 786440 | tf_op jit(solution)/shard_map/ppermute | solution.py:25
  47.6 35.1 %collective-permute-start.7 = (bf16[4,128,256]{2,1,0:T(8,128)(2,1)S(1)}, bf16[4,128,256]{2,1,0:T(8,128)(2,1)S(1)}, u32[]{:S(2)}, u32[]{:S(2)}) collective-permute-start(bf16[4,128,256]{2,1,0:T(8,128)(2,1)S(1)} %attend.7), channel_id=1, source_target_pairs={{0,28},{4,8},{8,4},{12,16},{16,12},{20,24},{24,20},{28,0},{1,29},{... | collective-permute-start | bytes 786440 | tf_op jit(solution)/shard_map/ppermute | solution.py:25
  47.9 34.9 %collective-permute-start.9 = (bf16[4,128,256]{2,1,0:T(8,128)(2,1)S(1)}, bf16[4,128,256]{2,1,0:T(8,128)(2,1)S(1)}, u32[]{:S(2)}, u32[]{:S(2)}) collective-permute-start(bf16[4,128,256]{2,1,0:T(8,128)(2,1)S(1)} %attend.8), channel_id=1, source_target_pairs={{0,4},{4,0},{8,12},{12,8},{16,20},{20,16},{24,28},{28,24},{1,5},{5... | collective-permute-start | bytes 786440 | tf_op jit(solution)/shard_map/ppermute | solution.py:25
  47.9 19.5 %collective-permute-start.1 = (bf16[4,128,256]{2,1,0:T(8,128)(2,1)S(1)}, bf16[4,128,256]{2,1,0:T(8,128)(2,1)S(1)}, u32[]{:S(2)}, u32[]{:S(2)}) collective-permute-start(bf16[4,128,256]{2,1,0:T(8,128)(2,1)S(1)} %get-tuple-element.38), channel_id=1, source_target_pairs={{0,4},{4,0},{8,12},{12,8},{16,20},{20,16},{24,28},{28,24},{1,5},{5... | collective-permute-start | bytes 786440 | tf_op jit(solution)/shard_map/ppermute | solution.py:25
  73.4 13.1 %collective-permute-start.10 = (bf16[4,128,256]{2,1,0:T(8,128)(2,1)S(1)}, bf16[4,128,256]{2,1,0:T(8,128)(2,1)S(1)}, u32[]{:S(2)}, u32[]{:S(2)}) collective-permute-start(bf16[4,128,256]{2,1,0:T(8,128)(2,1)S(1)} %attend.10), channel_id=1, source_target_pairs={{0,4},{4,0},{8,12},{12,8},{16,20},{20,16},{24,28},{28,24},{1,5},{5... | collective-permute-start | bytes 786440 | tf_op jit(solution)/shard_map/ppermute | solution.py:25
  73.5 10.3 %collective-permute-start.8 = (bf16[4,128,256]{2,1,0:T(8,128)(2,1)S(1)}, bf16[4,128,256]{2,1,0:T(8,128)(2,1)S(1)}, u32[]{:S(2)}, u32[]{:S(2)}) collective-permute-start(bf16[4,128,256]{2,1,0:T(8,128)(2,1)S(1)} %attend.9), channel_id=1, source_target_pairs={{0,28},{4,8},{8,4},{12,16},{16,12},{20,24},{24,20},{28,0},{1,29},{... | collective-permute-start | bytes 786440 | tf_op jit(solution)/shard_map/ppermute | solution.py:25
  82.7 3.8 %copy-start.4 = (bf16[256,256]{1,0:T(8,128)(2,1)S(1)}, bf16[256,256]{1,0:T(8,128)(2,1)}, u32[]{:S(2)}) copy-start(bf16[256,256]{1,0:T(8,128)(2,1)} %weight_ref.1) | copy-start | bytes 393220

commit v6 on v5

--- a/solution.py
+++ b/solution.py
@@ -81,7 +81,11 @@
             pltpu.VMEM(weight.shape, weight.dtype),
             pltpu.SemaphoreType.DMA((3,)),
         ],
-        out_shape=(jax.ShapeDtypeStruct((count, width), jnp.bfloat16),) + (slot_shape(blocks, width),) * 2,
+        out_shape=(
+            jax.ShapeDtypeStruct((count, width), jnp.bfloat16),
+            slot_shape(blocks, width),
+            slot_shape(BLK_DEV, width),
+        ),
         compiler_params=params(),
         cost_estimate=pl.CostEstimate(flops=4 << 30, bytes_accessed=2 << 20, transcendentals=0),
         name="project",
@@ -90,8 +94,8 @@
 
 def scatter_kernel(codes_ref, rows_ref, own_ref, *refs, blocks):
     rows = rows_ref[...]
-    for ref, first in zip(refs, (2 * BLK_DEV + blocks, blocks)):
-        fill_slots(codes_ref, rows, ref, first)
+    for ref in refs:
+        fill_slots(codes_ref, rows, ref, 2 * BLK_DEV + blocks)
     fill_slots(codes_ref, rows, own_ref, BLK_DEV)
 
 
@@ -100,7 +104,7 @@
     rest = BLK_DEV - blocks
     return pl.pallas_call(
         functools.partial(scatter_kernel, blocks=blocks),
-        out_shape=(slot_shape(BLK_DEV, width),) + ((slot_shape(rest, width),) * 2 if rest else ()),
+        out_shape=(slot_shape(BLK_DEV, width),) + ((slot_shape(rest, width),) if rest else ()),
         compiler_params=params(),
         cost_estimate=pl.CostEstimate(flops=1 << 30, bytes_accessed=2 << 20, transcendentals=0),
         name="scatter",
@@ -297,11 +301,8 @@
     blocks = BLK_DEV // 2 if staged else BLK_DEV
     projected, *ready = project(codes, rows_in, norm_gain.reshape(1, width), w_query, blocks)
 
-    def send(lower, upper):
-        lower = exchanged(lower, 0)
-        return lower, exchanged(upper, 1)
-
-    visits = [send(*ready)]
+    lowers = [exchanged(ready[0], 0)]
+    upper = exchanged(ready[1], 1)
     projected, *_ = lax.optimization_barrier((projected, *ready))
     slots_own, *ready = scatter(codes, projected, blocks)
     kvs = [keys_and_values(held[0], w_key, w_value, keys)]
@@ -309,21 +310,21 @@
     last = own[0]
     if staged:
         *ready, last = lax.optimization_barrier((*ready, last))
-        visits.append(send(*ready))
+        lowers.append(exchanged(ready[0], 0))
     back = []
-    for part, (lower, upper) in enumerate(visits):
+    for part, lower in enumerate(lowers):
         if part:
             kvs.append(keys_and_values([across, beyond], w_key, w_value, keys))
         arrived = {"lower": lower, "upper": upper}
+        starts = {"lower": 0, "upper": part * blocks}
         turns = ("upper", "lower") if part else ("lower", "upper")
         for name in turns:
             rows, last = lax.optimization_barrier((arrived[name], last))
-            last = arrived[name] = attend(rows, kvs[part])
-            if staged and part == 0 and name == turns[0]:
-                across, last = lax.optimization_barrier((across, last))
-                beyond = swapped(across, "band", 1)
+            last = arrived[name] = attend(rows, kvs[part], starts[name])
         if staged and not part:
-            arrived = dict(zip(arrived, lax.optimization_barrier(tuple(arrived.values()))))
+            *both, across = lax.optimization_barrier((*arrived.values(), across))
+            arrived = dict(zip(arrived, both))
+            beyond = swapped(across, "band", 1)
         for side, name in enumerate(("lower", "upper")):
             arrived[name] = exchanged(arrived[name], side)
         back.append((arrived["lower"], arrived["upper"]))

time: 88.7 us -> 83.4 us (0.940)
  waiting for transfers between devices: 21.5 us -> 15.2 us
  starting transfers between devices: 18.3 us -> 19.2 us
    ppermute x8 -> x7, waiting for transfers between devices: 21.4 us -> 15.2 us  [exchanged(): lax.ppermute(block, 'sector', [(i, ((i + side ^ 1) - side) % count) for i...]
    ppermute x8 -> x7, starting transfers between devices: 15.1 us -> 17 us  [exchanged(): lax.ppermute(block, 'sector', [(i, ((i + side ^ 1) - side) % count) for i...]
    ppermute x3, starting transfers between devices: 3.21 us -> 2.15 us  [swapped(): return lax.ppermute(block, axis, [(i, i ^ bit) for i in range(count)])]
  transfers between devices with their start and end apart: 11 -> 10, of which waited for: 4 -> 2; matrix products, arithmetic and copies ran while one was open for 1% -> 1% of each run, Pallas kernels for 52% -> 55%
where the time goes in v6:
time: 83.4 us; the launch traced here: 83.2 us
  Pallas kernels  47.7 us (57%)
  starting transfers between devices  19.2 us (23%)
  waiting for transfers between devices  15.2 us (18%)
    pallas_call x6, Pallas kernels, attend(): pl.pallas_call(functools.partial(attend_kernel, stack=stack, start=start)...  36.4 us
    ppermute x7, starting transfers between devices, exchanged(): lax.ppermute(block, 'sector', [(i, ((i + side ^ 1) - side) % count) for i...  17 us
    ppermute x7, waiting for transfers between devices, exchanged(): lax.ppermute(block, 'sector', [(i, ((i + side ^ 1) - side) % count) for i...  15.2 us
    pallas_call x2, Pallas kernels, keys_and_values(): pl.pallas_call(kv_kernel, out_shape=jax.ShapeDtypeStruct((count // keys,...  2.51 us
    pallas_call x1, Pallas kernels, picks(): pl.pallas_call(functools.partial(pick_kernel, groups=groups), out_shape=(...  2.5 us
    ppermute x3, starting transfers between devices, swapped(): return lax.ppermute(block, axis, [(i, i ^ bit) for i in range(count)])  2.15 us
    pallas_call x1, Pallas kernels, finish(): pl.pallas_call(functools.partial(final_kernel, places=places), out_shape=...  1.97 us
    pallas_call x1, Pallas kernels, project(): pl.pallas_call(project_kernel, in_specs=[pl.BlockSpec(memory_space=pltpu....  1.81 us
  transfers between devices with their start and end apart: 10, of which 2 were waited for; matrix products, arithmetic and copies ran while one was open for 1% of the time, Pallas kernels for 55%

profile of v6, /device:TPU:0, one launch (start us, length us, event | category | flops | bytes accessed | tf_op | source)
XLA Modules:
  0.0 83.2 jit_solution(17763680603891765724)
XLA Ops:
  0.0 0.6 collective-permute-start
  0.6 0.8 fusion.6
  1.3 0.1 reshape.12.codes_ref
  1.4 2.5 %picks.1 = (bf16[1024,1024]{1,0:T(8,128)(2,1)S(1)}, bf16[1024,1024]{1,0:T(8,128)(2,1)S(1)}, bf16[1024,1024]{1,0:T(8,128)(2,1)S(1)}) custom-call(s32[3,1024]{1,0:T(4,128)S(1)} %reshape.12.codes_ref), custom_call_target="tpu_custom_call" | custom-call | flops 1073741824 | bytes 2097152 | tf_op jit(solution)/shard_map/picks/pallas_call | solution.py:215
  4.0 0.0 copy-start
  4.0 0.0 copy-start.2
  4.0 0.0 copy-start.3
  4.0 1.8 %project.1 = (bf16[1024,256]{1,0:T(8,128)(2,1)S(1)}, bf16[4,128,256]{2,1,0:T(8,128)(2,1)S(1)}, bf16[8,128,256]{2,1,0:T(8,128)(2,1)S(1)}) custom-call(s32[3,1024]{1,0:T(4,128)S(1)} %reshape.12.codes_ref, bf16[1024,256]{1,0:T(8,128)(2,1)S(1)} %bitcast.5, f32[1,256]{1,0:T(1,128)S(1)} %bitcast.7, bf16[256,256]{1,0:T(8,128)(2,1)S(1)} %copy-done.5), custom_call_target="tpu_custom_call" | custom-call | flops 4294967296 | bytes 2097152 | tf_op jit(solution)/shard_map/project/pallas_call | solution.py:75
  5.8 2.7 %collective-permute-start.3 = (bf16[4,128,256]{2,1,0:T(8,128)(2,1)S(1)}, bf16[4,128,256]{2,1,0:T(8,128)(2,1)S(1)}, u32[]{:S(2)}, u32[]{:S(2)}) collective-permute-start(bf16[4,128,256]{2,1,0:T(8,128)(2,1)S(1)} %get-tuple-element.38), channel_id=1, source_target_pairs={{0,4},{4,0},{8,12},{12,8},{16,20},{20,16},{24,28},{28,24},{1,5},{5... | collective-permute-start | bytes 786440 | tf_op jit(solution)/shard_map/ppermute | solution.py:25
  8.5 1.5 %collective-permute-start.4 = (bf16[2048,256]{1,0:T(8,128)(2,1)S(1)}, bf16[2048,256]{1,0:T(8,128)(2,1)S(1)}, u32[]{:S(2)}, u32[]{:S(2)}) collective-permute-start(bf16[2048,256]{1,0:T(8,128)(2,1)S(1)} %copy-done), channel_id=1, source_target_pairs={{0,2},{1,3},{2,0},{3,1},{4,6},{5,7},{6,4},{7,5},{8,10},{9,11},{10,... | collective-permute-start | bytes 3145736 | tf_op jit(solution)/shard_map/ppermute | solution.py:30
  10.0 3.6 %collective-permute-start.2 = (bf16[8,128,256]{2,1,0:T(8,128)(2,1)S(1)}, bf16[8,128,256]{2,1,0:T(8,128)(2,1)S(1)}, u32[]{:S(2)}, u32[]{:S(2)}) collective-permute-start(bf16[8,128,256]{2,1,0:T(8,128)(2,1)S(1)} %get-tuple-element.37), channel_id=1, source_target_pairs={{0,28},{4,8},{8,4},{12,16},{16,12},{20,24},{24,20},{28,0},{1,29},{... | collective-permute-start | bytes 1572872 | tf_op jit(solution)/shard_map/ppermute | solution.py:25
  13.6 13.0 %collective-permute-done.3.rows_ref = bf16[4,128,256]{2,1,0:T(8,128)(2,1)S(1)} collective-permute-done((bf16[4,128,256]{2,1,0:T(8,128)(2,1)S(1)}, bf16[4,128,256]{2,1,0:T(8,128)(2,1)S(1)}, u32[]{:S(2)}, u32[]{:S(2)}) %collective-permute-start.3) | collective-permute-done | bytes 262176 | tf_op jit(solution)/shard_map/ppermute | solution.py:25
  26.6 0.0 collective-permute-done.refs_1_
  26.6 1.3 %keys_and_values.2.kv_ref = bf16[4,1024,512]{2,1,0:T(8,128)(2,1)S(1)} custom-call(bf16[256,256]{1,0:T(8,128)(2,1)S(1)} %copy-done.2, bf16[256,256]{1,0:T(8,128)(2,1)S(1)} %copy-done.3, bf16[2048,256]{1,0:T(8,128)(2,1)S(1)} %copy-done, bf16[2048,256]{1,0:T(8,128)(2,1)S(1)} %collective-permute-done.refs_1_), custom_call_target="tpu_custom_call" | custom-call | flops 1073741824 | bytes 6291456 | tf_op jit(solution)/shard_map/keys_and_values/pallas_call | solution.py:130
  27.8 6.0 %attend.7 = bf16[4,128,256]{2,1,0:T(8,128)(2,1)S(1)} custom-call(bf16[4,128,256]{2,1,0:T(8,128)(2,1)S(1)} %collective-permute-done.3.rows_ref, bf16[4,1024,512]{2,1,0:T(8,128)(2,1)S(1)} %keys_and_values.2.kv_ref), custom_call_target="tpu_custom_call" | custom-call | flops 4294967296 | bytes 4194304 | tf_op jit(solution)/shard_map/attend/pallas_call | solution.py:185
  33.9 6.0 %attend.8 = bf16[4,128,256]{2,1,0:T(8,128)(2,1)S(1)} custom-call(bf16[8,128,256]{2,1,0:T(8,128)(2,1)S(1)} %collective-permute-done.2.rows_ref, bf16[4,1024,512]{2,1,0:T(8,128)(2,1)S(1)} %keys_and_values.2.kv_ref), custom_call_target="tpu_custom_call" | custom-call | flops 4294967296 | bytes 4194304 | tf_op jit(solution)/shard_map/attend/pallas_call | solution.py:185
  39.9 0.1 collective-permute-start.5
  39.9 1.0 %scatter.1 = (bf16[8,128,256]{2,1,0:T(8,128)(2,1)S(1)}, bf16[4,128,256]{2,1,0:T(8,128)(2,1)S(1)}) custom-call(s32[3,1024]{1,0:T(4,128)S(1)} %reshape.12.codes_ref, bf16[1024,256]{1,0:T(8,128)(2,1)S(1)} %get-tuple-element.33.rows_ref), custom_call_target="tpu_custom_call" | custom-call | flops 1073741824 | bytes 2097152 | tf_op jit(solution)/shard_map/scatter/pallas_call | solution.py:105
  40.9 6.2 %attend.6.refs_3_ = bf16[4,128,256]{2,1,0:T(8,128)(2,1)S(1)} custom-call(bf16[8,128,256]{2,1,0:T(8,128)(2,1)S(1)} %get-tuple-element.43.rows_ref, bf16[4,1024,512]{2,1,0:T(8,128)(2,1)S(1)} %keys_and_values.2.kv_ref), custom_call_target="tpu_custom_call" | custom-call | flops 4294967296 | bytes 4194304 | tf_op jit(solution)/shard_map/attend/pallas_call | solution.py:185
  47.2 1.8 %collective-permute-start.1 = (bf16[4,128,256]{2,1,0:T(8,128)(2,1)S(1)}, bf16[4,128,256]{2,1,0:T(8,128)(2,1)S(1)}, u32[]{:S(2)}, u32[]{:S(2)}) collective-permute-start(bf16[4,128,256]{2,1,0:T(8,128)(2,1)S(1)} %get-tuple-element.36), channel_id=1, source_target_pairs={{0,4},{4,0},{8,12},{12,8},{16,20},{20,16},{24,28},{28,24},{1,5},{5... | collective-permute-start | bytes 786440 | tf_op jit(solution)/shard_map/ppermute | solution.py:25
  49.0 3.6 %collective-permute-start.6 = (bf16[4,128,256]{2,1,0:T(8,128)(2,1)S(1)}, bf16[4,128,256]{2,1,0:T(8,128)(2,1)S(1)}, u32[]{:S(2)}, u32[]{:S(2)}) collective-permute-start(bf16[4,128,256]{2,1,0:T(8,128)(2,1)S(1)} %attend.8), channel_id=1, source_target_pairs={{0,28},{4,8},{8,4},{12,16},{16,12},{20,24},{24,20},{28,0},{1,29},{... | collective-permute-start | bytes 786440 | tf_op jit(solution)/shard_map/ppermute | solution.py:25
  52.6 1.3 %keys_and_values.3.kv_ref = bf16[4,1024,512]{2,1,0:T(8,128)(2,1)S(1)} custom-call(bf16[256,256]{1,0:T(8,128)(2,1)S(1)} %copy-done.2, bf16[256,256]{1,0:T(8,128)(2,1)S(1)} %copy-done.3, bf16[2048,256]{1,0:T(8,128)(2,1)S(1)} %collective-permute-done.4.refs_0_, bf16[2048,256]{1,0:T(8,128)(2,1)S(1)} %collective-permute-done.5.refs_1_), custom_call_target="tpu_custom_call" | custom-call | flops 1073741824 | bytes 6291456 | tf_op jit(solution)/shard_map/keys_and_values/pallas_call | solution.py:130
  53.8 6.0 %attend.9 = bf16[4,128,256]{2,1,0:T(8,128)(2,1)S(1)} custom-call(bf16[8,128,256]{2,1,0:T(8,128)(2,1)S(1)} %collective-permute-done.2.rows_ref, bf16[4,1024,512]{2,1,0:T(8,128)(2,1)S(1)} %keys_and_values.3.kv_ref), custom_call_target="tpu_custom_call" | custom-call | flops 4294967296 | bytes 4194304 | tf_op jit(solution)/shard_map/attend/pallas_call | solution.py:185
  59.8 2.2 %collective-permute-done.1.rows_ref = bf16[4,128,256]{2,1,0:T(8,128)(2,1)S(1)} collective-permute-done((bf16[4,128,256]{2,1,0:T(8,128)(2,1)S(1)}, bf16[4,128,256]{2,1,0:T(8,128)(2,1)S(1)}, u32[]{:S(2)}, u32[]{:S(2)}) %collective-permute-start.1) | collective-permute-done | bytes 262176 | tf_op jit(solution)/shard_map/ppermute | solution.py:25
  62.0 6.0 %attend.10 = bf16[4,128,256]{2,1,0:T(8,128)(2,1)S(1)} custom-call(bf16[4,128,256]{2,1,0:T(8,128)(2,1)S(1)} %collective-permute-done.1.rows_ref, bf16[4,1024,512]{2,1,0:T(8,128)(2,1)S(1)} %keys_and_values.3.kv_ref), custom_call_target="tpu_custom_call" | custom-call | flops 4294967296 | bytes 4194304 | tf_op jit(solution)/shard_map/attend/pallas_call | solution.py:185
  68.0 1.8 %collective-permute-start.9 = (bf16[4,128,256]{2,1,0:T(8,128)(2,1)S(1)}, bf16[4,128,256]{2,1,0:T(8,128)(2,1)S(1)}, u32[]{:S(2)}, u32[]{:S(2)}) collective-permute-start(bf16[4,128,256]{2,1,0:T(8,128)(2,1)S(1)} %attend.10), channel_id=1, source_target_pairs={{0,4},{4,0},{8,12},{12,8},{16,20},{20,16},{24,28},{28,24},{1,5},{5... | collective-permute-start | bytes 786440 | tf_op jit(solution)/shard_map/ppermute | solution.py:25
  69.8 3.6 %collective-permute-start.7 = (bf16[4,128,256]{2,1,0:T(8,128)(2,1)S(1)}, bf16[4,128,256]{2,1,0:T(8,128)(2,1)S(1)}, u32[]{:S(2)}, u32[]{:S(2)}) collective-permute-start(bf16[4,128,256]{2,1,0:T(8,128)(2,1)S(1)} %attend.9), channel_id=1, source_target_pairs={{0,28},{4,8},{8,4},{12,16},{16,12},{20,24},{24,20},{28,0},{1,29},{... | collective-permute-start | bytes 786440 | tf_op jit(solution)/shard_map/ppermute | solution.py:25
  73.4 6.2 %attend.11.refs_4_ = bf16[4,128,256]{2,1,0:T(8,128)(2,1)S(1)} custom-call(bf16[8,128,256]{2,1,0:T(8,128)(2,1)S(1)} %get-tuple-element.43.rows_ref, bf16[4,1024,512]{2,1,0:T(8,128)(2,1)S(1)} %keys_and_values.3.kv_ref), custom_call_target="tpu_custom_call" | custom-call | flops 4294967296 | bytes 4194304 | tf_op jit(solution)/shard_map/attend/pallas_call | solution.py:185
  79.7 0.0 copy-start.4
  79.7 0.0 collective-permute-done.7.refs_6_
  79.7 1.5 %partial_sum.1.partial_ref = f32[1024,256]{1,0:T(8,128)S(1)} custom-call(bf16[1024,1024]{1,0:T(8,128)(2,1)S(1)} %get-tuple-element.29.refs_0_, bf16[1024,1024]{1,0:T(8,128)(2,1)S(1)} %get-tuple-element.30.refs_1_, bf16[1024,1024]{1,0:T(8,128)(2,1)S(1)} %get-tuple-element.31.refs_2_, bf16[4,128,256]{2,1,0:T(8,128)(2,1)S(1)} %attend.6.refs_3_, ...), custom_call_target="tpu_custom_call" | custom-call | flops 1073741824 | bytes 2097152 | tf_op jit(solution)/shard_map/partial_sum/pallas_call | solution.py:244
  81.2 2.0 %finish.1 = bf16[1024,256]{1,0:T(8,128)(2,1)} custom-call(f32[1024,256]{1,0:T(8,128)S(1)} %partial_sum.1.partial_ref, bf16[1024,256]{1,0:T(8,128)(2,1)S(1)} %bitcast.6, bf16[256,256]{1,0:T(8,128)(2,1)S(1)} %copy-done.4, bf16[1024,1024]{1,0:T(8,128)(2,1)S(1)} %get-tuple-element.29.refs_0_, bf16[1024,1024]{1,0:T(8,128)(2,1)S(1)} %get-tuple-element.30.refs_1_, ...), custom_call_target="tpu_custom_call" | custom-call | flops 1073741824 | bytes 2097152 | tf_op jit(solution)/shard_map/finish/pallas_call | solution.py:264
  (17 shorter events, 0.0 us)
Async XLA Ops:
  0.0 3.9 %copy-start.5 = (bf16[256,256]{1,0:T(8,128)(2,1)S(1)}, bf16[256,256]{1,0:T(8,128)(2,1)}, u32[]{:S(2)}) copy-start(bf16[256,256]{1,0:T(8,128)(2,1)} %weight_hbm.1) | copy-start | bytes 393220
  0.0 3.9 %copy-start.6 = (f32[256]{0:T(256)S(1)}, f32[256]{0:T(256)}, u32[]{:S(2)}) copy-start(f32[256]{0:T(256)} %param.10) | copy-start | bytes 3076
  0.0 3.9 %copy-start.1 = (bf16[16,64,256]{2,1,0:T(8,128)(2,1)S(1)}, bf16[16,64,256]{2,1,0:T(8,128)(2,1)}, u32[]{:S(2)}) copy-start(bf16[16,64,256]{2,1,0:T(8,128)(2,1)} %param.9) | copy-start | bytes 1572868
  0.0 26.6 %collective-permute-start = (bf16[2048,256]{1,0:T(8,128)(2,1)}, bf16[2048,256]{1,0:T(8,128)(2,1)S(1)}, u32[]{:S(2)}, u32[]{:S(2)}) collective-permute-start(bf16[2048,256]{1,0:T(8,128)(2,1)} %refs_0_.1), channel_id=1, source_target_pairs={{0,1},{1,0},{2,3},{3,2},{4,5},{5,4},{6,7},{7,6},{8,9},{9,8},{10,11... | collective-permute-start | bytes 3145736 | tf_op jit(solution)/shard_map/ppermute | solution.py:30
  4.0 4.5 %copy-start = (bf16[2048,256]{1,0:T(8,128)(2,1)S(1)}, bf16[2048,256]{1,0:T(8,128)(2,1)}, u32[]{:S(2)}) copy-start(bf16[2048,256]{1,0:T(8,128)(2,1)} %refs_0_.1) | copy-start | bytes 3145732
  4.0 22.6 %copy-start.2 = (bf16[256,256]{1,0:T(8,128)(2,1)S(1)}, bf16[256,256]{1,0:T(8,128)(2,1)}, u32[]{:S(2)}) copy-start(bf16[256,256]{1,0:T(8,128)(2,1)} %key_ref.3) | copy-start | bytes 393220
  4.0 22.6 %copy-start.3 = (bf16[256,256]{1,0:T(8,128)(2,1)S(1)}, bf16[256,256]{1,0:T(8,128)(2,1)}, u32[]{:S(2)}) copy-start(bf16[256,256]{1,0:T(8,128)(2,1)} %value_ref.3) | copy-start | bytes 393220
  5.8 20.8 %collective-permute-start.3 = (bf16[4,128,256]{2,1,0:T(8,128)(2,1)S(1)}, bf16[4,128,256]{2,1,0:T(8,128)(2,1)S(1)}, u32[]{:S(2)}, u32[]{:S(2)}) collective-permute-start(bf16[4,128,256]{2,1,0:T(8,128)(2,1)S(1)} %get-tuple-element.38), channel_id=1, source_target_pairs={{0,4},{4,0},{8,12},{12,8},{16,20},{20,16},{24,28},{28,24},{1,5},{5... | collective-permute-start | bytes 786440 | tf_op jit(solution)/shard_map/ppermute | solution.py:25
  8.5 31.4 %collective-permute-start.4 = (bf16[2048,256]{1,0:T(8,128)(2,1)S(1)}, bf16[2048,256]{1,0:T(8,128)(2,1)S(1)}, u32[]{:S(2)}, u32[]{:S(2)}) collective-permute-start(bf16[2048,256]{1,0:T(8,128)(2,1)S(1)} %copy-done), channel_id=1, source_target_pairs={{0,2},{1,3},{2,0},{3,1},{4,6},{5,7},{6,4},{7,5},{8,10},{9,11},{10,... | collective-permute-start | bytes 3145736 | tf_op jit(solution)/shard_map/ppermute | solution.py:30
  10.0 23.8 %collective-permute-start.2 = (bf16[8,128,256]{2,1,0:T(8,128)(2,1)S(1)}, bf16[8,128,256]{2,1,0:T(8,128)(2,1)S(1)}, u32[]{:S(2)}, u32[]{:S(2)}) collective-permute-start(bf16[8,128,256]{2,1,0:T(8,128)(2,1)S(1)} %get-tuple-element.37), channel_id=1, source_target_pairs={{0,28},{4,8},{8,4},{12,16},{16,12},{20,24},{24,20},{28,0},{1,29},{... | collective-permute-start | bytes 1572872 | tf_op jit(solution)/shard_map/ppermute | solution.py:25
  39.9 12.7 %collective-permute-start.5 = (bf16[2048,256]{1,0:T(8,128)(2,1)S(1)}, bf16[2048,256]{1,0:T(8,128)(2,1)S(1)}, u32[]{:S(2)}, u32[]{:S(2)}) collective-permute-start(bf16[2048,256]{1,0:T(8,128)(2,1)S(1)} %collective-permute-done.4.refs_0_), channel_id=1, source_target_pairs={{0,1},{1,0},{2,3},{3,2},{4,5},{5,4},{6,7},{7,6},{8,9},{9,8},{10,11... | collective-permute-start | bytes 3145736 | tf_op jit(solution)/shard_map/ppermute | solution.py:30
  47.2 14.9 %collective-permute-start.1 = (bf16[4,128,256]{2,1,0:T(8,128)(2,1)S(1)}, bf16[4,128,256]{2,1,0:T(8,128)(2,1)S(1)}, u32[]{:S(2)}, u32[]{:S(2)}) collective-permute-start(bf16[4,128,256]{2,1,0:T(8,128)(2,1)S(1)} %get-tuple-element.36), channel_id=1, source_target_pairs={{0,4},{4,0},{8,12},{12,8},{16,20},{20,16},{24,28},{28,24},{1,5},{5... | collective-permute-start | bytes 786440 | tf_op jit(solution)/shard_map/ppermute | solution.py:25
  49.0 30.7 %collective-permute-start.6 = (bf16[4,128,256]{2,1,0:T(8,128)(2,1)S(1)}, bf16[4,128,256]{2,1,0:T(8,128)(2,1)S(1)}, u32[]{:S(2)}, u32[]{:S(2)}) collective-permute-start(bf16[4,128,256]{2,1,0:T(8,128)(2,1)S(1)} %attend.8), channel_id=1, source_target_pairs={{0,28},{4,8},{8,4},{12,16},{16,12},{20,24},{24,20},{28,0},{1,29},{... | collective-permute-start | bytes 786440 | tf_op jit(solution)/shard_map/ppermute | solution.py:25
  52.6 27.1 %collective-permute-start.8 = (bf16[4,128,256]{2,1,0:T(8,128)(2,1)S(1)}, bf16[4,128,256]{2,1,0:T(8,128)(2,1)S(1)}, u32[]{:S(2)}, u32[]{:S(2)}) collective-permute-start(bf16[4,128,256]{2,1,0:T(8,128)(2,1)S(1)} %attend.7), channel_id=1, source_target_pairs={{0,4},{4,0},{8,12},{12,8},{16,20},{20,16},{24,28},{28,24},{1,5},{5... | collective-permute-start | bytes 786440 | tf_op jit(solution)/shard_map/ppermute | solution.py:25
  68.0 13.2 %collective-permute-start.9 = (bf16[4,128,256]{2,1,0:T(8,128)(2,1)S(1)}, bf16[4,128,256]{2,1,0:T(8,128)(2,1)S(1)}, u32[]{:S(2)}, u32[]{:S(2)}) collective-permute-start(bf16[4,128,256]{2,1,0:T(8,128)(2,1)S(1)} %attend.10), channel_id=1, source_target_pairs={{0,4},{4,0},{8,12},{12,8},{16,20},{20,16},{24,28},{28,24},{1,5},{5... | collective-permute-start | bytes 786440 | tf_op jit(solution)/shard_map/ppermute | solution.py:25
  69.8 9.9 %collective-permute-start.7 = (bf16[4,128,256]{2,1,0:T(8,128)(2,1)S(1)}, bf16[4,128,256]{2,1,0:T(8,128)(2,1)S(1)}, u32[]{:S(2)}, u32[]{:S(2)}) collective-permute-start(bf16[4,128,256]{2,1,0:T(8,128)(2,1)S(1)} %attend.9), channel_id=1, source_target_pairs={{0,28},{4,8},{8,4},{12,16},{16,12},{20,24},{24,20},{28,0},{1,29},{... | collective-permute-start | bytes 786440 | tf_op jit(solution)/shard_map/ppermute | solution.py:25
  79.7 1.6 %copy-start.4 = (bf16[256,256]{1,0:T(8,128)(2,1)S(1)}, bf16[256,256]{1,0:T(8,128)(2,1)}, u32[]{:S(2)}) copy-start(bf16[256,256]{1,0:T(8,128)(2,1)} %weight_ref.1) | copy-start | bytes 393220

commit v7 on v5

--- a/solution.py
+++ b/solution.py
@@ -132,7 +132,7 @@
     )(w_key, w_value, *features)
 
 
-def attend_kernel(rows_ref, kv_ref, out_ref, scores_ref, *, stack, start):
+def attend_kernel(rows_ref, kv_ref, out_ref, scores_ref, *, stack, start, unroll):
     blocks, (_, count, width) = kv_ref.shape[0], rows_ref.shape
     head_size = width // HEADS
     factor = head_size ** (-0.5) * LOG2_E
@@ -148,17 +148,15 @@
             jnp.concatenate(kept, axis=0), kv_ref[b, :, side],
             (((1,), (1,)), ((), ())), preferred_element_type=jnp.float32)
 
-    scores_ref[...] = scores_of(0, 0)
-
-    @pl.loop(0, blocks // UNROLL)
-    def _(step):
-        scores = scores_ref[...]
-        for unit in range(UNROLL):
-            b = step * UNROLL + unit
+    def visit(step, scores, closing):
+        for unit in range(unroll):
+            b = step * unroll + unit
             merged = None
             for at, first in enumerate(firsts):
                 if at + 1 < len(firsts):
                     following = scores_of(b, firsts[at + 1])
+                elif closing and unit + 1 == unroll:
+                    following = None
                 else:
                     following = scores_of(jnp.minimum(b + 1, blocks - 1), 0)
                 peak = jnp.max(scores, axis=1, keepdims=True)
@@ -170,16 +168,25 @@
                     merged = part if first + i == 0 else jnp.where(head_of == first + i, part, merged)
                 scores = following
             out_ref[b] = merged.astype(jnp.bfloat16)
-        scores_ref[...] = scores
-
-
-def attend(rows, kv, start=0):
+        return scores
+
+    if unroll == blocks:
+        visit(0, scores_of(0, 0), True)
+        return
+    scores_ref[...] = scores_of(0, 0)
+
+    @pl.loop(0, blocks // unroll)
+    def _(step):
+        scores_ref[...] = visit(step, scores_ref[...], False)
+
+
+def attend(rows, kv, start=0, unroll=UNROLL):
     _, count, width = rows.shape
     blocks, keys = kv.shape[:2]
     stack = 2
     pairs = blocks * count * keys
     return pl.pallas_call(
-        functools.partial(attend_kernel, stack=stack, start=start),
+        functools.partial(attend_kernel, stack=stack, start=start, unroll=unroll),
         out_shape=jax.ShapeDtypeStruct((blocks, count, width), jnp.bfloat16),
         scratch_shapes=[pltpu.VMEM((stack * count, keys), jnp.float32)],
         compiler_params=params(),
@@ -194,8 +201,12 @@
     entries, count = codes_ref.shape
     spare = jnp.zeros((8 - entries, count), jnp.int32)
     at = jnp.concatenate([codes_ref[...], spare], axis=0).T
-    lane = lax.broadcasted_iota(jnp.int32, (count, CAP), 1).astype(jnp.int16)
-    near = [jnp.broadcast_to(at[:, entry:entry + 1], (count, CAP)).astype(jnp.int16) for entry in range(entries)]
+    tile = 16
+    lane = lax.broadcasted_iota(jnp.int32, (1, tile, CAP), 2).astype(jnp.int16)
+    near = [
+        jnp.broadcast_to(at[:, entry:entry + 1], (count, CAP)).astype(jnp.int16).reshape(count // tile, tile, CAP)
+        for entry in range(entries)
+    ]
     one, zero = jnp.ones((), jnp.bfloat16), jnp.zeros((), jnp.bfloat16)
     for group, out_ref in zip(groups, out_refs):
         for step in range(out_ref.shape[1] // CAP):
@@ -203,7 +214,7 @@
             hit = slot == near[0]
             for entry in range(1, entries):
                 hit = hit | (slot == near[entry])
-            out_ref[:, step * CAP:(step + 1) * CAP] = jnp.where(hit, one, zero)
+            out_ref[:, step * CAP:(step + 1) * CAP] = jnp.where(hit, one, zero).reshape(count, CAP)
 
 
 def picks(codes, groups):
@@ -305,7 +316,7 @@
     projected, *_ = lax.optimization_barrier((projected, *ready))
     slots_own, *ready = scatter(codes, projected, blocks)
     kvs = [keys_and_values(held[0], w_key, w_value, keys)]
-    own = [attend(slots_own, kvs[0])]
+    own = [attend(slots_own, kvs[0], unroll=4 if staged else UNROLL)]
     last = own[0]
     if staged:
         *ready, last = lax.optimization_barrier((*ready, last))
@@ -319,17 +330,16 @@
         for name in turns:
             rows, last = lax.optimization_barrier((arrived[name], last))
             last = arrived[name] = attend(rows, kvs[part])
-            if staged and part == 0 and name == turns[0]:
-                across, last = lax.optimization_barrier((across, last))
-                beyond = swapped(across, "band", 1)
         if staged and not part:
-            arrived = dict(zip(arrived, lax.optimization_barrier(tuple(arrived.values()))))
+            *both, across = lax.optimization_barrier((*arrived.values(), across))
+            arrived = dict(zip(arrived, both))
+            beyond = swapped(across, "band", 1)
         for side, name in enumerate(("lower", "upper")):
             arrived[name] = exchanged(arrived[name], side)
         back.append((arrived["lower"], arrived["upper"]))
     if staged:
         turn, last = lax.optimization_barrier((slots_own, last))
-        own.append(attend(turn, kvs[1], blocks))
+        own.append(attend(turn, kvs[1], blocks, unroll=4))
 
     cuts = [i * blocks * CAP for i in range(len(kvs))]
     early = [((1, at), rows) for at, rows in zip(cuts, own)]

time: 88.7 us -> 92.1 us (1.038)
  waiting for transfers between devices: 21.5 us -> 23.8 us
  starting transfers between devices: 18.3 us -> 19.9 us
    ppermute x8, starting transfers between devices: 15.1 us -> 17.8 us  [exchanged(): lax.ppermute(block, 'sector', [(i, ((i + side ^ 1) - side) % count) for i...]
    ppermute x8, waiting for transfers between devices: 21.4 us -> 23.8 us  [exchanged(): lax.ppermute(block, 'sector', [(i, ((i + side ^ 1) - side) % count) for i...]
    ppermute x3, starting transfers between devices: 3.21 us -> 2.15 us  [swapped(): return lax.ppermute(block, axis, [(i, i ^ bit) for i in range(count)])]
  transfers between devices with their start and end apart: 11 -> 11, of which waited for: 4 -> 5; matrix products, arithmetic and copies ran while one was open for 1% -> 1% of each run, Pallas kernels for 52% -> 49%
where the time goes in v7:
time: 92.1 us; the launch traced here: 92 us
  Pallas kernels  47.1 us (51%)
  waiting for transfers between devices  23.8 us (26%)
  starting transfers between devices  19.9 us (22%)
    pallas_call x6, Pallas kernels, attend(): pl.pallas_call(functools.partial(attend_kernel, stack=stack, start=start,...  36 us
    ppermute x8, waiting for transfers between devices, exchanged(): lax.ppermute(block, 'sector', [(i, ((i + side ^ 1) - side) % count) for i...  23.8 us
    ppermute x8, starting transfers between devices, exchanged(): lax.ppermute(block, 'sector', [(i, ((i + side ^ 1) - side) % count) for i...  17.8 us
    pallas_call x2, Pallas kernels, keys_and_values(): pl.pallas_call(kv_kernel, out_shape=jax.ShapeDtypeStruct((count // keys,...  2.51 us
    pallas_call x1, Pallas kernels, picks(): pl.pallas_call(functools.partial(pick_kernel, groups=groups), out_shape=(...  2.5 us
    ppermute x3, starting transfers between devices, swapped(): return lax.ppermute(block, axis, [(i, i ^ bit) for i in range(count)])  2.15 us
    pallas_call x1, Pallas kernels, finish(): pl.pallas_call(functools.partial(final_kernel, places=places), out_shape=...  1.97 us
  transfers between devices with their start and end apart: 11, of which 5 were waited for; matrix products, arithmetic and copies ran while one was open for 1% of the time, Pallas kernels for 49%

profile of v7, /device:TPU:0, one launch (start us, length us, event | category | flops | bytes accessed | tf_op | source)
XLA Modules:
  0.0 92.0 jit_solution(17212753549197948955)
XLA Ops:
  0.0 0.6 collective-permute-start
  0.6 0.8 fusion.6
  1.3 0.1 reshape.12.codes_ref
  1.4 2.5 %picks.1 = (bf16[1024,1024]{1,0:T(8,128)(2,1)S(1)}, bf16[1024,1024]{1,0:T(8,128)(2,1)S(1)}, bf16[1024,1024]{1,0:T(8,128)(2,1)S(1)}) custom-call(s32[3,1024]{1,0:T(4,128)S(1)} %reshape.12.codes_ref), custom_call_target="tpu_custom_call" | custom-call | flops 1073741824 | bytes 2097152 | tf_op jit(solution)/shard_map/picks/pallas_call | solution.py:222
  4.0 0.0 copy-start
  4.0 0.0 copy-start.2
  4.0 1.4 %project.1 = (bf16[1024,256]{1,0:T(8,128)(2,1)S(1)}, bf16[4,128,256]{2,1,0:T(8,128)(2,1)S(1)}, bf16[4,128,256]{2,1,0:T(8,128)(2,1)S(1)}) custom-call(s32[3,1024]{1,0:T(4,128)S(1)} %reshape.12.codes_ref, bf16[1024,256]{1,0:T(8,128)(2,1)S(1)} %bitcast.5, f32[1,256]{1,0:T(1,128)S(1)} %bitcast.7, bf16[256,256]{1,0:T(8,128)(2,1)S(1)} %copy-done.5), custom_call_target="tpu_custom_call" | custom-call | flops 4294967296 | bytes 2097152 | tf_op jit(solution)/shard_map/project/pallas_call | solution.py:75
  5.4 2.7 %collective-permute-start.4 = (bf16[4,128,256]{2,1,0:T(8,128)(2,1)S(1)}, bf16[4,128,256]{2,1,0:T(8,128)(2,1)S(1)}, u32[]{:S(2)}, u32[]{:S(2)}) collective-permute-start(bf16[4,128,256]{2,1,0:T(8,128)(2,1)S(1)} %get-tuple-element.42), channel_id=1, source_target_pairs={{0,4},{4,0},{8,12},{12,8},{16,20},{20,16},{24,28},{28,24},{1,5},{5... | collective-permute-start | bytes 786440 | tf_op jit(solution)/shard_map/ppermute | solution.py:25
  8.0 1.5 %collective-permute-start.5 = (bf16[2048,256]{1,0:T(8,128)(2,1)S(1)}, bf16[2048,256]{1,0:T(8,128)(2,1)S(1)}, u32[]{:S(2)}, u32[]{:S(2)}) collective-permute-start(bf16[2048,256]{1,0:T(8,128)(2,1)S(1)} %copy-done), channel_id=1, source_target_pairs={{0,2},{1,3},{2,0},{3,1},{4,6},{5,7},{6,4},{7,5},{8,10},{9,11},{10,... | collective-permute-start | bytes 3145736 | tf_op jit(solution)/shard_map/ppermute | solution.py:30
  9.6 3.6 %collective-permute-start.3 = (bf16[4,128,256]{2,1,0:T(8,128)(2,1)S(1)}, bf16[4,128,256]{2,1,0:T(8,128)(2,1)S(1)}, u32[]{:S(2)}, u32[]{:S(2)}) collective-permute-start(bf16[4,128,256]{2,1,0:T(8,128)(2,1)S(1)} %get-tuple-element.41), channel_id=1, source_target_pairs={{0,28},{4,8},{8,4},{12,16},{16,12},{20,24},{24,20},{28,0},{1,29},{... | collective-permute-start | bytes 786440 | tf_op jit(solution)/shard_map/ppermute | solution.py:25
  13.1 7.4 %collective-permute-done.4.rows_ref = bf16[4,128,256]{2,1,0:T(8,128)(2,1)S(1)} collective-permute-done((bf16[4,128,256]{2,1,0:T(8,128)(2,1)S(1)}, bf16[4,128,256]{2,1,0:T(8,128)(2,1)S(1)}, u32[]{:S(2)}, u32[]{:S(2)}) %collective-permute-start.4) | collective-permute-done | bytes 262176 | tf_op jit(solution)/shard_map/ppermute | solution.py:25
  20.5 1.3 %keys_and_values.2.kv_ref = bf16[4,1024,512]{2,1,0:T(8,128)(2,1)S(1)} custom-call(bf16[256,256]{1,0:T(8,128)(2,1)S(1)} %copy-done.2, bf16[256,256]{1,0:T(8,128)(2,1)S(1)} %copy-done.3, bf16[2048,256]{1,0:T(8,128)(2,1)S(1)} %copy-done, bf16[2048,256]{1,0:T(8,128)(2,1)S(1)} %collective-permute-done.refs_1_), custom_call_target="tpu_custom_call" | custom-call | flops 1073741824 | bytes 6291456 | tf_op jit(solution)/shard_map/keys_and_values/pallas_call | solution.py:126
  21.8 6.0 %attend.7 = bf16[4,128,256]{2,1,0:T(8,128)(2,1)S(1)} custom-call(bf16[4,128,256]{2,1,0:T(8,128)(2,1)S(1)} %collective-permute-done.4.rows_ref, bf16[4,1024,512]{2,1,0:T(8,128)(2,1)S(1)} %keys_and_values.2.kv_ref), custom_call_target="tpu_custom_call" | custom-call | flops 4294967296 | bytes 4194304 | tf_op jit(solution)/shard_map/attend/pallas_call | solution.py:188
  27.8 6.2 %attend.8 = bf16[4,128,256]{2,1,0:T(8,128)(2,1)S(1)} custom-call(bf16[4,128,256]{2,1,0:T(8,128)(2,1)S(1)} %collective-permute-done.3.rows_ref, bf16[4,1024,512]{2,1,0:T(8,128)(2,1)S(1)} %keys_and_values.2.kv_ref), custom_call_target="tpu_custom_call" | custom-call | flops 4294967296 | bytes 4194304 | tf_op jit(solution)/shard_map/attend/pallas_call | solution.py:188
  34.0 0.1 collective-permute-start.6
  34.1 1.3 %scatter.1 = (bf16[8,128,256]{2,1,0:T(8,128)(2,1)S(1)}, bf16[4,128,256]{2,1,0:T(8,128)(2,1)S(1)}, bf16[4,128,256]{2,1,0:T(8,128)(2,1)S(1)}) custom-call(s32[3,1024]{1,0:T(4,128)S(1)} %reshape.12.codes_ref, bf16[1024,256]{1,0:T(8,128)(2,1)S(1)} %get-tuple-element.35.rows_ref), custom_call_target="tpu_custom_call" | custom-call | flops 1073741824 | bytes 2097152 | tf_op jit(solution)/shard_map/scatter/pallas_call | solution.py:101
  35.4 5.8 %attend.6.refs_3_ = bf16[4,128,256]{2,1,0:T(8,128)(2,1)S(1)} custom-call(bf16[8,128,256]{2,1,0:T(8,128)(2,1)S(1)} %get-tuple-element.47.rows_ref, bf16[4,1024,512]{2,1,0:T(8,128)(2,1)S(1)} %keys_and_values.2.kv_ref), custom_call_target="tpu_custom_call" | custom-call | flops 4294967296 | bytes 4194304 | tf_op jit(solution)/shard_map/attend/pallas_call | solution.py:188
  41.2 4.8 %collective-permute-start.2 = (bf16[4,128,256]{2,1,0:T(8,128)(2,1)S(1)}, bf16[4,128,256]{2,1,0:T(8,128)(2,1)S(1)}, u32[]{:S(2)}, u32[]{:S(2)}) collective-permute-start(bf16[4,128,256]{2,1,0:T(8,128)(2,1)S(1)} %get-tuple-element.40), channel_id=1, source_target_pairs={{0,28},{4,8},{8,4},{12,16},{16,12},{20,24},{24,20},{28,0},{1,29},{... | collective-permute-start | bytes 786440 | tf_op jit(solution)/shard_map/ppermute | solution.py:25
  46.0 0.1 collective-permute-start.7
  46.1 2.0 %collective-permute-start.1 = (bf16[4,128,256]{2,1,0:T(8,128)(2,1)S(1)}, bf16[4,128,256]{2,1,0:T(8,128)(2,1)S(1)}, u32[]{:S(2)}, u32[]{:S(2)}) collective-permute-start(bf16[4,128,256]{2,1,0:T(8,128)(2,1)S(1)} %get-tuple-element.39), channel_id=1, source_target_pairs={{0,4},{4,0},{8,12},{12,8},{16,20},{20,16},{24,28},{28,24},{1,5},{5... | collective-permute-start | bytes 786440 | tf_op jit(solution)/shard_map/ppermute | solution.py:25
  48.1 5.2 %collective-permute-done.2.rows_ref = bf16[4,128,256]{2,1,0:T(8,128)(2,1)S(1)} collective-permute-done((bf16[4,128,256]{2,1,0:T(8,128)(2,1)S(1)}, bf16[4,128,256]{2,1,0:T(8,128)(2,1)S(1)}, u32[]{:S(2)}, u32[]{:S(2)}) %collective-permute-start.2) | collective-permute-done | bytes 262176 | tf_op jit(solution)/shard_map/ppermute | solution.py:25
  53.3 1.3 %keys_and_values.3.kv_ref = bf16[4,1024,512]{2,1,0:T(8,128)(2,1)S(1)} custom-call(bf16[256,256]{1,0:T(8,128)(2,1)S(1)} %copy-done.2, bf16[256,256]{1,0:T(8,128)(2,1)S(1)} %copy-done.3, bf16[2048,256]{1,0:T(8,128)(2,1)S(1)} %collective-permute-done.5.refs_0_, bf16[2048,256]{1,0:T(8,128)(2,1)S(1)} %collective-permute-done.6.refs_1_), custom_call_target="tpu_custom_call" | custom-call | flops 1073741824 | bytes 6291456 | tf_op jit(solution)/shard_map/keys_and_values/pallas_call | solution.py:126
  54.6 6.0 %attend.9 = bf16[4,128,256]{2,1,0:T(8,128)(2,1)S(1)} custom-call(bf16[4,128,256]{2,1,0:T(8,128)(2,1)S(1)} %collective-permute-done.2.rows_ref, bf16[4,1024,512]{2,1,0:T(8,128)(2,1)S(1)} %keys_and_values.3.kv_ref), custom_call_target="tpu_custom_call" | custom-call | flops 4294967296 | bytes 4194304 | tf_op jit(solution)/shard_map/attend/pallas_call | solution.py:188
  60.6 9.3 %collective-permute-done.1.rows_ref = bf16[4,128,256]{2,1,0:T(8,128)(2,1)S(1)} collective-permute-done((bf16[4,128,256]{2,1,0:T(8,128)(2,1)S(1)}, bf16[4,128,256]{2,1,0:T(8,128)(2,1)S(1)}, u32[]{:S(2)}, u32[]{:S(2)}) %collective-permute-start.1) | collective-permute-done | bytes 262176 | tf_op jit(solution)/shard_map/ppermute | solution.py:25
  69.8 6.2 %attend.10 = bf16[4,128,256]{2,1,0:T(8,128)(2,1)S(1)} custom-call(bf16[4,128,256]{2,1,0:T(8,128)(2,1)S(1)} %collective-permute-done.1.rows_ref, bf16[4,1024,512]{2,1,0:T(8,128)(2,1)S(1)} %keys_and_values.3.kv_ref), custom_call_target="tpu_custom_call" | custom-call | flops 4294967296 | bytes 4194304 | tf_op jit(solution)/shard_map/attend/pallas_call | solution.py:188
  76.1 0.1 collective-permute-start.10
  76.1 4.5 %collective-permute-start.8 = (bf16[4,128,256]{2,1,0:T(8,128)(2,1)S(1)}, bf16[4,128,256]{2,1,0:T(8,128)(2,1)S(1)}, u32[]{:S(2)}, u32[]{:S(2)}) collective-permute-start(bf16[4,128,256]{2,1,0:T(8,128)(2,1)S(1)} %attend.9), channel_id=1, source_target_pairs={{0,28},{4,8},{8,4},{12,16},{16,12},{20,24},{24,20},{28,0},{1,29},{... | collective-permute-start | bytes 786440 | tf_op jit(solution)/shard_map/ppermute | solution.py:25
  80.6 5.8 %attend.11.refs_4_ = bf16[4,128,256]{2,1,0:T(8,128)(2,1)S(1)} custom-call(bf16[8,128,256]{2,1,0:T(8,128)(2,1)S(1)} %get-tuple-element.47.rows_ref, bf16[4,1024,512]{2,1,0:T(8,128)(2,1)S(1)} %keys_and_values.3.kv_ref), custom_call_target="tpu_custom_call" | custom-call | flops 4294967296 | bytes 4194304 | tf_op jit(solution)/shard_map/attend/pallas_call | solution.py:188
  86.5 0.8 collective-permute-done.8.refs_6_
  87.3 1.5 %partial_sum.1.partial_ref = f32[1024,256]{1,0:T(8,128)S(1)} custom-call(bf16[1024,1024]{1,0:T(8,128)(2,1)S(1)} %get-tuple-element.31.refs_0_, bf16[1024,1024]{1,0:T(8,128)(2,1)S(1)} %get-tuple-element.32.refs_1_, bf16[1024,1024]{1,0:T(8,128)(2,1)S(1)} %get-tuple-element.33.refs_2_, bf16[4,128,256]{2,1,0:T(8,128)(2,1)S(1)} %attend.6.refs_3_, ...), custom_call_target="tpu_custom_call" | custom-call | flops 1073741824 | bytes 2097152 | tf_op jit(solution)/shard_map/partial_sum/pallas_call | solution.py:251
  88.8 1.2 %collective-permute-done.10.refs_3_ = bf16[4,128,256]{2,1,0:T(8,128)(2,1)S(1)} collective-permute-done((bf16[4,128,256]{2,1,0:T(8,128)(2,1)S(1)}, bf16[4,128,256]{2,1,0:T(8,128)(2,1)S(1)}, u32[]{:S(2)}, u32[]{:S(2)}) %collective-permute-start.10) | collective-permute-done | bytes 262176 | tf_op jit(solution)/shard_map/ppermute | solution.py:25
  90.0 2.0 %finish.1 = bf16[1024,256]{1,0:T(8,128)(2,1)} custom-call(f32[1024,256]{1,0:T(8,128)S(1)} %partial_sum.1.partial_ref, bf16[1024,256]{1,0:T(8,128)(2,1)S(1)} %bitcast.6, bf16[256,256]{1,0:T(8,128)(2,1)S(1)} %copy-done.4, bf16[1024,1024]{1,0:T(8,128)(2,1)S(1)} %get-tuple-element.31.refs_0_, bf16[1024,1024]{1,0:T(8,128)(2,1)S(1)} %get-tuple-element.32.refs_1_, ...), custom_call_target="tpu_custom_call" | custom-call | flops 1073741824 | bytes 2097152 | tf_op jit(solution)/shard_map/finish/pallas_call | solution.py:271
  (19 shorter events, 0.0 us)
Async XLA Ops:
  0.0 3.9 %copy-start.5 = (bf16[256,256]{1,0:T(8,128)(2,1)S(1)}, bf16[256,256]{1,0:T(8,128)(2,1)}, u32[]{:S(2)}) copy-start(bf16[256,256]{1,0:T(8,128)(2,1)} %weight_hbm.1) | copy-start | bytes 393220
  0.0 3.9 %copy-start.6 = (f32[256]{0:T(256)S(1)}, f32[256]{0:T(256)}, u32[]{:S(2)}) copy-start(f32[256]{0:T(256)} %param.10) | copy-start | bytes 3076
  0.0 3.9 %copy-start.1 = (bf16[16,64,256]{2,1,0:T(8,128)(2,1)S(1)}, bf16[16,64,256]{2,1,0:T(8,128)(2,1)}, u32[]{:S(2)}) copy-start(bf16[16,64,256]{2,1,0:T(8,128)(2,1)} %param.9) | copy-start | bytes 1572868
  0.0 20.5 %collective-permute-start = (bf16[2048,256]{1,0:T(8,128)(2,1)}, bf16[2048,256]{1,0:T(8,128)(2,1)S(1)}, u32[]{:S(2)}, u32[]{:S(2)}) collective-permute-start(bf16[2048,256]{1,0:T(8,128)(2,1)} %refs_0_.1), channel_id=1, source_target_pairs={{0,1},{1,0},{2,3},{3,2},{4,5},{5,4},{6,7},{7,6},{8,9},{9,8},{10,11... | collective-permute-start | bytes 3145736 | tf_op jit(solution)/shard_map/ppermute | solution.py:30
  4.0 4.1 %copy-start = (bf16[2048,256]{1,0:T(8,128)(2,1)S(1)}, bf16[2048,256]{1,0:T(8,128)(2,1)}, u32[]{:S(2)}) copy-start(bf16[2048,256]{1,0:T(8,128)(2,1)} %refs_0_.1) | copy-start | bytes 3145732
  4.0 16.5 %copy-start.2 = (bf16[256,256]{1,0:T(8,128)(2,1)S(1)}, bf16[256,256]{1,0:T(8,128)(2,1)}, u32[]{:S(2)}) copy-start(bf16[256,256]{1,0:T(8,128)(2,1)} %key_ref.3) | copy-start | bytes 393220
  4.0 16.5 %copy-start.3 = (bf16[256,256]{1,0:T(8,128)(2,1)S(1)}, bf16[256,256]{1,0:T(8,128)(2,1)}, u32[]{:S(2)}) copy-start(bf16[256,256]{1,0:T(8,128)(2,1)} %value_ref.3) | copy-start | bytes 393220
  5.4 15.1 %collective-permute-start.4 = (bf16[4,128,256]{2,1,0:T(8,128)(2,1)S(1)}, bf16[4,128,256]{2,1,0:T(8,128)(2,1)S(1)}, u32[]{:S(2)}, u32[]{:S(2)}) collective-permute-start(bf16[4,128,256]{2,1,0:T(8,128)(2,1)S(1)} %get-tuple-element.42), channel_id=1, source_target_pairs={{0,4},{4,0},{8,12},{12,8},{16,20},{20,16},{24,28},{28,24},{1,5},{5... | collective-permute-start | bytes 786440 | tf_op jit(solution)/shard_map/ppermute | solution.py:25
  8.0 26.0 %collective-permute-start.5 = (bf16[2048,256]{1,0:T(8,128)(2,1)S(1)}, bf16[2048,256]{1,0:T(8,128)(2,1)S(1)}, u32[]{:S(2)}, u32[]{:S(2)}) collective-permute-start(bf16[2048,256]{1,0:T(8,128)(2,1)S(1)} %copy-done), channel_id=1, source_target_pairs={{0,2},{1,3},{2,0},{3,1},{4,6},{5,7},{6,4},{7,5},{8,10},{9,11},{10,... | collective-permute-start | bytes 3145736 | tf_op jit(solution)/shard_map/ppermute | solution.py:30
  9.6 18.2 %collective-permute-start.3 = (bf16[4,128,256]{2,1,0:T(8,128)(2,1)S(1)}, bf16[4,128,256]{2,1,0:T(8,128)(2,1)S(1)}, u32[]{:S(2)}, u32[]{:S(2)}) collective-permute-start(bf16[4,128,256]{2,1,0:T(8,128)(2,1)S(1)} %get-tuple-element.41), channel_id=1, source_target_pairs={{0,28},{4,8},{8,4},{12,16},{16,12},{20,24},{24,20},{28,0},{1,29},{... | collective-permute-start | bytes 786440 | tf_op jit(solution)/shard_map/ppermute | solution.py:25
  34.0 19.3 %collective-permute-start.6 = (bf16[2048,256]{1,0:T(8,128)(2,1)S(1)}, bf16[2048,256]{1,0:T(8,128)(2,1)S(1)}, u32[]{:S(2)}, u32[]{:S(2)}) collective-permute-start(bf16[2048,256]{1,0:T(8,128)(2,1)S(1)} %collective-permute-done.5.refs_0_), channel_id=1, source_target_pairs={{0,1},{1,0},{2,3},{3,2},{4,5},{5,4},{6,7},{7,6},{8,9},{9,8},{10,11... | collective-permute-start | bytes 3145736 | tf_op jit(solution)/shard_map/ppermute | solution.py:30
  41.2 12.1 %collective-permute-start.2 = (bf16[4,128,256]{2,1,0:T(8,128)(2,1)S(1)}, bf16[4,128,256]{2,1,0:T(8,128)(2,1)S(1)}, u32[]{:S(2)}, u32[]{:S(2)}) collective-permute-start(bf16[4,128,256]{2,1,0:T(8,128)(2,1)S(1)} %get-tuple-element.40), channel_id=1, source_target_pairs={{0,28},{4,8},{8,4},{12,16},{16,12},{20,24},{24,20},{28,0},{1,29},{... | collective-permute-start | bytes 786440 | tf_op jit(solution)/shard_map/ppermute | solution.py:25
  46.0 40.4 %collective-permute-start.7 = (bf16[4,128,256]{2,1,0:T(8,128)(2,1)S(1)}, bf16[4,128,256]{2,1,0:T(8,128)(2,1)S(1)}, u32[]{:S(2)}, u32[]{:S(2)}) collective-permute-start(bf16[4,128,256]{2,1,0:T(8,128)(2,1)S(1)} %attend.8), channel_id=1, source_target_pairs={{0,28},{4,8},{8,4},{12,16},{16,12},{20,24},{24,20},{28,0},{1,29},{... | collective-permute-start | bytes 786440 | tf_op jit(solution)/shard_map/ppermute | solution.py:25
  46.1 40.3 %collective-permute-start.9 = (bf16[4,128,256]{2,1,0:T(8,128)(2,1)S(1)}, bf16[4,128,256]{2,1,0:T(8,128)(2,1)S(1)}, u32[]{:S(2)}, u32[]{:S(2)}) collective-permute-start(bf16[4,128,256]{2,1,0:T(8,128)(2,1)S(1)} %attend.7), channel_id=1, source_target_pairs={{0,4},{4,0},{8,12},{12,8},{16,20},{20,16},{24,28},{28,24},{1,5},{5... | collective-permute-start | bytes 786440 | tf_op jit(solution)/shard_map/ppermute | solution.py:25
  46.1 23.7 %collective-permute-start.1 = (bf16[4,128,256]{2,1,0:T(8,128)(2,1)S(1)}, bf16[4,128,256]{2,1,0:T(8,128)(2,1)S(1)}, u32[]{:S(2)}, u32[]{:S(2)}) collective-permute-start(bf16[4,128,256]{2,1,0:T(8,128)(2,1)S(1)} %get-tuple-element.39), channel_id=1, source_target_pairs={{0,4},{4,0},{8,12},{12,8},{16,20},{20,16},{24,28},{28,24},{1,5},{5... | collective-permute-start | bytes 786440 | tf_op jit(solution)/shard_map/ppermute | solution.py:25
  76.1 13.9 %collective-permute-start.10 = (bf16[4,128,256]{2,1,0:T(8,128)(2,1)S(1)}, bf16[4,128,256]{2,1,0:T(8,128)(2,1)S(1)}, u32[]{:S(2)}, u32[]{:S(2)}) collective-permute-start(bf16[4,128,256]{2,1,0:T(8,128)(2,1)S(1)} %attend.10), channel_id=1, source_target_pairs={{0,4},{4,0},{8,12},{12,8},{16,20},{20,16},{24,28},{28,24},{1,5},{5... | collective-permute-start | bytes 786440 | tf_op jit(solution)/shard_map/ppermute | solution.py:25
  76.1 11.1 %collective-permute-start.8 = (bf16[4,128,256]{2,1,0:T(8,128)(2,1)S(1)}, bf16[4,128,256]{2,1,0:T(8,128)(2,1)S(1)}, u32[]{:S(2)}, u32[]{:S(2)}) collective-permute-start(bf16[4,128,256]{2,1,0:T(8,128)(2,1)S(1)} %attend.9), channel_id=1, source_target_pairs={{0,28},{4,8},{8,4},{12,16},{16,12},{20,24},{24,20},{28,0},{1,29},{... | collective-permute-start | bytes 786440 | tf_op jit(solution)/shard_map/ppermute | solution.py:25
  86.4 3.6 %copy-start.4 = (bf16[256,256]{1,0:T(8,128)(2,1)S(1)}, bf16[256,256]{1,0:T(8,128)(2,1)}, u32[]{:S(2)}) copy-start(bf16[256,256]{1,0:T(8,128)(2,1)} %weight_ref.1) | copy-start | bytes 393220

commit v8 on v5

--- a/solution.py
+++ b/solution.py
@@ -319,11 +319,10 @@
         for name in turns:
             rows, last = lax.optimization_barrier((arrived[name], last))
             last = arrived[name] = attend(rows, kvs[part])
-            if staged and part == 0 and name == turns[0]:
-                across, last = lax.optimization_barrier((across, last))
-                beyond = swapped(across, "band", 1)
         if staged and not part:
-            arrived = dict(zip(arrived, lax.optimization_barrier(tuple(arrived.values()))))
+            *both, across = lax.optimization_barrier((*arrived.values(), across))
+            arrived = dict(zip(arrived, both))
+            beyond = swapped(across, "band", 1)
         for side, name in enumerate(("lower", "upper")):
             arrived[name] = exchanged(arrived[name], side)
         back.append((arrived["lower"], arrived["upper"]))

time: 88.7 us -> 92.3 us (1.041)
  waiting for transfers between devices: 21.5 us -> 23.4 us
  starting transfers between devices: 18.3 us -> 19.9 us
    ppermute x8, starting transfers between devices: 15.1 us -> 17.8 us  [exchanged(): lax.ppermute(block, 'sector', [(i, ((i + side ^ 1) - side) % count) for i...]
    ppermute x8, waiting for transfers between devices: 21.4 us -> 23.4 us  [exchanged(): lax.ppermute(block, 'sector', [(i, ((i + side ^ 1) - side) % count) for i...]
    ppermute x3, starting transfers between devices: 3.21 us -> 2.15 us  [swapped(): return lax.ppermute(block, axis, [(i, i ^ bit) for i in range(count)])]
  transfers between devices with their start and end apart: 11 -> 11, of which waited for: 4 -> 5; matrix products, arithmetic and copies ran while one was open for 1% -> 1% of each run, Pallas kernels for 52% -> 50%
where the time goes in v8:
time: 92.3 us; the launch traced here: 92.2 us
  Pallas kernels  47.8 us (52%)
  waiting for transfers between devices  23.4 us (25%)
  starting transfers between devices  19.9 us (22%)
    pallas_call x6, Pallas kernels, attend(): pl.pallas_call(functools.partial(attend_kernel, stack=stack, start=start)...  36.5 us
    ppermute x8, waiting for transfers between devices, exchanged(): lax.ppermute(block, 'sector', [(i, ((i + side ^ 1) - side) % count) for i...  23.4 us
    ppermute x8, starting transfers between devices, exchanged(): lax.ppermute(block, 'sector', [(i, ((i + side ^ 1) - side) % count) for i...  17.8 us
    pallas_call x2, Pallas kernels, keys_and_values(): pl.pallas_call(kv_kernel, out_shape=jax.ShapeDtypeStruct((count // keys,...  2.51 us
    pallas_call x1, Pallas kernels, picks(): pl.pallas_call(functools.partial(pick_kernel, groups=groups), out_shape=(...  2.5 us
    ppermute x3, starting transfers between devices, swapped(): return lax.ppermute(block, axis, [(i, i ^ bit) for i in range(count)])  2.15 us
    pallas_call x1, Pallas kernels, finish(): pl.pallas_call(functools.partial(final_kernel, places=places), out_shape=...  1.97 us
  transfers between devices with their start and end apart: 11, of which 5 were waited for; matrix products, arithmetic and copies ran while one was open for 1% of the time, Pallas kernels for 50%

profile of v8, /device:TPU:0, one launch (start us, length us, event | category | flops | bytes accessed | tf_op | source)
XLA Modules:
  0.0 92.2 jit_solution(515854051449558733)
XLA Ops:
  0.0 0.6 collective-permute-start
  0.6 0.8 fusion.6
  1.3 0.1 reshape.12.codes_ref
  1.4 2.5 %picks.1 = (bf16[1024,1024]{1,0:T(8,128)(2,1)S(1)}, bf16[1024,1024]{1,0:T(8,128)(2,1)S(1)}, bf16[1024,1024]{1,0:T(8,128)(2,1)S(1)}) custom-call(s32[3,1024]{1,0:T(4,128)S(1)} %reshape.12.codes_ref), custom_call_target="tpu_custom_call" | custom-call | flops 1073741824 | bytes 2097152 | tf_op jit(solution)/shard_map/picks/pallas_call | solution.py:211
  4.0 0.0 copy-start
  4.0 0.0 copy-start.2
  4.0 1.5 %project.1 = (bf16[1024,256]{1,0:T(8,128)(2,1)S(1)}, bf16[4,128,256]{2,1,0:T(8,128)(2,1)S(1)}, bf16[4,128,256]{2,1,0:T(8,128)(2,1)S(1)}) custom-call(s32[3,1024]{1,0:T(4,128)S(1)} %reshape.12.codes_ref, bf16[1024,256]{1,0:T(8,128)(2,1)S(1)} %bitcast.5, f32[1,256]{1,0:T(1,128)S(1)} %bitcast.7, bf16[256,256]{1,0:T(8,128)(2,1)S(1)} %copy-done.5), custom_call_target="tpu_custom_call" | custom-call | flops 4294967296 | bytes 2097152 | tf_op jit(solution)/shard_map/project/pallas_call | solution.py:75
  5.5 2.7 %collective-permute-start.4 = (bf16[4,128,256]{2,1,0:T(8,128)(2,1)S(1)}, bf16[4,128,256]{2,1,0:T(8,128)(2,1)S(1)}, u32[]{:S(2)}, u32[]{:S(2)}) collective-permute-start(bf16[4,128,256]{2,1,0:T(8,128)(2,1)S(1)} %get-tuple-element.42), channel_id=1, source_target_pairs={{0,4},{4,0},{8,12},{12,8},{16,20},{20,16},{24,28},{28,24},{1,5},{5... | collective-permute-start | bytes 786440 | tf_op jit(solution)/shard_map/ppermute | solution.py:25
  8.2 1.5 %collective-permute-start.5 = (bf16[2048,256]{1,0:T(8,128)(2,1)S(1)}, bf16[2048,256]{1,0:T(8,128)(2,1)S(1)}, u32[]{:S(2)}, u32[]{:S(2)}) collective-permute-start(bf16[2048,256]{1,0:T(8,128)(2,1)S(1)} %copy-done), channel_id=1, source_target_pairs={{0,2},{1,3},{2,0},{3,1},{4,6},{5,7},{6,4},{7,5},{8,10},{9,11},{10,... | collective-permute-start | bytes 3145736 | tf_op jit(solution)/shard_map/ppermute | solution.py:30
  9.7 3.6 %collective-permute-start.3 = (bf16[4,128,256]{2,1,0:T(8,128)(2,1)S(1)}, bf16[4,128,256]{2,1,0:T(8,128)(2,1)S(1)}, u32[]{:S(2)}, u32[]{:S(2)}) collective-permute-start(bf16[4,128,256]{2,1,0:T(8,128)(2,1)S(1)} %get-tuple-element.41), channel_id=1, source_target_pairs={{0,28},{4,8},{8,4},{12,16},{16,12},{20,24},{24,20},{28,0},{1,29},{... | collective-permute-start | bytes 786440 | tf_op jit(solution)/shard_map/ppermute | solution.py:25
  13.3 7.4 %collective-permute-done.4.rows_ref = bf16[4,128,256]{2,1,0:T(8,128)(2,1)S(1)} collective-permute-done((bf16[4,128,256]{2,1,0:T(8,128)(2,1)S(1)}, bf16[4,128,256]{2,1,0:T(8,128)(2,1)S(1)}, u32[]{:S(2)}, u32[]{:S(2)}) %collective-permute-start.4) | collective-permute-done | bytes 262176 | tf_op jit(solution)/shard_map/ppermute | solution.py:25
  20.7 1.3 %keys_and_values.2.kv_ref = bf16[4,1024,512]{2,1,0:T(8,128)(2,1)S(1)} custom-call(bf16[256,256]{1,0:T(8,128)(2,1)S(1)} %copy-done.2, bf16[256,256]{1,0:T(8,128)(2,1)S(1)} %copy-done.3, bf16[2048,256]{1,0:T(8,128)(2,1)S(1)} %copy-done, bf16[2048,256]{1,0:T(8,128)(2,1)S(1)} %collective-permute-done.refs_1_), custom_call_target="tpu_custom_call" | custom-call | flops 1073741824 | bytes 6291456 | tf_op jit(solution)/shard_map/keys_and_values/pallas_call | solution.py:126
  22.0 6.0 %attend.7 = bf16[4,128,256]{2,1,0:T(8,128)(2,1)S(1)} custom-call(bf16[4,128,256]{2,1,0:T(8,128)(2,1)S(1)} %collective-permute-done.4.rows_ref, bf16[4,1024,512]{2,1,0:T(8,128)(2,1)S(1)} %keys_and_values.2.kv_ref), custom_call_target="tpu_custom_call" | custom-call | flops 4294967296 | bytes 4194304 | tf_op jit(solution)/shard_map/attend/pallas_call | solution.py:181
  28.0 6.1 %attend.8 = bf16[4,128,256]{2,1,0:T(8,128)(2,1)S(1)} custom-call(bf16[4,128,256]{2,1,0:T(8,128)(2,1)S(1)} %collective-permute-done.3.rows_ref, bf16[4,1024,512]{2,1,0:T(8,128)(2,1)S(1)} %keys_and_values.2.kv_ref), custom_call_target="tpu_custom_call" | custom-call | flops 4294967296 | bytes 4194304 | tf_op jit(solution)/shard_map/attend/pallas_call | solution.py:181
  34.0 0.1 collective-permute-start.6
  34.1 1.3 %scatter.1 = (bf16[8,128,256]{2,1,0:T(8,128)(2,1)S(1)}, bf16[4,128,256]{2,1,0:T(8,128)(2,1)S(1)}, bf16[4,128,256]{2,1,0:T(8,128)(2,1)S(1)}) custom-call(s32[3,1024]{1,0:T(4,128)S(1)} %reshape.12.codes_ref, bf16[1024,256]{1,0:T(8,128)(2,1)S(1)} %get-tuple-element.35.rows_ref), custom_call_target="tpu_custom_call" | custom-call | flops 1073741824 | bytes 2097152 | tf_op jit(solution)/shard_map/scatter/pallas_call | solution.py:101
  35.4 6.2 %attend.6.refs_3_ = bf16[4,128,256]{2,1,0:T(8,128)(2,1)S(1)} custom-call(bf16[8,128,256]{2,1,0:T(8,128)(2,1)S(1)} %get-tuple-element.47.rows_ref, bf16[4,1024,512]{2,1,0:T(8,128)(2,1)S(1)} %keys_and_values.2.kv_ref), custom_call_target="tpu_custom_call" | custom-call | flops 4294967296 | bytes 4194304 | tf_op jit(solution)/shard_map/attend/pallas_call | solution.py:181
  41.6 4.9 %collective-permute-start.2 = (bf16[4,128,256]{2,1,0:T(8,128)(2,1)S(1)}, bf16[4,128,256]{2,1,0:T(8,128)(2,1)S(1)}, u32[]{:S(2)}, u32[]{:S(2)}) collective-permute-start(bf16[4,128,256]{2,1,0:T(8,128)(2,1)S(1)} %get-tuple-element.40), channel_id=1, source_target_pairs={{0,28},{4,8},{8,4},{12,16},{16,12},{20,24},{24,20},{28,0},{1,29},{... | collective-permute-start | bytes 786440 | tf_op jit(solution)/shard_map/ppermute | solution.py:25
  46.5 0.1 collective-permute-start.7
  46.5 2.0 %collective-permute-start.1 = (bf16[4,128,256]{2,1,0:T(8,128)(2,1)S(1)}, bf16[4,128,256]{2,1,0:T(8,128)(2,1)S(1)}, u32[]{:S(2)}, u32[]{:S(2)}) collective-permute-start(bf16[4,128,256]{2,1,0:T(8,128)(2,1)S(1)} %get-tuple-element.39), channel_id=1, source_target_pairs={{0,4},{4,0},{8,12},{12,8},{16,20},{20,16},{24,28},{28,24},{1,5},{5... | collective-permute-start | bytes 786440 | tf_op jit(solution)/shard_map/ppermute | solution.py:25
  48.6 5.2 %collective-permute-done.2.rows_ref = bf16[4,128,256]{2,1,0:T(8,128)(2,1)S(1)} collective-permute-done((bf16[4,128,256]{2,1,0:T(8,128)(2,1)S(1)}, bf16[4,128,256]{2,1,0:T(8,128)(2,1)S(1)}, u32[]{:S(2)}, u32[]{:S(2)}) %collective-permute-start.2) | collective-permute-done | bytes 262176 | tf_op jit(solution)/shard_map/ppermute | solution.py:25
  53.7 1.3 %keys_and_values.3.kv_ref = bf16[4,1024,512]{2,1,0:T(8,128)(2,1)S(1)} custom-call(bf16[256,256]{1,0:T(8,128)(2,1)S(1)} %copy-done.2, bf16[256,256]{1,0:T(8,128)(2,1)S(1)} %copy-done.3, bf16[2048,256]{1,0:T(8,128)(2,1)S(1)} %collective-permute-done.5.refs_0_, bf16[2048,256]{1,0:T(8,128)(2,1)S(1)} %collective-permute-done.6.refs_1_), custom_call_target="tpu_custom_call" | custom-call | flops 1073741824 | bytes 6291456 | tf_op jit(solution)/shard_map/keys_and_values/pallas_call | solution.py:126
  55.0 6.0 %attend.9 = bf16[4,128,256]{2,1,0:T(8,128)(2,1)S(1)} custom-call(bf16[4,128,256]{2,1,0:T(8,128)(2,1)S(1)} %collective-permute-done.2.rows_ref, bf16[4,1024,512]{2,1,0:T(8,128)(2,1)S(1)} %keys_and_values.3.kv_ref), custom_call_target="tpu_custom_call" | custom-call | flops 4294967296 | bytes 4194304 | tf_op jit(solution)/shard_map/attend/pallas_call | solution.py:181
  61.0 9.3 %collective-permute-done.1.rows_ref = bf16[4,128,256]{2,1,0:T(8,128)(2,1)S(1)} collective-permute-done((bf16[4,128,256]{2,1,0:T(8,128)(2,1)S(1)}, bf16[4,128,256]{2,1,0:T(8,128)(2,1)S(1)}, u32[]{:S(2)}, u32[]{:S(2)}) %collective-permute-start.1) | collective-permute-done | bytes 262176 | tf_op jit(solution)/shard_map/ppermute | solution.py:25
  70.3 6.0 %attend.10 = bf16[4,128,256]{2,1,0:T(8,128)(2,1)S(1)} custom-call(bf16[4,128,256]{2,1,0:T(8,128)(2,1)S(1)} %collective-permute-done.1.rows_ref, bf16[4,1024,512]{2,1,0:T(8,128)(2,1)S(1)} %keys_and_values.3.kv_ref), custom_call_target="tpu_custom_call" | custom-call | flops 4294967296 | bytes 4194304 | tf_op jit(solution)/shard_map/attend/pallas_call | solution.py:181
  76.3 0.1 collective-permute-start.10
  76.4 4.5 %collective-permute-start.8 = (bf16[4,128,256]{2,1,0:T(8,128)(2,1)S(1)}, bf16[4,128,256]{2,1,0:T(8,128)(2,1)S(1)}, u32[]{:S(2)}, u32[]{:S(2)}) collective-permute-start(bf16[4,128,256]{2,1,0:T(8,128)(2,1)S(1)} %attend.9), channel_id=1, source_target_pairs={{0,28},{4,8},{8,4},{12,16},{16,12},{20,24},{24,20},{28,0},{1,29},{... | collective-permute-start | bytes 786440 | tf_op jit(solution)/shard_map/ppermute | solution.py:25
  80.9 6.2 %attend.11.refs_4_ = bf16[4,128,256]{2,1,0:T(8,128)(2,1)S(1)} custom-call(bf16[8,128,256]{2,1,0:T(8,128)(2,1)S(1)} %get-tuple-element.47.rows_ref, bf16[4,1024,512]{2,1,0:T(8,128)(2,1)S(1)} %keys_and_values.3.kv_ref), custom_call_target="tpu_custom_call" | custom-call | flops 4294967296 | bytes 4194304 | tf_op jit(solution)/shard_map/attend/pallas_call | solution.py:181
  87.1 0.3 collective-permute-done.8.refs_6_
  87.5 1.5 %partial_sum.1.partial_ref = f32[1024,256]{1,0:T(8,128)S(1)} custom-call(bf16[1024,1024]{1,0:T(8,128)(2,1)S(1)} %get-tuple-element.31.refs_0_, bf16[1024,1024]{1,0:T(8,128)(2,1)S(1)} %get-tuple-element.32.refs_1_, bf16[1024,1024]{1,0:T(8,128)(2,1)S(1)} %get-tuple-element.33.refs_2_, bf16[4,128,256]{2,1,0:T(8,128)(2,1)S(1)} %attend.6.refs_3_, ...), custom_call_target="tpu_custom_call" | custom-call | flops 1073741824 | bytes 2097152 | tf_op jit(solution)/shard_map/partial_sum/pallas_call | solution.py:240
  89.0 1.2 %collective-permute-done.10.refs_3_ = bf16[4,128,256]{2,1,0:T(8,128)(2,1)S(1)} collective-permute-done((bf16[4,128,256]{2,1,0:T(8,128)(2,1)S(1)}, bf16[4,128,256]{2,1,0:T(8,128)(2,1)S(1)}, u32[]{:S(2)}, u32[]{:S(2)}) %collective-permute-start.10) | collective-permute-done | bytes 262176 | tf_op jit(solution)/shard_map/ppermute | solution.py:25
  90.2 2.0 %finish.1 = bf16[1024,256]{1,0:T(8,128)(2,1)} custom-call(f32[1024,256]{1,0:T(8,128)S(1)} %partial_sum.1.partial_ref, bf16[1024,256]{1,0:T(8,128)(2,1)S(1)} %bitcast.6, bf16[256,256]{1,0:T(8,128)(2,1)S(1)} %copy-done.4, bf16[1024,1024]{1,0:T(8,128)(2,1)S(1)} %get-tuple-element.31.refs_0_, bf16[1024,1024]{1,0:T(8,128)(2,1)S(1)} %get-tuple-element.32.refs_1_, ...), custom_call_target="tpu_custom_call" | custom-call | flops 1073741824 | bytes 2097152 | tf_op jit(solution)/shard_map/finish/pallas_call | solution.py:260
  (19 shorter events, 0.0 us)
Async XLA Ops:
  0.0 3.9 %copy-start.5 = (bf16[256,256]{1,0:T(8,128)(2,1)S(1)}, bf16[256,256]{1,0:T(8,128)(2,1)}, u32[]{:S(2)}) copy-start(bf16[256,256]{1,0:T(8,128)(2,1)} %weight_hbm.1) | copy-start | bytes 393220
  0.0 3.9 %copy-start.6 = (f32[256]{0:T(256)S(1)}, f32[256]{0:T(256)}, u32[]{:S(2)}) copy-start(f32[256]{0:T(256)} %param.10) | copy-start | bytes 3076
  0.0 3.9 %copy-start.1 = (bf16[16,64,256]{2,1,0:T(8,128)(2,1)S(1)}, bf16[16,64,256]{2,1,0:T(8,128)(2,1)}, u32[]{:S(2)}) copy-start(bf16[16,64,256]{2,1,0:T(8,128)(2,1)} %param.9) | copy-start | bytes 1572868
  0.0 20.7 %collective-permute-start = (bf16[2048,256]{1,0:T(8,128)(2,1)}, bf16[2048,256]{1,0:T(8,128)(2,1)S(1)}, u32[]{:S(2)}, u32[]{:S(2)}) collective-permute-start(bf16[2048,256]{1,0:T(8,128)(2,1)} %refs_0_.1), channel_id=1, source_target_pairs={{0,1},{1,0},{2,3},{3,2},{4,5},{5,4},{6,7},{7,6},{8,9},{9,8},{10,11... | collective-permute-start | bytes 3145736 | tf_op jit(solution)/shard_map/ppermute | solution.py:30
  4.0 4.3 %copy-start = (bf16[2048,256]{1,0:T(8,128)(2,1)S(1)}, bf16[2048,256]{1,0:T(8,128)(2,1)}, u32[]{:S(2)}) copy-start(bf16[2048,256]{1,0:T(8,128)(2,1)} %refs_0_.1) | copy-start | bytes 3145732
  4.0 16.7 %copy-start.2 = (bf16[256,256]{1,0:T(8,128)(2,1)S(1)}, bf16[256,256]{1,0:T(8,128)(2,1)}, u32[]{:S(2)}) copy-start(bf16[256,256]{1,0:T(8,128)(2,1)} %key_ref.3) | copy-start | bytes 393220
  4.0 16.7 %copy-start.3 = (bf16[256,256]{1,0:T(8,128)(2,1)S(1)}, bf16[256,256]{1,0:T(8,128)(2,1)}, u32[]{:S(2)}) copy-start(bf16[256,256]{1,0:T(8,128)(2,1)} %value_ref.3) | copy-start | bytes 393220
  5.5 15.1 %collective-permute-start.4 = (bf16[4,128,256]{2,1,0:T(8,128)(2,1)S(1)}, bf16[4,128,256]{2,1,0:T(8,128)(2,1)S(1)}, u32[]{:S(2)}, u32[]{:S(2)}) collective-permute-start(bf16[4,128,256]{2,1,0:T(8,128)(2,1)S(1)} %get-tuple-element.42), channel_id=1, source_target_pairs={{0,4},{4,0},{8,12},{12,8},{16,20},{20,16},{24,28},{28,24},{1,5},{5... | collective-permute-start | bytes 786440 | tf_op jit(solution)/shard_map/ppermute | solution.py:25
  8.2 25.8 %collective-permute-start.5 = (bf16[2048,256]{1,0:T(8,128)(2,1)S(1)}, bf16[2048,256]{1,0:T(8,128)(2,1)S(1)}, u32[]{:S(2)}, u32[]{:S(2)}) collective-permute-start(bf16[2048,256]{1,0:T(8,128)(2,1)S(1)} %copy-done), channel_id=1, source_target_pairs={{0,2},{1,3},{2,0},{3,1},{4,6},{5,7},{6,4},{7,5},{8,10},{9,11},{10,... | collective-permute-start | bytes 3145736 | tf_op jit(solution)/shard_map/ppermute | solution.py:30
  9.7 18.2 %collective-permute-start.3 = (bf16[4,128,256]{2,1,0:T(8,128)(2,1)S(1)}, bf16[4,128,256]{2,1,0:T(8,128)(2,1)S(1)}, u32[]{:S(2)}, u32[]{:S(2)}) collective-permute-start(bf16[4,128,256]{2,1,0:T(8,128)(2,1)S(1)} %get-tuple-element.41), channel_id=1, source_target_pairs={{0,28},{4,8},{8,4},{12,16},{16,12},{20,24},{24,20},{28,0},{1,29},{... | collective-permute-start | bytes 786440 | tf_op jit(solution)/shard_map/ppermute | solution.py:25
  34.0 19.7 %collective-permute-start.6 = (bf16[2048,256]{1,0:T(8,128)(2,1)S(1)}, bf16[2048,256]{1,0:T(8,128)(2,1)S(1)}, u32[]{:S(2)}, u32[]{:S(2)}) collective-permute-start(bf16[2048,256]{1,0:T(8,128)(2,1)S(1)} %collective-permute-done.5.refs_0_), channel_id=1, source_target_pairs={{0,1},{1,0},{2,3},{3,2},{4,5},{5,4},{6,7},{7,6},{8,9},{9,8},{10,11... | collective-permute-start | bytes 3145736 | tf_op jit(solution)/shard_map/ppermute | solution.py:30
  41.6 12.1 %collective-permute-start.2 = (bf16[4,128,256]{2,1,0:T(8,128)(2,1)S(1)}, bf16[4,128,256]{2,1,0:T(8,128)(2,1)S(1)}, u32[]{:S(2)}, u32[]{:S(2)}) collective-permute-start(bf16[4,128,256]{2,1,0:T(8,128)(2,1)S(1)} %get-tuple-element.40), channel_id=1, source_target_pairs={{0,28},{4,8},{8,4},{12,16},{16,12},{20,24},{24,20},{28,0},{1,29},{... | collective-permute-start | bytes 786440 | tf_op jit(solution)/shard_map/ppermute | solution.py:25
  46.5 40.7 %collective-permute-start.7 = (bf16[4,128,256]{2,1,0:T(8,128)(2,1)S(1)}, bf16[4,128,256]{2,1,0:T(8,128)(2,1)S(1)}, u32[]{:S(2)}, u32[]{:S(2)}) collective-permute-start(bf16[4,128,256]{2,1,0:T(8,128)(2,1)S(1)} %attend.8), channel_id=1, source_target_pairs={{0,28},{4,8},{8,4},{12,16},{16,12},{20,24},{24,20},{28,0},{1,29},{... | collective-permute-start | bytes 786440 | tf_op jit(solution)/shard_map/ppermute | solution.py:25
  46.5 40.6 %collective-permute-start.9 = (bf16[4,128,256]{2,1,0:T(8,128)(2,1)S(1)}, bf16[4,128,256]{2,1,0:T(8,128)(2,1)S(1)}, u32[]{:S(2)}, u32[]{:S(2)}) collective-permute-start(bf16[4,128,256]{2,1,0:T(8,128)(2,1)S(1)} %attend.7), channel_id=1, source_target_pairs={{0,4},{4,0},{8,12},{12,8},{16,20},{20,16},{24,28},{28,24},{1,5},{5... | collective-permute-start | bytes 786440 | tf_op jit(solution)/shard_map/ppermute | solution.py:25
  46.5 23.7 %collective-permute-start.1 = (bf16[4,128,256]{2,1,0:T(8,128)(2,1)S(1)}, bf16[4,128,256]{2,1,0:T(8,128)(2,1)S(1)}, u32[]{:S(2)}, u32[]{:S(2)}) collective-permute-start(bf16[4,128,256]{2,1,0:T(8,128)(2,1)S(1)} %get-tuple-element.39), channel_id=1, source_target_pairs={{0,4},{4,0},{8,12},{12,8},{16,20},{20,16},{24,28},{28,24},{1,5},{5... | collective-permute-start | bytes 786440 | tf_op jit(solution)/shard_map/ppermute | solution.py:25
  76.3 13.9 %collective-permute-start.10 = (bf16[4,128,256]{2,1,0:T(8,128)(2,1)S(1)}, bf16[4,128,256]{2,1,0:T(8,128)(2,1)S(1)}, u32[]{:S(2)}, u32[]{:S(2)}) collective-permute-start(bf16[4,128,256]{2,1,0:T(8,128)(2,1)S(1)} %attend.10), channel_id=1, source_target_pairs={{0,4},{4,0},{8,12},{12,8},{16,20},{20,16},{24,28},{28,24},{1,5},{5... | collective-permute-start | bytes 786440 | tf_op jit(solution)/shard_map/ppermute | solution.py:25
  76.4 11.1 %collective-permute-start.8 = (bf16[4,128,256]{2,1,0:T(8,128)(2,1)S(1)}, bf16[4,128,256]{2,1,0:T(8,128)(2,1)S(1)}, u32[]{:S(2)}, u32[]{:S(2)}) collective-permute-start(bf16[4,128,256]{2,1,0:T(8,128)(2,1)S(1)} %attend.9), channel_id=1, source_target_pairs={{0,28},{4,8},{8,4},{12,16},{16,12},{20,24},{24,20},{28,0},{1,29},{... | collective-permute-start | bytes 786440 | tf_op jit(solution)/shard_map/ppermute | solution.py:25
  87.1 3.1 %copy-start.4 = (bf16[256,256]{1,0:T(8,128)(2,1)S(1)}, bf16[256,256]{1,0:T(8,128)(2,1)}, u32[]{:S(2)}) copy-start(bf16[256,256]{1,0:T(8,128)(2,1)} %weight_ref.1) | copy-start | bytes 393220
